TPU v7x, 32 devices: a whole 2x2x4 slice. The times are simulated.
32 devices in a mesh: dp: 8 (over z, y), stream: 2 (over x), tensor: 2 (over core).
Axes of the slice: x: 2, y: 2, z: 4, core: 2. Of those that a mesh axis runs over, the one named last changes fastest.
Arguments:
- word_states: bfloat16 [8, 512, 768], P('dp', 'stream'), may hold values from -6 to 6
- entity_shard: int32 [2, 8, 64, 1], P('stream', 'dp'), may hold values from 0 to 15; in each aligned block of 64 rows (0 to 63, 64 to 127, ..., all dimensions but the last counted through in order) at most 8 rows name the same one
- entity_row: int32 [2, 8, 64], P('stream', 'dp'), may hold values from 0 to 4095
- word_segments: int32 [8, 512], P('dp'), may hold values from 0 to 3, never falling along the last dimension, each value on 1 to 256 neighbouring positions
- entity_segments: int32 [8, 128], P('dp'), may hold values from 0 to 3, never falling along the last dimension, each value on 1 to 64 neighbouring positions
- entity_table: bfloat16 [65536, 256], P(('dp', 'stream')), may hold values from -6 to 6
- adam_first: float32 [65536, 256], P(('dp', 'stream')), may hold values from -4 to 4
- adam_second: float32 [65536, 256], P(('dp', 'stream')), may hold values from 0.1 to 1
- w_entity: bfloat16 [256, 768], replicated, may hold values from -0.375 to 0.375
- norm_gain: float32 [3, 768], replicated, may hold values from 0.5 to 1.5
- norm_bias: float32 [3, 768], replicated, may hold values from -3 to 3
- w_query: bfloat16 [4, 768, 768], P(None, None, 'tensor'), may hold values from -0.21875 to 0.21875
- b_query: float32 [4, 768], P(None, 'tensor'), may hold values from -3 to 3
- w_keyval: bfloat16 [2, 768, 768], P(None, None, 'tensor'), may hold values from -0.21875 to 0.21875
- b_value: float32 [768], P('tensor'), may hold values from -3 to 3
- w_out: bfloat16 [768, 768], P('tensor'), may hold values from -2.5 to 2.5
- b_out: float32 [768], replicated, may hold values from -3 to 3
- w_up: bfloat16 [768, 3072], P(None, 'tensor'), may hold values from -0.21875 to 0.21875
- b_up: float32 [3072], P('tensor'), may hold values from -3 to 3
- w_down: bfloat16 [3072, 768], P('tensor'), may hold values from -0.109375 to 0.109375
- b_down: float32 [768], replicated, may hold values from -3 to 3
- cot_words: bfloat16 [8, 512, 768], P('dp', 'stream'), may hold values from -6 to 6
- cot_entities: bfloat16 [8, 128, 768], P('dp', 'stream'), may hold values from -6 to 6
Outputs:
- out_words: bfloat16 [8, 512, 768], P('dp', ('stream', 'tensor'))
- out_entities: bfloat16 [8, 128, 768], P('dp', ('stream', 'tensor'))
- grad_words: float32 [8, 512, 768], P('dp', ('stream', 'tensor'))
- grad_entity: float32 [256, 768], P(None, ('dp', 'stream'))
- grad_gain: float32 [3, 768], P(None, ('dp', 'stream'))
- grad_norm_bias: float32 [3, 768], P(None, ('dp', 'stream'))
- grad_query: float32 [4, 768, 768], P(None, ('dp', 'stream'), 'tensor')
- grad_query_bias: float32 [4, 768], P(None, 'tensor')
- grad_keyval: float32 [2, 768, 768], P(None, ('dp', 'stream'), 'tensor')
- grad_value_bias: float32 [768], P('tensor')
- grad_out: float32 [768, 768], P('tensor', ('dp', 'stream'))
- grad_out_bias: float32 [768], P(('dp', 'stream'))
- grad_up: float32 [768, 3072], P(('dp', 'stream'), 'tensor')
- grad_up_bias: float32 [3072], P('tensor')
- grad_down: float32 [3072, 768], P('tensor', ('dp', 'stream'))
- grad_down_bias: float32 [768], P(('dp', 'stream'))
- table_update: float32 [65536, 256], P(('dp', 'stream'))
- new_first: float32 [65536, 256], P(('dp', 'stream'))
- new_second: float32 [65536, 256], P(('dp', 'stream'))
Inputs may be any that keep to these rules, and one draw needn't show every extreme that they name: Among the 64 entities of one device (an aligned block of entity_shard), at most 8 name the same shard, and in some blocks one shard is named by exactly 8. `word_segments`: never falls along a sequence; every one of the 4 documents holds at least one word. `entity_segments`: never falls along a sequence; every one of the 4 documents holds at least one entity.
All inputs are finite; a program needn't handle non-finite values.
Results may differ from a plain program's by a relative error of at most 0.014.
Values may be sent and summed in bfloat16 or wider, within the bound.
A program may use at most 128 MiB of HBM per device.

v0:
```python
import jax
import jax.numpy as jnp
from jax import lax
from jax.sharding import PartitionSpec as P

HD = 64


norm_eps = 1e-05
score_scale = 0.125
masked_score = -1e30
beta_one = 0.9
beta_two = 0.99
adam_steps = 10
adam_eps = 1e-08


def from_partner(block, axis, apart):
    count = lax.axis_size(axis)
    route = []
    for low in range(count):
        high = low | 1 << apart
        if high != low and high < count:
            route += [(low, high), (high, low)]
    return lax.ppermute(block, axis, route)


def layer_norm(values_in, gain_row, shift_row):
    center = values_in - jnp.mean(values_in, -1, keepdims=True)
    spread = jnp.mean(center * center, -1, keepdims=True)
    return center * lax.rsqrt(spread + norm_eps) * gain_row + shift_row


def gelu_exact(values_in):
    return jax.nn.gelu(values_in, approximate=False)


def matmul(matrix_a, matrix_b):
    return jnp.dot(matrix_a, matrix_b, preferred_element_type=jnp.float32)


def tensor_total(values_in):
    return lax.psum(values_in, "tensor")


def local(
    word_states,
    entity_shard,
    entity_row,
    word_segments,
    entity_segments,
    entity_table,
    adam_first,
    adam_second,
    w_entity,
    norm_gain,
    norm_bias,
    w_query,
    b_query,
    w_keyval,
    b_value,
    w_out,
    b_out,
    w_up,
    b_up,
    w_down,
    b_down,
    cot_words,
    cot_entities,
):
    seq_count, half_words, width = word_states.shape
    half_ents = entity_row.shape[2]
    table_rows, embed_width = entity_table.shape
    local_width = w_query.shape[2]
    local_heads = local_width // HD
    owners = lax.axis_size(("dp", "stream"))
    stream_index = lax.axis_index("stream")
    parts = lax.axis_size("tensor")
    part_index = lax.axis_index("tensor")
    word_part = half_words // parts
    ent_part = half_ents // parts
    ent_count = seq_count * half_ents
    word_count = seq_count * half_words
    local_rows = half_words + half_ents
    share_words = seq_count * word_part
    owner_flat = entity_shard.reshape(ent_count)
    row_flat = entity_row.reshape(ent_count)

    def pick(block, count):
        shaped = block.reshape(seq_count, parts, count // parts, block.shape[-1])
        return lax.dynamic_index_in_dim(shaped, part_index, 1, keepdims=False).reshape(
            seq_count * (count // parts), block.shape[-1]
        )

    def own_share(rows):
        return jnp.concatenate(
            [pick(rows[:word_count], half_words), pick(rows[word_count:], half_ents)], 0
        )

    capacity = 2 * ent_count // owners
    owner_hits = (owner_flat[:, None] == jnp.arange(owners, dtype=jnp.int32)[None, :]).astype(
        jnp.int32
    )
    before = jnp.cumsum(owner_hits, 0) - owner_hits
    ranking = jnp.sum(before * owner_hits, 1)
    slot_index = owner_flat * capacity + ranking
    request = (
        jnp.full((owners * capacity,), -1, jnp.int32)
        .at[slot_index]
        .set(row_flat)
        .reshape(owners, capacity)
    )
    asked_ids = lax.all_to_all(request, ("dp", "stream"), split_axis=0, concat_axis=0, tiled=True)
    present = asked_ids >= 0
    found_rows = jnp.take(entity_table, jnp.clip(asked_ids, 0, table_rows - 1), axis=0)
    found_rows = jnp.where(present[..., None], found_rows, jnp.zeros_like(found_rows))
    found_rows, asked_rows = (found_rows, asked_ids)
    answered = lax.all_to_all(found_rows, ("dp", "stream"), split_axis=0, concat_axis=0, tiled=True)
    looked = answered.reshape(owners * capacity, embed_width)[slot_index]
    ent_lin = matmul(looked, w_entity)
    x_entity, entity_norm_back = jax.vjp(layer_norm, ent_lin, norm_gain[0], norm_bias[0])
    entity_low = x_entity.astype(jnp.bfloat16)
    word_low = word_states.reshape(word_count, width)
    query_words = (
        jnp.einsum("rd,jdc->jrc", word_low, w_query[:2], preferred_element_type=jnp.float32)
        + b_query[:2, None, :]
    ).astype(jnp.bfloat16)
    query_ents = (
        jnp.einsum("rd,jdc->jrc", entity_low, w_query[2:], preferred_element_type=jnp.float32)
        + b_query[2:, None, :]
    ).astype(jnp.bfloat16)
    value_shift = jnp.stack([jnp.zeros_like(b_value), b_value])[:, None, :]
    keyval_words = (
        jnp.einsum("rd,jdc->jrc", word_low, w_keyval, preferred_element_type=jnp.float32)
        + value_shift
    ).astype(jnp.bfloat16)
    keyval_ents = (
        jnp.einsum("rd,jdc->jrc", entity_low, w_keyval, preferred_element_type=jnp.float32)
        + value_shift
    ).astype(jnp.bfloat16)
    far_words, far_ents = from_partner((keyval_words, keyval_ents), "stream", 0)

    def by_heads(block, count):
        return block.reshape(block.shape[0], seq_count, count, local_heads, HD)

    queries = jnp.concatenate(
        [by_heads(query_words, half_words), by_heads(query_ents, half_ents)], 2
    )
    keyval_w = jnp.concatenate(
        [by_heads(keyval_words, half_words), by_heads(far_words, half_words)], 2
    )
    keyval_e = jnp.concatenate([by_heads(keyval_ents, half_ents), by_heads(far_ents, half_ents)], 2)
    own_wseg = lax.dynamic_slice_in_dim(word_segments, stream_index * half_words, half_words, 1)
    far_wseg = lax.dynamic_slice_in_dim(
        word_segments, (1 - stream_index) * half_words, half_words, 1
    )
    own_eseg = lax.dynamic_slice_in_dim(entity_segments, stream_index * half_ents, half_ents, 1)
    far_eseg = lax.dynamic_slice_in_dim(
        entity_segments, (1 - stream_index) * half_ents, half_ents, 1
    )
    query_seg = jnp.concatenate([own_wseg, own_eseg], 1)
    key_wseg = jnp.concatenate([own_wseg, far_wseg], 1)
    key_eseg = jnp.concatenate([own_eseg, far_eseg], 1)
    allow_words = query_seg[:, None, :, None] == key_wseg[:, None, None, :]
    allow_ents = query_seg[:, None, :, None] == key_eseg[:, None, None, :]

    def scores_of():
        raw_words = (
            jnp.einsum(
                "sqhd,skhd->shqk", queries[0], keyval_w[0], preferred_element_type=jnp.float32
            )
            * score_scale
        )
        raw_ents = (
            jnp.einsum(
                "sqhd,skhd->shqk", queries[1], keyval_e[0], preferred_element_type=jnp.float32
            )
            * score_scale
        )
        return (
            jnp.where(allow_words, raw_words, masked_score),
            jnp.where(allow_ents, raw_ents, masked_score),
        )

    score_words, score_ents = scores_of()
    highest = jnp.maximum(
        jnp.max(score_words, -1, keepdims=True), jnp.max(score_ents, -1, keepdims=True)
    )
    totals = jnp.sum(jnp.exp(score_words - highest), -1, keepdims=True) + jnp.sum(
        jnp.exp(score_ents - highest), -1, keepdims=True
    )
    log_total = highest + jnp.log(totals)
    low_words = jnp.exp(score_words - log_total).astype(jnp.bfloat16)
    low_ents = jnp.exp(score_ents - log_total).astype(jnp.bfloat16)
    heads_out = jnp.einsum(
        "shqk,skhd->sqhd", low_words, keyval_w[1], preferred_element_type=jnp.float32
    )
    heads_out = heads_out + jnp.einsum(
        "shqk,skhd->sqhd", low_ents, keyval_e[1], preferred_element_type=jnp.float32
    )
    heads_out = heads_out.astype(jnp.bfloat16).reshape(seq_count, local_rows, local_width)
    heads_dense = jnp.concatenate(
        [
            heads_out[:, :half_words].reshape(word_count, local_width),
            heads_out[:, half_words:].reshape(ent_count, local_width),
        ],
        0,
    )
    resid_in = jnp.concatenate([word_low.astype(jnp.float32), x_entity], 0)
    cotangent = jnp.concatenate(
        [cot_words.reshape(word_count, width), cot_entities.reshape(ent_count, width)], 0
    ).astype(jnp.float32)
    attn_out = tensor_total(matmul(heads_dense, w_out)) + b_out
    first_norm, first_back = jax.vjp(layer_norm, resid_in + attn_out, norm_gain[1], norm_bias[1])
    first_low = first_norm.astype(jnp.bfloat16)
    up_value = matmul(first_low, w_up) + b_up
    active, gelu_back = jax.vjp(gelu_exact, up_value)
    active_low = active.astype(jnp.bfloat16)
    ffn_out = tensor_total(matmul(active_low, w_down)) + b_down
    final_norm, final_back = jax.vjp(layer_norm, first_norm + ffn_out, norm_gain[2], norm_bias[2])
    final_share = own_share(final_norm)
    grad_final, gain_final, shift_final = final_back(cotangent)
    grad_ffn = grad_final.astype(jnp.bfloat16)
    out_words = final_share[:share_words].reshape(seq_count, word_part, width).astype(jnp.bfloat16)
    out_entities = (
        final_share[share_words:].reshape(seq_count, ent_part, width).astype(jnp.bfloat16)
    )
    grad_down = jnp.einsum("rf,rd->fd", active_low, grad_ffn, preferred_element_type=jnp.float32)
    grad_down_bias = jnp.sum(grad_ffn.astype(jnp.float32), 0)
    (grad_pre,) = gelu_back(
        jnp.einsum("rd,fd->rf", grad_ffn, w_down, preferred_element_type=jnp.float32)
    )
    grad_up_low = grad_pre.astype(jnp.bfloat16)
    grad_up = jnp.einsum("rd,rf->df", first_low, grad_up_low, preferred_element_type=jnp.float32)
    grad_up_bias = jnp.sum(grad_up_low.astype(jnp.float32), 0)
    ffn_term = jnp.einsum("rf,df->rd", grad_up_low, w_up, preferred_element_type=jnp.float32)
    grad_first, gain_first, shift_first = first_back(grad_final + tensor_total(ffn_term))
    grad_attn = grad_first.astype(jnp.bfloat16)
    grad_out = jnp.einsum("rc,rd->cd", heads_dense, grad_attn, preferred_element_type=jnp.float32)
    grad_out_bias = jnp.sum(grad_attn.astype(jnp.float32), 0)
    grad_heads = jnp.einsum(
        "rd,cd->rc", grad_attn, w_out, preferred_element_type=jnp.float32
    ).astype(jnp.bfloat16)
    grad_heads = jnp.concatenate(
        [
            grad_heads[:word_count].reshape(seq_count, half_words, local_heads, HD),
            grad_heads[word_count:].reshape(seq_count, half_ents, local_heads, HD),
        ],
        1,
    )
    score_words, score_ents = scores_of()
    prob_words = jnp.exp(score_words - log_total)
    prob_ents = jnp.exp(score_ents - log_total)
    low_words = prob_words.astype(jnp.bfloat16)
    low_ents = prob_ents.astype(jnp.bfloat16)
    dprob_words = jnp.einsum(
        "sqhd,skhd->shqk", grad_heads, keyval_w[1], preferred_element_type=jnp.float32
    )
    dprob_ents = jnp.einsum(
        "sqhd,skhd->shqk", grad_heads, keyval_e[1], preferred_element_type=jnp.float32
    )
    inner_sum = jnp.sum(prob_words * dprob_words, -1, keepdims=True) + jnp.sum(
        prob_ents * dprob_ents, -1, keepdims=True
    )
    dscore_words = (prob_words * (dprob_words - inner_sum)).astype(jnp.bfloat16)
    dscore_ents = (prob_ents * (dprob_ents - inner_sum)).astype(jnp.bfloat16)
    grad_to_words = (
        jnp.einsum("shqk,skhd->sqhd", dscore_words, keyval_w[0], preferred_element_type=jnp.float32)
        * score_scale
    ).astype(jnp.bfloat16)
    grad_to_ents = (
        jnp.einsum("shqk,skhd->sqhd", dscore_ents, keyval_e[0], preferred_element_type=jnp.float32)
        * score_scale
    ).astype(jnp.bfloat16)
    kv_grad_words = jnp.stack(
        [
            jnp.einsum(
                "shqk,sqhd->skhd", dscore_words, queries[0], preferred_element_type=jnp.float32
            )
            * score_scale,
            jnp.einsum(
                "shqk,sqhd->skhd", low_words, grad_heads, preferred_element_type=jnp.float32
            ),
        ]
    )
    kv_grad_ents = jnp.stack(
        [
            jnp.einsum(
                "shqk,sqhd->skhd", dscore_ents, queries[1], preferred_element_type=jnp.float32
            )
            * score_scale,
            jnp.einsum("shqk,sqhd->skhd", low_ents, grad_heads, preferred_element_type=jnp.float32),
        ]
    )
    back_words, back_ents = (
        from_partner(kv_grad_words[:, :, half_words:].astype(jnp.bfloat16), "stream", 0).astype(
            jnp.float32
        ),
        from_partner(kv_grad_ents[:, :, half_ents:].astype(jnp.bfloat16), "stream", 0).astype(
            jnp.float32
        ),
    )
    grad_kv_words = (
        (kv_grad_words[:, :, :half_words] + back_words)
        .reshape(2, word_count, local_width)
        .astype(jnp.bfloat16)
    )
    grad_kv_ents = (
        (kv_grad_ents[:, :, :half_ents] + back_ents)
        .reshape(2, ent_count, local_width)
        .astype(jnp.bfloat16)
    )
    grad_q_words = jnp.stack([grad_to_words[:, :half_words], grad_to_ents[:, :half_words]]).reshape(
        2, word_count, local_width
    )
    grad_q_ents = jnp.stack([grad_to_words[:, half_words:], grad_to_ents[:, half_words:]]).reshape(
        2, ent_count, local_width
    )
    grad_query = jnp.concatenate(
        [
            jnp.einsum("rd,jrc->jdc", word_low, grad_q_words, preferred_element_type=jnp.float32),
            jnp.einsum("rd,jrc->jdc", entity_low, grad_q_ents, preferred_element_type=jnp.float32),
        ],
        0,
    )
    grad_query_bias = jnp.concatenate(
        [jnp.sum(grad_q_words.astype(jnp.float32), 1), jnp.sum(grad_q_ents.astype(jnp.float32), 1)],
        0,
    )
    grad_keyval = jnp.einsum(
        "rd,jrc->jdc", word_low, grad_kv_words, preferred_element_type=jnp.float32
    ) + jnp.einsum("rd,jrc->jdc", entity_low, grad_kv_ents, preferred_element_type=jnp.float32)
    grad_value_bias = jnp.sum(grad_kv_words[1].astype(jnp.float32), 0) + jnp.sum(
        grad_kv_ents[1].astype(jnp.float32), 0
    )
    input_words = jnp.einsum(
        "jrc,jdc->rd", grad_q_words, w_query[:2], preferred_element_type=jnp.float32
    ) + jnp.einsum("jrc,jdc->rd", grad_kv_words, w_keyval, preferred_element_type=jnp.float32)
    input_ents = jnp.einsum(
        "jrc,jdc->rd", grad_q_ents, w_query[2:], preferred_element_type=jnp.float32
    ) + jnp.einsum("jrc,jdc->rd", grad_kv_ents, w_keyval, preferred_element_type=jnp.float32)
    input_term = jnp.concatenate([input_words, input_ents], 0)
    grad_input = grad_first + tensor_total(input_term)
    grad_share = own_share(grad_input)
    grad_lin, gain_entity, shift_entity = entity_norm_back(grad_input[word_count:])
    grad_lin_low = grad_lin.astype(jnp.bfloat16)
    gain_grads = jnp.stack([gain_entity, gain_first, gain_final])
    shift_grads = jnp.stack([shift_entity, shift_first, shift_final])
    grad_words = grad_share[:share_words].reshape(seq_count, word_part, width)
    grad_entity = jnp.einsum("re,rd->ed", looked, grad_lin_low, preferred_element_type=jnp.float32)
    grad_looked = jnp.einsum(
        "rd,ed->re", grad_lin_low, w_entity, preferred_element_type=jnp.float32
    )
    outgoing = (
        jnp.zeros((owners * capacity, embed_width), jnp.float32)
        .at[slot_index]
        .set(grad_looked)
        .reshape(owners, capacity, embed_width)
    )
    incoming = lax.all_to_all(
        outgoing.astype(jnp.bfloat16), ("dp", "stream"), split_axis=0, concat_axis=0, tiled=True
    ).astype(outgoing.dtype)
    target = jnp.where(asked_rows >= 0, asked_rows, table_rows).reshape(-1)
    gradient_sum = (
        jnp.zeros((table_rows, embed_width), jnp.float32)
        .at[target]
        .add(incoming.reshape(-1, embed_width), mode="drop")
    )
    use_count = jnp.zeros((table_rows,), jnp.float32).at[target].add(1.0, mode="drop")
    touched = (use_count > 0.0)[:, None]
    first_next = beta_one * adam_first + (1.0 - beta_one) * gradient_sum
    second_next = beta_two * adam_second + (1.0 - beta_two) * gradient_sum * gradient_sum
    direction = (
        first_next
        / (1.0 - beta_one**adam_steps)
        / (jnp.sqrt(second_next / (1.0 - beta_two**adam_steps)) + adam_eps)
    )
    table_update = jnp.where(touched, direction, jnp.zeros_like(direction))
    new_first = jnp.where(touched, first_next, adam_first)
    new_second = jnp.where(touched, second_next, adam_second)
    (
        red_entity,
        red_gain,
        red_shift,
        red_query,
        red_keyval,
        red_out,
        red_out_bias,
        red_up,
        red_down,
        red_down_bias,
    ) = (
        lax.psum_scatter(grad_entity, ("dp", "stream"), scatter_dimension=1, tiled=True),
        lax.psum_scatter(gain_grads, ("dp", "stream"), scatter_dimension=1, tiled=True),
        lax.psum_scatter(shift_grads, ("dp", "stream"), scatter_dimension=1, tiled=True),
        lax.psum_scatter(grad_query, ("dp", "stream"), scatter_dimension=1, tiled=True),
        lax.psum_scatter(grad_keyval, ("dp", "stream"), scatter_dimension=1, tiled=True),
        lax.psum_scatter(grad_out, ("dp", "stream"), scatter_dimension=1, tiled=True),
        lax.psum_scatter(grad_out_bias, ("dp", "stream"), scatter_dimension=0, tiled=True),
        lax.psum_scatter(grad_up, ("dp", "stream"), scatter_dimension=0, tiled=True),
        lax.psum_scatter(grad_down, ("dp", "stream"), scatter_dimension=1, tiled=True),
        lax.psum_scatter(grad_down_bias, ("dp", "stream"), scatter_dimension=0, tiled=True),
    )
    red_query_bias, red_value_bias, red_up_bias = lax.psum(
        (grad_query_bias, grad_value_bias, grad_up_bias), ("dp", "stream")
    )
    return (
        out_words,
        out_entities,
        grad_words,
        red_entity,
        red_gain,
        red_shift,
        red_query,
        red_query_bias,
        red_keyval,
        red_value_bias,
        red_out,
        red_out_bias,
        red_up,
        red_up_bias,
        red_down,
        red_down_bias,
        table_update,
        new_first,
        new_second,
    )


def solution(mesh):
    placed = (
        P("dp", "stream", None),
        P("stream", "dp", None, None),
        P("stream", "dp", None),
        P("dp", None),
        P("dp", None),
        P(("dp", "stream"), None),
        P(("dp", "stream"), None),
        P(("dp", "stream"), None),
        P(),
        P(),
        P(),
        P(None, None, "tensor"),
        P(None, "tensor"),
        P(None, None, "tensor"),
        P("tensor"),
        P("tensor", None),
        P(),
        P(None, "tensor"),
        P("tensor"),
        P("tensor", None),
        P(),
        P("dp", "stream", None),
        P("dp", "stream", None),
    )
    return jax.shard_map(
        local,
        mesh=mesh,
        in_specs=placed,
        out_specs=(
            P("dp", ("stream", "tensor"), None),
            P("dp", ("stream", "tensor"), None),
            P("dp", ("stream", "tensor"), None),
            P(None, ("dp", "stream")),
            P(None, ("dp", "stream")),
            P(None, ("dp", "stream")),
            P(None, ("dp", "stream"), "tensor"),
            P(None, "tensor"),
            P(None, ("dp", "stream"), "tensor"),
            P("tensor"),
            P("tensor", ("dp", "stream")),
            P(("dp", "stream")),
            P(("dp", "stream"), "tensor"),
            P("tensor"),
            P("tensor", ("dp", "stream")),
            P(("dp", "stream")),
            P(("dp", "stream"), None),
            P(("dp", "stream"), None),
            P(("dp", "stream"), None),
        ),
        check_vma=False,
    )
```

profile of v0, /device:TPU:0, one launch (start us, length us, event | category | flops | bytes accessed | tf_op | source)
XLA Modules:
  0.0 1257.9 jit_solution(774999277799180108)
XLA Ops:
  11.3 8.3 all-to-all-start
  20.4 2.6 fusion.16
  26.5 2.5 fusion.17
  35.0 3.2 gather_fusion
  39.9 5.6 all-to-all-start.1
  48.3 4.8 all-to-all-done.1
  78.0 15.3 %all-reduce.13.cloned.1.call-done = f32[320,768]{1,0:T(8,128)} async-done(((f32[320,768]{1,0:T(8,128)}), f32[320,768]{1,0:T(8,128)}) %all-reduce.13.cloned.1.call-update) | async-done | bytes 983056 | tf_op jit(solution)/shard_map/psum | solution.py:43
  95.9 6.3 multiply_convert_fusion.1
  105.2 20.8 %all-reduce.15.cloned.1.call-done = f32[320,768]{1,0:T(8,128)} async-done(((f32[320,768]{1,0:T(8,128)}), f32[320,768]{1,0:T(8,128)}) %all-reduce.15.cloned.1.call-update) | async-done | bytes 983056 | tf_op jit(solution)/shard_map/psum | solution.py:43
  139.3 18.0 %all-reduce.17.cloned.1.call-done = f32[320,768]{1,0:T(8,128)} async-done(((f32[320,768]{1,0:T(8,128)}), f32[320,768]{1,0:T(8,128)}) %all-reduce.17.cloned.1.call-update) | async-done | bytes 983056 | tf_op jit(solution)/shard_map/psum | solution.py:43
  157.3 2.7 multiply_reduce_fusion.1
  169.0 4.3 convolution_bitcast_fusion.4
  174.4 2.7 multiply_reduce_fusion
  190.7 3.6 collective-permute-done.3
  197.8 4.2 collective-permute-done.2
  207.9 2.6 pad_maximum_fusion
  210.6 6.6 copy.120
  218.5 7.0 all-reduce.19.cloned.1.call-done
  232.6 3.0 add_bitcast_fusion
  235.6 5.3 copy.122
  245.4 3.8 fusion.111
  250.6 3.6 fusion.126
  267.4 6.8 all-to-all-start.2
  274.3 77.1 %all-reduce.5 = (f32[4,384]{1,0:T(4,128)}, f32[384]{0:T(512)}, f32[768]{0:T(1024)S(1)}, f32[1536]{0:T(1024)}, f32[768]{0:T(1024)S(1)}) all-reduce(f32[4,384]{1,0:T(4,128)S(1)} %pad_maximum_fusion.19, f32[384]{0:T(512)S(1)} %add.369, f32[768]{0:T(1024)S(1)} %copy-done.96, ...), channel_id=1, replica_groups=mesh['dp'=8,'stream'=2,'tensor'=2] {'dp','stream'}, use_global_device_ids=true, to_apply=%region_37.38 | all-reduce | flops 4992 | bytes 39936 | tf_op jit(solution)/shard_map/psum | solution.py:404
  354.9 124.5 %reduce-scatter.19.cloned.1.call-done = f32[48,3]{1,0:T(8,128)} async-done(((f32[768,3]{1,0:T(8,128)}), f32[48,3]{1,0:T(8,128)}) %reduce-scatter.19.cloned.1.call-update) | async-done | bytes 592
  480.8 3.6 scatter_custom_fusion.3
  484.4 12.1 fusion.2
  496.6 215.7 %all-reduce.21.cloned.1.call-done = (f32[4,768,384]{2,0,1:T(4,128)}, f32[2,768,384]{2,0,1:T(2,128)}) async-done(((f32[4,768,384]{2,0,1:T(4,128)}, f32[2,768,384]{2,0,1:T(2,128)}), (f32[4,768,384]{2,0,1:T(4,128)}, f32[2,768,384]{2,0,1:T(2,128)})) %all-reduce.21.cloned.1.call-update) | async-done | bytes 7077904
  715.7 124.6 %reduce-scatter.13.cloned.1.call-done = f32[384,48]{0,1:T(8,128)} async-done(((f32[384,768]{0,1:T(8,128)}), f32[384,48]{0,1:T(8,128)}) %reduce-scatter.13.cloned.1.call-update) | async-done | bytes 73744 | tf_op jit(solution)/shard_map/reduce_scatter | solution.py:398
  840.3 126.6 %reduce-scatter.11.cloned.1.call-done = f32[256,48]{0,1:T(8,128)} async-done(((f32[256,768]{0,1:T(8,128)}), f32[256,48]{0,1:T(8,128)}) %reduce-scatter.11.cloned.1.call-update) | async-done | bytes 49168 | tf_op jit(solution)/shard_map/reduce_scatter | solution.py:393
  966.9 141.9 %reduce-scatter.15.cloned.1.call-done = f32[48,1536]{1,0:T(8,128)} async-done(((f32[768,1536]{1,0:T(8,128)}), f32[48,1536]{1,0:T(8,128)}) %reduce-scatter.15.cloned.1.call-update) | async-done | bytes 294928 | tf_op jit(solution)/shard_map/reduce_scatter | solution.py:400
  1108.8 142.2 %reduce-scatter.17.cloned.1.call-done = f32[1536,48]{0,1:T(8,128)} async-done(((f32[1536,768]{0,1:T(8,128)}), f32[1536,48]{0,1:T(8,128)}) %reduce-scatter.17.cloned.1.call-update) | async-done | bytes 294928 | tf_op jit(solution)/shard_map/reduce_scatter | solution.py:401
  (436 shorter events, 129.3 us)
Async XLA Ops:
  7.2 88.7 %copy-start = (bf16[768,1536]{1,0:T(8,128)(2,1)S(1)}, bf16[768,1536]{1,0:T(8,128)(2,1)}, u32[]{:S(2)}) copy-start(bf16[768,1536]{1,0:T(8,128)(2,1)} %param.40) | copy-start | bytes 7077892
  7.2 19.3 %copy-start.24 = (bf16[1,256,768]{2,1,0:T(8,128)(2,1)S(1)}, bf16[1,256,768]{2,1,0:T(8,128)(2,1)}, u32[]{:S(2)}) copy-start(bf16[1,256,768]{2,1,0:T(8,128)(2,1)} %param.23) | copy-start | bytes 1179652
  7.2 17.7 %copy-start.111 = (s32[1,128]{1,0:T(1,128)S(1)}, s32[1,128]{1,0:T(1,128)}, u32[]{:S(2)}) copy-start(s32[1,128]{1,0:T(1,128)} %param.27) | copy-start | bytes 1540
  7.2 17.8 %copy-start.112 = (s32[1,512]{1,0:T(1,128)S(1)}, s32[1,512]{1,0:T(1,128)}, u32[]{:S(2)}) copy-start(s32[1,512]{1,0:T(1,128)} %param.26) | copy-start | bytes 6148
  7.2 17.9 %copy-start.105 = (f32[4,384]{1,0:T(4,128)S(1)}, f32[4,384]{1,0:T(4,128)}, u32[]{:S(2)}) copy-start(f32[4,384]{1,0:T(4,128)} %param.35) | copy-start | bytes 18436
  9.7 16.8 %copy-start.116 = (s32[64]{0:T(128)}, s32[64]{0:T(128)S(1)}, u32[]{:S(2)}) copy-start(s32[64]{0:T(128)S(1)} %fusion.84) | copy-start | bytes 772
  11.3 18.4 %all-to-all-start = ((s32[16,1,8]{2,1,0:T(1,128)}), s32[16,1,8]{2,1,0:T(1,128)S(1)}, u32[]{:S(2)}, u32[]{:S(2)}) async-start(s32[16,1,8]{2,1,0:T(1,128)} %bitcast.6), calls=%async_computation | async-start | bytes 16384 | tf_op jit(solution)/shard_map/all_to_all | solution.py:113
  23.0 45.3 %collective-permute-start = (bf16[2,256,384]{1,2,0:T(8,128)(2,1)}, bf16[2,256,384]{1,2,0:T(8,128)(2,1)}, u32[]{:S(2)}, u32[]{:S(2)}) collective-permute-start(bf16[2,256,384]{1,2,0:T(8,128)(2,1)} %bitcast.13), channel_id=1, source_target_pairs={{0,2},{2,0},{1,3},{3,1},{4,6},{6,4},{5,7},{7,5},{8,10},{10,8},{9,1... | collective-permute-start | bytes 1179656 | tf_op jit(solution)/shard_map/ppermute | solution.py:25
  29.1 29.9 %copy-start.8 = (bf16[2,768,384]{2,1,0:T(8,128)(2,1)S(1)}, bf16[2,768,384]{2,1,0:T(8,128)(2,1)}, u32[]{:S(2)}) copy-start(bf16[2,768,384]{2,1,0:T(8,128)(2,1)} %param.36) | copy-start | bytes 3538948
  29.8 30.9 %copy-start.78 = (s32[16,1,8]{2,1,0:T(1,128)}, s32[16,1,8]{2,1,0:T(1,128)S(1)}, u32[]{:S(2)}) copy-start(s32[16,1,8]{2,1,0:T(1,128)S(1)} %all-to-all-done) | copy-start | bytes 1540
  39.9 13.2 %all-to-all-start.1 = ((bf16[16,8,256]{2,1,0:T(8,128)(2,1)}), bf16[16,8,256]{2,1,0:T(8,128)(2,1)}, u32[]{:S(2)}, u32[]{:S(2)}) async-start(bf16[16,8,256]{2,1,0:T(8,128)(2,1)} %fusion.70), calls=%async_computation.1 | async-start | bytes 131072 | tf_op jit(solution)/shard_map/all_to_all | solution.py:118
  45.5 47.8 %all-reduce.13.cloned.1.call-start = ((), (), s32[]{:S(2)}) async-start(), calls=%async_computation.9 | async-start | bytes 1966080 | tf_op jit(solution)/shard_map/psum | solution.py:43
  60.7 4.9 collective-permute-start.1
  76.9 49.1 %all-reduce.15.cloned.1.call-start = ((), (), s32[]{:S(2)}) async-start(), calls=%async_computation.10 | async-start | bytes 1966080 | tf_op jit(solution)/shard_map/psum | solution.py:43
  105.1 52.2 %all-reduce.17.cloned.1.call-start = ((), (), s32[]{:S(2)}) async-start(), calls=%async_computation.11 | async-start | bytes 1966080 | tf_op jit(solution)/shard_map/psum | solution.py:43
  136.5 89.1 %all-reduce.19.cloned.1.call-start = ((), (), s32[]{:S(2)}) async-start(), calls=%async_computation.12 | async-start | bytes 1966080 | tf_op jit(solution)/shard_map/psum | solution.py:43
  139.3 20.7 %copy-start.92 = (f32[320]{0:T(512)S(1)}, f32[320]{0:T(512)}, u32[]{:S(2)}) copy-start(f32[320]{0:T(512)} %copy-done.91) | copy-start | bytes 3844
  139.3 20.7 %copy-start.73 = (f32[320]{0:T(512)S(1)}, f32[320]{0:T(512)}, u32[]{:S(2)}) copy-start(f32[320]{0:T(512)} %copy-done.72) | copy-start | bytes 3844
  139.3 20.7 %copy-start.76 = (f32[320]{0:T(512)S(1)}, f32[320]{0:T(512)}, u32[]{:S(2)}) copy-start(f32[320]{0:T(512)} %copy-done.75) | copy-start | bytes 3844
  186.2 8.0 collective-permute-start.3
  188.7 13.3 %collective-permute-start.2 = (bf16[2,1,256,6,64]{2,4,3,1,0:T(8,128)(2,1)}, bf16[2,1,256,6,64]{2,4,3,1,0:T(8,128)(2,1)}, u32[]{:S(2)}, u32[]{:S(2)}) collective-permute-start(bf16[2,1,256,6,64]{2,4,3,1,0:T(8,128)(2,1)} %fusion.40), channel_id=1, source_target_pairs={{0,2},{2,0},{1,3},{3,1},{4,6},{6,4},{5,7},{7,5},{8,10},{10,8},{9,1... | collective-permute-start | bytes 1179656 | tf_op jit(solution)/shard_map/ppermute | solution.py:25
  195.4 21.8 %copy-start.32 = (bf16[2,1,64,6,64]{2,4,3,1,0:T(8,128)(2,1)}, bf16[2,1,64,6,64]{2,4,3,1,0:T(8,128)(2,1)S(1)}, u32[]{:S(2)}) copy-start(bf16[2,1,64,6,64]{2,4,3,1,0:T(8,128)(2,1)S(1)} %fusion.45) | copy-start | bytes 294916
  204.7 148.8 %reduce-scatter.21.cloned.1.call-start = ((), (), s32[]{:S(2)}) async-start(), calls=%async_computation.18 | async-start | bytes 417792
  230.5 248.9 %reduce-scatter.19.cloned.1.call-start = ((), (), s32[]{:S(2)}) async-start(), calls=%async_computation.17 | async-start | bytes 417792
  232.5 479.8 %all-reduce.21.cloned.1.call-start = ((), (), s32[]{:S(2)}) async-start(), calls=%async_computation.19 | async-start | bytes 14155776
  241.0 599.3 %reduce-scatter.13.cloned.1.call-start = ((), (), s32[]{:S(2)}) async-start(), calls=%async_computation.14 | async-start | bytes 1253376 | tf_op jit(solution)/shard_map/reduce_scatter | solution.py:398
  243.7 723.2 %reduce-scatter.11.cloned.1.call-start = ((), (), s32[]{:S(2)}) async-start(), calls=%async_computation.13 | async-start | bytes 835584 | tf_op jit(solution)/shard_map/reduce_scatter | solution.py:393
  245.4 863.4 %reduce-scatter.15.cloned.1.call-start = ((), (), s32[]{:S(2)}) async-start(), calls=%async_computation.15 | async-start | bytes 5013504 | tf_op jit(solution)/shard_map/reduce_scatter | solution.py:400
  249.3 1001.6 %reduce-scatter.17.cloned.1.call-start = ((), (), s32[]{:S(2)}) async-start(), calls=%async_computation.16 | async-start | bytes 5013504 | tf_op jit(solution)/shard_map/reduce_scatter | solution.py:401
  263.7 88.9 %slice-start = ((f32[320,768]{1,0:T(8,128)}), f32[256,768]{1,0:T(8,128)S(1)}, s32[]{:S(2)}) async-start(f32[320,768]{1,0:T(8,128)} %copy-done.18), calls=%async_computation.20 | async-start | bytes 1572864 | tf_op jit(solution)/shard_map/slice | solution.py:97
  267.4 213.4 %all-to-all-start.2 = ((bf16[16,8,256]{2,1,0:T(8,128)(2,1)}), bf16[16,8,256]{2,1,0:T(8,128)(2,1)S(1)}, u32[]{:S(2)}, u32[]{:S(2)}) async-start(bf16[16,8,256]{2,1,0:T(8,128)(2,1)} %convert_bitcast_fusion), calls=%async_computation.6 | async-start | bytes 131072 | tf_op jit(solution)/shard_map/all_to_all | solution.py:360
  484.4 766.5 %copy-start.1 = (bf16[768,1536]{1,0:T(8,128)(2,1)S(1)}, bf16[768,1536]{1,0:T(8,128)(2,1)}, u32[]{:S(2)}) copy-start(bf16[768,1536]{1,0:T(8,128)(2,1)} %param.40) | copy-start | bytes 7077892
  (112 other events, 487.0 us)
Sparse Core Ops, SparseCore 0:
  77.0 16.2 all-reduce.12
  105.2 20.6 all-reduce.14
  136.6 20.6 all-reduce.16
  204.8 20.6 all-reduce.18
  230.6 122.8 reduce-scatter.20
  358.7 120.6 reduce-scatter.18
  485.8 226.4 all-reduce.20
  717.6 122.6 reduce-scatter.12
  845.6 121.2 reduce-scatter.10
  972.5 136.2 reduce-scatter.14
  1115.3 135.5 reduce-scatter.16
where the time goes:
time: 1270 us; the launch traced here: 1260 us
  waiting for transfers between devices  952 us (75%)
  blocking collectives  77.1 us (6%)
  matrix products  65.8 us (5%)
  local copies, waits for them, and re-layouts  61.7 us (5%)
  other arithmetic  58.1 us (5%)
  starting transfers between devices  26.6 us (2%)
  between operations  16.5 us (1%)
    unnamed x14, waiting for transfers between devices  341 us
    reduce_scatter x1, waiting for transfers between devices, local(): lax.psum_scatter(grad_down, ('dp', 'stream'), scatter_dimension=1, tiled=...  142 us
    reduce_scatter x1, waiting for transfers between devices, local(): lax.psum_scatter(grad_up, ('dp', 'stream'), scatter_dimension=0, tiled=True)  142 us
    reduce_scatter x1, waiting for transfers between devices, local(): lax.psum_scatter(grad_entity, ('dp', 'stream'), scatter_dimension=1, tile...  127 us
    reduce_scatter x1, waiting for transfers between devices, local(): lax.psum_scatter(grad_out, ('dp', 'stream'), scatter_dimension=1, tiled=T...  125 us
    psum x1, blocking collectives, local(): lax.psum((grad_query_bias, grad_value_bias, grad_up_bias), ('dp', 'stream'))  77.1 us
    psum x4, waiting for transfers between devices, tensor_total(): return lax.psum(values_in, 'tensor')  61.1 us
  transfers between devices with their start and end apart: 18, of which 15 were waited for; matrix products, arithmetic and copies ran while one was open for 9% of the time, Pallas kernels for 0%

commit v1 on v0

--- a/solution.py
+++ b/solution.py
@@ -1,9 +1,168 @@
+import functools
+
 import jax
 import jax.numpy as jnp
 from jax import lax
+from jax.experimental import pallas as pl
+from jax.experimental.pallas import tpu as pltpu
 from jax.sharding import PartitionSpec as P
 
 HD = 64
+MESH_ID = pl.DeviceIdType.MESH
+CHUNK = 384
+
+
+def greet(peers):
+    barrier = pltpu.get_barrier_semaphore()
+    for peer in peers:
+        pl.semaphore_signal(barrier, inc=1, device_id=peer, device_id_type=MESH_ID)
+    pl.semaphore_wait(barrier, len(peers))
+
+
+def send(source, target, send_sem, recv_sem, peer):
+    return pltpu.make_async_remote_copy(
+        src_ref=source,
+        dst_ref=target,
+        send_sem=send_sem,
+        recv_sem=recv_sem,
+        device_id=peer,
+        device_id_type=MESH_ID,
+    )
+
+
+def pair_kernel(part_ref, total_ref, far, send_sem, recv_sem):
+    peer = {"tensor": 1 - lax.axis_index("tensor")}
+    greet([peer])
+    copy = send(part_ref, far, send_sem, recv_sem, peer)
+    copy.start()
+    copy.wait()
+    total_ref[...] = part_ref[...] + far[...]
+
+
+def pair_total(part):
+    return pl.pallas_call(
+        pair_kernel,
+        out_shape=jax.ShapeDtypeStruct(part.shape, part.dtype),
+        in_specs=[pl.BlockSpec(memory_space=pltpu.VMEM)],
+        out_specs=pl.BlockSpec(memory_space=pltpu.VMEM),
+        scratch_shapes=[
+            pltpu.VMEM(part.shape, part.dtype),
+            pltpu.SemaphoreType.DMA,
+            pltpu.SemaphoreType.DMA,
+        ],
+        compiler_params=pltpu.CompilerParams(collective_id=0, has_side_effects=True),
+    )(part)
+
+
+def scatter_kernel(grads, out, near1, near2, part1, part2, far3, s1, r1, s2, r2, s3, r3):
+    chunks, deep = grads.shape[0], grads.shape[1]
+    dp, x = lax.axis_index("dp"), lax.axis_index("stream")
+    y, z = lax.rem(dp, 2), dp // 2
+    x_peer, y_peer = {"stream": 1 - x}, {"dp": z * 2 + 1 - y}
+    z_peers = [{"dp": lax.rem(z + k, deep) * 2 + y} for k in range(1, deep)]
+    greet([x_peer, y_peer] + z_peers)
+
+    def first(c, flip):
+        if flip:
+            return send(grads.at[c, :, 1 - y], near1.at[c], s1.at[c], r1.at[c], y_peer)
+        return send(grads.at[c, :, :, 1 - x], near1.at[c], s1.at[c], r1.at[c], x_peer)
+
+    def second(c, flip):
+        if flip:
+            return send(part1.at[c, :, 1 - x], near2.at[c], s2.at[c], r2.at[c], x_peer)
+        return send(part1.at[c, :, 1 - y], near2.at[c], s2.at[c], r2.at[c], y_peer)
+
+    def third(c, k):
+        target = lax.rem(z + k, deep)
+        return send(
+            part2.at[c, target], far3.at[c, k - 1], s3.at[c, k - 1], r3.at[c, k - 1], z_peers[k - 1]
+        )
+
+    def add_first(c, flip):
+        own = grads.at[c, :, y] if flip else grads.at[c, :, :, x]
+        total = own[...].astype(jnp.float32) + near1[c].astype(jnp.float32)
+        part1[c] = total.astype(jnp.bfloat16)
+
+    def add_second(c, flip):
+        own = part1.at[c, :, x] if flip else part1.at[c, :, y]
+        total = own[...].astype(jnp.float32) + near2[c].astype(jnp.float32)
+        part2[c] = total.astype(jnp.bfloat16)
+
+    def to_second(c, flip):
+        first(c, flip).wait()
+        add_first(c, flip)
+        second(c, flip).start()
+
+    def to_third(c, flip):
+        second(c, flip).wait()
+        add_second(c, flip)
+        for k in range(1, deep):
+            third(c, k).start()
+
+    ahead = 2
+    pairs = chunks // 2
+
+    def each(pair, what):
+        what(2 * pair, False)
+        what(2 * pair + 1, True)
+
+    for pair in range(ahead):
+        each(pair, lambda c, flip: first(c, flip).start())
+
+    def body(pair, carry):
+        @pl.when(pair < pairs)
+        def _():
+            each(pair, to_second)
+
+        @pl.when(pair + ahead < pairs)
+        def _():
+            each(pair + ahead, lambda c, flip: first(c, flip).start())
+
+        @pl.when(pair >= 1)
+        def _():
+            each(pair - 1, to_third)
+
+        return carry
+
+    lax.fori_loop(0, pairs + 1, body, 0)
+
+    def finish(c, carry):
+        for k in range(1, deep):
+            third(c, k).wait()
+        total = part2[c, z].astype(jnp.float32)
+        for k in range(1, deep):
+            total = total + far3[c, k - 1].astype(jnp.float32)
+        out[c] = total
+        return carry
+
+    lax.fori_loop(0, chunks, finish, 0)
+
+
+def scatter_total(grads):
+    chunks, deep, _, _, rows, width = grads.shape
+    low = jnp.bfloat16
+    return pl.pallas_call(
+        scatter_kernel,
+        out_shape=jax.ShapeDtypeStruct((chunks, rows, width), jnp.float32),
+        in_specs=[pl.BlockSpec(memory_space=pltpu.VMEM)],
+        out_specs=pl.BlockSpec(memory_space=pltpu.VMEM),
+        scratch_shapes=[
+            pltpu.VMEM((chunks, deep, 2, rows, width), low),
+            pltpu.VMEM((chunks, deep, rows, width), low),
+            pltpu.VMEM((chunks, deep, 2, rows, width), low),
+            pltpu.VMEM((chunks, deep, rows, width), low),
+            pltpu.VMEM((chunks, deep - 1, rows, width), low),
+            pltpu.SemaphoreType.DMA((chunks,)),
+            pltpu.SemaphoreType.DMA((chunks,)),
+            pltpu.SemaphoreType.DMA((chunks,)),
+            pltpu.SemaphoreType.DMA((chunks,)),
+            pltpu.SemaphoreType.DMA((chunks, deep - 1)),
+            pltpu.SemaphoreType.DMA((chunks, deep - 1)),
+        ],
+        compiler_params=pltpu.CompilerParams(
+            collective_id=1, has_side_effects=True, vmem_limit_bytes=60 * 2**20
+        ),
+    )(grads)
 
 
 norm_eps = 1e-05
@@ -40,6 +199,8 @@
 
 
 def tensor_total(values_in):
+    if lax.axis_size("tensor") == 2:
+        return pair_total(values_in)
     return lax.psum(values_in, "tensor")
 
 
@@ -378,32 +539,48 @@
     table_update = jnp.where(touched, direction, jnp.zeros_like(direction))
     new_first = jnp.where(touched, first_next, adam_first)
     new_second = jnp.where(touched, second_next, adam_second)
-    (
-        red_entity,
-        red_gain,
-        red_shift,
-        red_query,
-        red_keyval,
-        red_out,
-        red_out_bias,
-        red_up,
-        red_down,
-        red_down_bias,
-    ) = (
-        lax.psum_scatter(grad_entity, ("dp", "stream"), scatter_dimension=1, tiled=True),
-        lax.psum_scatter(gain_grads, ("dp", "stream"), scatter_dimension=1, tiled=True),
-        lax.psum_scatter(shift_grads, ("dp", "stream"), scatter_dimension=1, tiled=True),
-        lax.psum_scatter(grad_query, ("dp", "stream"), scatter_dimension=1, tiled=True),
-        lax.psum_scatter(grad_keyval, ("dp", "stream"), scatter_dimension=1, tiled=True),
-        lax.psum_scatter(grad_out, ("dp", "stream"), scatter_dimension=1, tiled=True),
-        lax.psum_scatter(grad_out_bias, ("dp", "stream"), scatter_dimension=0, tiled=True),
-        lax.psum_scatter(grad_up, ("dp", "stream"), scatter_dimension=0, tiled=True),
-        lax.psum_scatter(grad_down, ("dp", "stream"), scatter_dimension=1, tiled=True),
-        lax.psum_scatter(grad_down_bias, ("dp", "stream"), scatter_dimension=0, tiled=True),
-    )
-    red_query_bias, red_value_bias, red_up_bias = lax.psum(
-        (grad_query_bias, grad_value_bias, grad_up_bias), ("dp", "stream")
-    )
+    groups = ("dp", "stream")
+    share = width // owners
+    if parts == 2 and lax.axis_size("stream") == 2 and share % 16 == 0 and local_width == CHUNK:
+        pieces = (
+            [block.T for block in jnp.split(grad_down, grad_down.shape[0] // CHUNK, 0)]
+            + jnp.split(grad_up, grad_up.shape[1] // CHUNK, 1)
+            + [grad_out.T, *grad_query, *grad_keyval]
+            + [jnp.pad(grad_entity.T, ((0, 0), (0, CHUNK - embed_width)))]
+        )
+        stacked = jnp.stack([piece.astype(jnp.bfloat16) for piece in pieces])
+        reduced = scatter_total(
+            stacked.reshape(len(pieces), owners // 4, 2, 2, share, CHUNK)
+        )
+        downs = grad_down.shape[0] // CHUNK
+        ups = grad_up.shape[1] // CHUNK
+        red_down = jnp.transpose(reduced[:downs], (0, 2, 1)).reshape(grad_down.shape[0], share)
+        red_up = jnp.transpose(reduced[downs : downs + ups], (1, 0, 2)).reshape(share, -1)
+        base = downs + ups
+        red_out = reduced[base].T
+        red_query = reduced[base + 1 : base + 5]
+        red_keyval = reduced[base + 5 : base + 7]
+        red_entity = reduced[base + 7, :, :embed_width].T
+    else:
+        red_entity, red_query, red_keyval, red_out, red_up, red_down = (
+            lax.psum_scatter(grad_entity, groups, scatter_dimension=1, tiled=True),
+            lax.psum_scatter(grad_query, groups, scatter_dimension=1, tiled=True),
+            lax.psum_scatter(grad_keyval, groups, scatter_dimension=1, tiled=True),
+            lax.psum_scatter(grad_out, groups, scatter_dimension=1, tiled=True),
+            lax.psum_scatter(grad_up, groups, scatter_dimension=0, tiled=True),
+            lax.psum_scatter(grad_down, groups, scatter_dimension=1, tiled=True),
+        )
+    across = jnp.concatenate([gain_grads, shift_grads, grad_out_bias[None], grad_down_bias[None]], 0)
+    small = [across, grad_query_bias, grad_value_bias, grad_up_bias]
+    flat = lax.psum(jnp.concatenate([item.reshape(-1) for item in small]), groups)
+    totals = []
+    for item in small:
+        totals.append(flat[: item.size].reshape(item.shape))
+        flat = flat[item.size :]
+    across, red_query_bias, red_value_bias, red_up_bias = totals
+    own = lax.axis_index(groups) * share
+    across = lax.dynamic_slice_in_dim(across, own, share, 1)
+    red_gain, red_shift, red_out_bias, red_down_bias = across[:3], across[3:6], across[6], across[7]
     return (
         out_words,
         out_entities,

time: 1270 us -> 424 us (0.33)
  waiting for transfers between devices: 952 us -> 6.1 us
  Pallas kernels: 0 us -> 116 us
  local copies, waits for them, and re-layouts: 61.7 us -> 78.5 us
  between operations: 16.5 us -> 2.5 us
    reduce_scatter x4 -> x0, waiting for transfers between devices: 535 us -> none  [the longest x1 142 us: local(): lax.psum_scatter(grad_down, ('dp', 'stream'), scatter_dimension=1, tiled=...]
    unnamed x14 -> x0, waiting for transfers between devices: 341 us -> none
    pallas_call x0 -> x5, Pallas kernels: none -> 116 us  [the longest x1 96 us: scatter_total(): pl.pallas_call(scatter_kernel, out_shape=jax.ShapeDtypeStruct((chunks, ro...]
    psum x4 -> x0, waiting for transfers between devices: 61.1 us -> none  [tensor_total(): return lax.psum(values_in, 'tensor')]
  transfers between devices with their start and end apart: 18 -> 7, of which waited for: 15 -> 3; matrix products, arithmetic and copies ran while one was open for 9% -> 20% of each run, Pallas kernels for 0% -> 0%
where the time goes in v1:
time: 424 us; the launch traced here: 418 us
  Pallas kernels  116 us (27%)
  local copies, waits for them, and re-layouts  78.5 us (19%)
  blocking collectives  75.5 us (18%)
  matrix products  59.8 us (14%)
  other arithmetic  58.2 us (14%)
  starting transfers between devices  22.2 us (5%)
  waiting for transfers between devices  6.1 us (1%)
    pallas_call x1, Pallas kernels, scatter_total(): pl.pallas_call(scatter_kernel, out_shape=jax.ShapeDtypeStruct((chunks, ro...  96 us
    psum x1, blocking collectives, local(): lax.psum(jnp.concatenate([item.reshape(-1) for item in small]), groups)  75.5 us
    unnamed x274, local copies, waits for them, and re-layouts  24.4 us
    pallas_call x4, Pallas kernels, pair_total(): pl.pallas_call(pair_kernel, out_shape=jax.ShapeDtypeStruct(part.shape, pa...  19.7 us
    select_n x1, other arithmetic, local(): new_second = jnp.where(touched, second_next, adam_second)  12 us
    dot_general x4, matrix products, matmul(): return jnp.dot(matrix_a, matrix_b, preferred_element_type=jnp.float32)  11.3 us
    another operation x9, local copies, waits for them, and re-layouts, local(): pieces = [block.T for block in jnp.split(grad_down, grad_down.shape[0] //...  10.3 us
  transfers between devices with their start and end apart: 7, of which 3 were waited for; matrix products, arithmetic and copies ran while one was open for 20% of the time, Pallas kernels for 0%

profile of v1, /device:TPU:0, one launch (start us, length us, event | category | flops | bytes accessed | tf_op | source)
XLA Modules:
  0.0 418.4 jit_solution(3494127596968281819)
XLA Ops:
  4.8 8.3 %all-to-all-start = ((s32[16,1,8]{2,1,0:T(1,128)}), s32[16,1,8]{2,1,0:T(1,128)S(1)}, u32[]{:S(2)}, u32[]{:S(2)}) async-start(s32[16,1,8]{2,1,0:T(1,128)} %bitcast.6), calls=%async_computation | async-start | bytes 16384 | tf_op jit(solution)/shard_map/all_to_all | solution.py:274
  13.8 2.6 fusion.19
  22.9 2.7 fusion.20
  33.4 3.2 gather_fusion
  38.3 5.6 %all-to-all-start.1 = ((bf16[16,8,256]{2,1,0:T(8,128)(2,1)}), bf16[16,8,256]{2,1,0:T(8,128)(2,1)}, u32[]{:S(2)}, u32[]{:S(2)}) async-start(bf16[16,8,256]{2,1,0:T(8,128)(2,1)} %fusion.72), calls=%async_computation.1 | async-start | bytes 131072 | tf_op jit(solution)/shard_map/all_to_all | solution.py:279
  51.5 2.2 gather_fusion.1
  61.4 2.4 collective-permute-done.1
  66.4 2.1 fusion.3
  71.0 2.3 fusion.22
  76.0 4.9 %shard_map.366 = f32[320,768]{1,0:T(8,128)} custom-call(f32[320,768]{1,0:T(8,128)} %fusion.58.part_ref), custom_call_target="tpu_custom_call" | custom-call | tf_op jit(solution)/shard_map/pallas_call | solution.py:43
  83.6 6.6 %multiply_convert_fusion.1 = (bf16[320,1536]{1,0:T(8,128)(2,1)S(1)}, f32[320,1536]{1,0:T(8,128)}, f32[320,1536]{1,0:T(8,128)}) fusion(f32[1536]{0:T(1024)S(1)} %copy-done.121, bf16[768,1536]{1,0:T(8,128)(2,1)S(1)} %copy-done, f32[320,768]{1,0:T(8,128)S(1)} %get-tuple-element.52, f32[768]{0:T(1024)S(1)} %copy-done.94, f32[768]{0:T(1024)S(1)} %copy-done.78, ...), kind=kOutput, calls=%fused_computation.29 | convolution fusion | flops 788643840 | bytes 8272384 | tf_op jit(solution)/shard_map/dot_general | solution.py:198
  93.1 4.8 %shard_map.367 = f32[320,768]{1,0:T(8,128)} custom-call(f32[320,768]{1,0:T(8,128)} %fusion.131.part_ref), custom_call_target="tpu_custom_call" | custom-call | tf_op jit(solution)/shard_map/pallas_call | solution.py:43
  104.4 2.1 convert_reduce_fusion
  109.4 5.0 %shard_map.368 = f32[320,768]{1,0:T(8,128)} custom-call(f32[320,768]{1,0:T(8,128)} %fusion.132.part_ref), custom_call_target="tpu_custom_call" | custom-call | tf_op jit(solution)/shard_map/pallas_call | solution.py:43
  114.5 2.4 multiply_reduce_fusion.1
  121.6 2.1 convolution_bitcast_fusion.3
  125.6 4.0 multiply_reduce_fusion
  136.4 2.1 convolution_bitcast_fusion.2
  138.5 2.8 convolution_convert_fusion.1
  141.4 3.0 convolution_convert_fusion
  146.2 2.8 convolution_bitcast_fusion.1
  163.0 2.1 copy.130
  165.1 2.2 copy.131
  169.2 2.2 copy.133
  198.6 5.0 %shard_map.369 = f32[320,768]{1,0:T(8,128)} custom-call(f32[320,768]{1,0:T(8,128)} %pad_maximum_fusion.part_ref), custom_call_target="tpu_custom_call" | custom-call | tf_op jit(solution)/shard_map/pallas_call | solution.py:43
  203.7 2.4 add_add_fusion.3
  211.7 96.0 %shard_map.370 = f32[16,48,384]{2,1,0:T(8,128)} custom-call(bf16[16,4,2,2,48,384]{5,4,3,2,1,0:T(8,128)(2,1)} %constant_dynamic-update-slice_fusion.grads), custom_call_target="tpu_custom_call" | custom-call | tf_op jit(solution)/shard_map/pallas_call | solution.py:144
  311.4 75.5 %psum.7 = f32[9600]{0:T(1024)S(1)} all-reduce(f32[9600]{0:T(1024)S(1)} %pad_maximum_fusion.14), channel_id=1, replica_groups=mesh['dp'=8,'stream'=2,'tensor'=2] {'dp','stream'}, use_global_device_ids=true, to_apply=%region_34.35 | all-reduce | flops 9600 | bytes 76800 | tf_op jit(solution)/shard_map/psum | solution.py:575
  391.6 3.5 all-to-all-start.2
  400.6 2.0 all-to-all-done.2
  402.6 3.6 scatter_custom_fusion.3
  406.2 12.0 %fusion.2 = (f32[4096,256]{1,0:T(8,128)}, f32[4096,256]{1,0:T(8,128)}, f32[4096,256]{1,0:T(8,128)}) fusion(f32[4096,256]{1,0:T(8,128)} %param.30, f32[4096,256]{1,0:T(8,128)} %scatter_custom_fusion.3, pred[4096]{0:T(1024)(128)(4,1)S(1)} %copy-done.97, f32[4096,256]{1,0:T(8,128)} %param.29), kind=kLoop, calls=%fused_computation.18 | loop fusion | flops 14680064 | bytes 25169920 | tf_op jit(solution)/shard_map/jit(_where)/select_n | solution.py:541
  (456 shorter events, 135.4 us)
Async XLA Ops:
  0.7 82.9 %copy-start = (bf16[768,1536]{1,0:T(8,128)(2,1)S(1)}, bf16[768,1536]{1,0:T(8,128)(2,1)}, u32[]{:S(2)}) copy-start(bf16[768,1536]{1,0:T(8,128)(2,1)} %param.40) | copy-start | bytes 7077892
  0.7 18.3 %copy-start.22 = (bf16[1,256,768]{2,1,0:T(8,128)(2,1)S(1)}, bf16[1,256,768]{2,1,0:T(8,128)(2,1)}, u32[]{:S(2)}) copy-start(bf16[1,256,768]{2,1,0:T(8,128)(2,1)} %param.23) | copy-start | bytes 1179652
  0.7 19.3 %copy-start.110 = (f32[4,384]{1,0:T(4,128)S(1)}, f32[4,384]{1,0:T(4,128)}, u32[]{:S(2)}) copy-start(f32[4,384]{1,0:T(4,128)} %param.35) | copy-start | bytes 18436
  0.7 19.8 %copy-start.114 = (s32[1,128]{1,0:T(1,128)S(1)}, s32[1,128]{1,0:T(1,128)}, u32[]{:S(2)}) copy-start(s32[1,128]{1,0:T(1,128)} %param.27) | copy-start | bytes 1540
  0.7 20.0 %copy-start.115 = (s32[1,512]{1,0:T(1,128)S(1)}, s32[1,512]{1,0:T(1,128)}, u32[]{:S(2)}) copy-start(s32[1,512]{1,0:T(1,128)} %param.26) | copy-start | bytes 6148
  0.7 21.6 %copy-start.108 = (f32[3,768]{1,0:T(4,128)S(1)}, f32[3,768]{1,0:T(4,128)}, u32[]{:S(2)}) copy-start(f32[3,768]{1,0:T(4,128)} %param.33) | copy-start | bytes 27652
  0.7 21.6 %copy-start.109 = (f32[3,768]{1,0:T(4,128)S(1)}, f32[3,768]{1,0:T(4,128)}, u32[]{:S(2)}) copy-start(f32[3,768]{1,0:T(4,128)} %param.32) | copy-start | bytes 27652
  3.2 17.3 %copy-start.118 = (s32[64]{0:T(128)}, s32[64]{0:T(128)S(1)}, u32[]{:S(2)}) copy-start(s32[64]{0:T(128)S(1)} %fusion.86) | copy-start | bytes 772
  4.8 20.8 %all-to-all-start = ((s32[16,1,8]{2,1,0:T(1,128)}), s32[16,1,8]{2,1,0:T(1,128)S(1)}, u32[]{:S(2)}, u32[]{:S(2)}) async-start(s32[16,1,8]{2,1,0:T(1,128)} %bitcast.6), calls=%async_computation | async-start | bytes 16384 | tf_op jit(solution)/shard_map/all_to_all | solution.py:274
  16.5 49.9 %collective-permute-start = (bf16[2,256,384]{1,2,0:T(8,128)(2,1)}, bf16[2,256,384]{1,2,0:T(8,128)(2,1)}, u32[]{:S(2)}, u32[]{:S(2)}) collective-permute-start(bf16[2,256,384]{1,2,0:T(8,128)(2,1)} %bitcast.13), channel_id=1, source_target_pairs={{0,2},{2,0},{1,3},{3,1},{4,6},{6,4},{5,7},{7,5},{8,10},{10,8},{9,1... | collective-permute-start | bytes 1179656 | tf_op jit(solution)/shard_map/ppermute | solution.py:184
  22.9 34.4 %copy-start.6 = (bf16[2,768,384]{2,1,0:T(8,128)(2,1)S(1)}, bf16[2,768,384]{2,1,0:T(8,128)(2,1)}, u32[]{:S(2)}) copy-start(bf16[2,768,384]{2,1,0:T(8,128)(2,1)} %param.36) | copy-start | bytes 3538948
  36.7 23.2 %copy-start.113 = (f32[2,384]{1,0:T(2,128)S(1)}, f32[2,384]{1,0:T(2,128)}, u32[]{:S(2)}) copy-start(f32[2,384]{1,0:T(2,128)} %get-tuple-element.78) | copy-start | bytes 9220
  38.3 13.2 %all-to-all-start.1 = ((bf16[16,8,256]{2,1,0:T(8,128)(2,1)}), bf16[16,8,256]{2,1,0:T(8,128)(2,1)}, u32[]{:S(2)}, u32[]{:S(2)}) async-start(bf16[16,8,256]{2,1,0:T(8,128)(2,1)} %fusion.72), calls=%async_computation.1 | async-start | bytes 131072 | tf_op jit(solution)/shard_map/all_to_all | solution.py:279
  59.0 4.8 %collective-permute-start.1 = (bf16[2,64,384]{2,1,0:T(8,128)(2,1)}, bf16[2,64,384]{2,1,0:T(8,128)(2,1)S(1)}, u32[]{:S(2)}, u32[]{:S(2)}) collective-permute-start(bf16[2,64,384]{2,1,0:T(8,128)(2,1)} %fusion.33), channel_id=1, source_target_pairs={{0,2},{2,0},{1,3},{3,1},{4,6},{6,4},{5,7},{7,5},{8,10},{10,8},{9,1... | collective-permute-start | bytes 294920 | tf_op jit(solution)/shard_map/ppermute | solution.py:184
  154.3 37.4 %collective-permute-start.3 = (bf16[2,1,64,6,64]{2,4,3,1,0:T(8,128)(2,1)}, bf16[2,1,64,6,64]{2,4,3,1,0:T(8,128)(2,1)}, u32[]{:S(2)}, u32[]{:S(2)}) collective-permute-start(bf16[2,1,64,6,64]{2,4,3,1,0:T(8,128)(2,1)} %fusion.47), channel_id=1, source_target_pairs={{0,2},{2,0},{1,3},{3,1},{4,6},{6,4},{5,7},{7,5},{8,10},{10,8},{9,1... | collective-permute-start | bytes 294920 | tf_op jit(solution)/shard_map/ppermute | solution.py:184
  156.9 38.8 %collective-permute-start.2 = (bf16[2,1,256,6,64]{2,4,3,1,0:T(8,128)(2,1)}, bf16[2,1,256,6,64]{2,4,3,1,0:T(8,128)(2,1)}, u32[]{:S(2)}, u32[]{:S(2)}) collective-permute-start(bf16[2,1,256,6,64]{2,4,3,1,0:T(8,128)(2,1)} %fusion.43), channel_id=1, source_target_pairs={{0,2},{2,0},{1,3},{3,1},{4,6},{6,4},{5,7},{7,5},{8,10},{10,8},{9,1... | collective-permute-start | bytes 1179656 | tf_op jit(solution)/shard_map/ppermute | solution.py:184
  167.2 12.4 %slice-start.1 = ((bf16[320,768]{1,0:T(8,128)(2,1)}), bf16[256,768]{1,0:T(8,128)(2,1)S(1)}, s32[]{:S(2)}) async-start(bf16[320,768]{1,0:T(8,128)(2,1)} %copy-done.47), calls=%async_computation.4 | async-start | bytes 786432 | tf_op jit(solution)/shard_map/slice | solution.py:258
  168.2 12.2 %copy-start.38 = (bf16[384,768]{0,1:T(8,128)(2,1)S(1)}, bf16[384,768]{0,1:T(8,128)(2,1)}, u32[]{:S(2)}) copy-start(bf16[384,768]{0,1:T(8,128)(2,1)} %get-tuple-element.64) | copy-start | bytes 1769476
  168.2 13.1 %copy-start.37 = (bf16[384,768]{0,1:T(8,128)(2,1)S(1)}, bf16[384,768]{0,1:T(8,128)(2,1)}, u32[]{:S(2)}) copy-start(bf16[384,768]{0,1:T(8,128)(2,1)} %get-tuple-element.63) | copy-start | bytes 1769476
  168.2 13.9 %copy-start.35 = (bf16[384,768]{0,1:T(8,128)(2,1)S(1)}, bf16[384,768]{0,1:T(8,128)(2,1)}, u32[]{:S(2)}) copy-start(bf16[384,768]{0,1:T(8,128)(2,1)} %get-tuple-element.62) | copy-start | bytes 1769476
  169.2 13.8 %copy-start.36 = (bf16[768,384]{1,0:T(8,128)(2,1)S(1)}, bf16[768,384]{1,0:T(8,128)(2,1)}, u32[]{:S(2)}) copy-start(bf16[768,384]{1,0:T(8,128)(2,1)} %get-tuple-element.61) | copy-start | bytes 1769476
  211.7 99.5 %copy-start.99 = (f32[1,768]{1,0:T(1,128)S(1)}, f32[1,768]{1,0:T(1,128)}, u32[]{:S(2)}) copy-start(f32[1,768]{1,0:T(1,128)} %reshape.684) | copy-start | bytes 9220
  211.7 99.5 %copy-start.100 = (f32[1,768]{1,0:T(1,128)S(1)}, f32[1,768]{1,0:T(1,128)}, u32[]{:S(2)}) copy-start(f32[1,768]{1,0:T(1,128)} %reshape.685) | copy-start | bytes 9220
  211.7 99.5 %copy-start.101 = (f32[1,768]{1,0:T(1,128)S(1)}, f32[1,768]{1,0:T(1,128)}, u32[]{:S(2)}) copy-start(f32[1,768]{1,0:T(1,128)} %reshape.687) | copy-start | bytes 9220
  211.7 99.6 %copy-start.102 = (f32[1,768]{1,0:T(1,128)S(1)}, f32[1,768]{1,0:T(1,128)}, u32[]{:S(2)}) copy-start(f32[1,768]{1,0:T(1,128)} %reshape.688) | copy-start | bytes 9220
  211.7 99.6 %copy-start.103 = (f32[1,768]{1,0:T(1,128)S(1)}, f32[1,768]{1,0:T(1,128)}, u32[]{:S(2)}) copy-start(f32[1,768]{1,0:T(1,128)} %broadcast_in_dim.147) | copy-start | bytes 9220
  211.7 99.6 %copy-start.104 = (f32[1,768]{1,0:T(1,128)S(1)}, f32[1,768]{1,0:T(1,128)}, u32[]{:S(2)}) copy-start(f32[1,768]{1,0:T(1,128)} %broadcast_in_dim.148) | copy-start | bytes 9220
  211.7 99.6 %copy-start.105 = (f32[1536]{0:T(1024)S(1)}, f32[1536]{0:T(1024)}, u32[]{:S(2)}) copy-start(f32[1536]{0:T(1024)} %get-tuple-element.38) | copy-start | bytes 18436
  307.7 81.2 %copy-start.55 = (bf16[256,768]{1,0:T(8,128)(2,1)S(1)}, bf16[256,768]{1,0:T(8,128)(2,1)}, u32[]{:S(2)}) copy-start(bf16[256,768]{1,0:T(8,128)(2,1)} %param.31) | copy-start | bytes 1179652
  311.3 88.5 %slice-start = ((f32[320,768]{1,0:T(8,128)}), f32[256,768]{1,0:T(8,128)S(1)}, s32[]{:S(2)}) async-start(f32[320,768]{1,0:T(8,128)} %add_add_fusion.3), calls=%async_computation.3 | async-start | bytes 1572864 | tf_op jit(solution)/shard_map/slice | solution.py:258
  391.6 11.0 %all-to-all-start.2 = ((bf16[16,8,256]{2,1,0:T(8,128)(2,1)}), bf16[16,8,256]{2,1,0:T(8,128)(2,1)S(1)}, u32[]{:S(2)}, u32[]{:S(2)}) async-start(bf16[16,8,256]{2,1,0:T(8,128)(2,1)} %convert_bitcast_fusion), calls=%async_computation.2 | async-start | bytes 131072 | tf_op jit(solution)/shard_map/all_to_all | solution.py:521
  406.2 12.0 %copy-start.1 = (bf16[768,1536]{1,0:T(8,128)(2,1)S(1)}, bf16[768,1536]{1,0:T(8,128)(2,1)}, u32[]{:S(2)}) copy-start(bf16[768,1536]{1,0:T(8,128)(2,1)} %param.40) | copy-start | bytes 7077892
  (111 other events, 386.0 us)

commit v2 on v0

--- a/solution.py
+++ b/solution.py
@@ -1,9 +1,16 @@
+import functools
+import math
+import types
+
 import jax
 import jax.numpy as jnp
 from jax import lax
+from jax.experimental import pallas as pl
+from jax.experimental.pallas import tpu as pltpu
 from jax.sharding import PartitionSpec as P
 
 HD = 64
+MESH_ID = pl.DeviceIdType.MESH
 
 
 norm_eps = 1e-05
@@ -43,7 +50,1043 @@
     return lax.psum(values_in, "tensor")
 
 
-def local(
+def send(source, target, send_sem, recv_sem, peer):
+    return pltpu.make_async_remote_copy(
+        src_ref=source,
+        dst_ref=target,
+        send_sem=send_sem,
+        recv_sem=recv_sem,
+        device_id=peer,
+        device_id_type=MESH_ID,
+    )
+
+
+def row_sum(block):
+    return jnp.sum(block, 0, keepdims=True)
+
+
+def lane_mean(block):
+    return jnp.mean(block, -1, keepdims=True)
+
+
+def dot_nn(left, right):
+    return jnp.dot(left, right, preferred_element_type=jnp.float32)
+
+
+def dot_nt(left, right):
+    return lax.dot_general(
+        left, right, (((1,), (1,)), ((), ())), preferred_element_type=jnp.float32
+    )
+
+
+def dot_tn(left, right):
+    return lax.dot_general(
+        left, right, (((0,), (0,)), ((), ())), preferred_element_type=jnp.float32
+    )
+
+
+def normalize(rows):
+    center = rows - lane_mean(rows)
+    scale = lax.rsqrt(lane_mean(center * center) + norm_eps)
+    return center * scale, scale
+
+
+def normalize_back(grad, normed, scale, gain):
+    inner = grad * gain
+    return scale * (inner - lane_mean(inner) - normed * lane_mean(inner * normed))
+
+
+def aligned(index, step):
+    return pl.ds(pl.multiple_of(index * step, step), step)
+
+
+def layer_kernel(names, flips, schedule, *refs):
+    r = types.SimpleNamespace(**dict(zip(names, refs, strict=True)))
+    low, full = jnp.bfloat16, jnp.float32
+    dp, x, t = lax.axis_index("dp"), lax.axis_index("stream"), lax.axis_index("tensor")
+    y, z = lax.rem(dp, 2), dp // 2
+    deep = lax.axis_size("dp") // 2
+    owners = 4 * deep
+    half_words, width = r.words.shape
+    half_ents = r.shard.shape[1]
+    rows, words = half_words + half_ents, 2 * half_words
+    everyone = 2 * rows
+    capacity = r.ask.shape[1]
+    slots = owners * capacity
+    heads = r.prob.shape[0]
+    share = width // owners
+    side = heads * HD
+    hidden = r.w_up.shape[1]
+    block = half_ents
+    blocks = rows // block
+    word_blocks = half_words // block
+    wide = 256
+
+    core, x_peer, y_peer = {"tensor": 1 - t}, {"stream": 1 - x}, {"dp": z * 2 + 1 - y}
+    z_peers = [{"dp": lax.rem(z + k, deep) * 2 + y} for k in range(1, deep)]
+    flat = dp * 2 + x
+    others = []
+    for k in range(1, owners):
+        other = lax.rem(flat + k, owners)
+        others.append((other, {"dp": other // 2, "stream": lax.rem(other, 2)}))
+
+    barrier = pltpu.get_barrier_semaphore()
+    for peer in [core] + [peer for _, peer in others]:
+        pl.semaphore_signal(barrier, inc=1, device_id=peer, device_id_type=MESH_ID)
+
+    loads = {}
+
+    def load(source, target):
+        loads[id(target)] = pltpu.make_async_copy(source, target, r.load_s.at[len(loads)])
+        loads[id(target)].start()
+
+    def loaded(target):
+        loads.pop(id(target)).wait()
+
+    load(r.hbm_query, r.w_query)
+    load(r.hbm_keyval, r.w_keyval)
+    load(r.hbm_table, r.table)
+    load(r.hbm_entity, r.w_entity)
+    load(r.hbm_out, r.w_out)
+    load(r.hbm_up, r.w_up)
+    load(r.hbm_down, r.w_down)
+
+    shard_row = r.shard[...]
+    shard_all = jnp.broadcast_to(shard_row.astype(full), (half_ents, half_ents)).T
+    shard_all = shard_all.astype(jnp.int32)
+    shard_col = shard_all[:, 0:1]
+    below = lax.broadcasted_iota(jnp.int32, (half_ents, half_ents), 0)
+    beside = lax.broadcasted_iota(jnp.int32, (half_ents, half_ents), 1)
+    same = shard_all == shard_row
+    rank_row = row_sum(jnp.where(same & (below < beside), 1.0, 0.0)).astype(jnp.int32)
+    rank_col = jnp.sum(jnp.where(same & (beside < below), 1.0, 0.0), 1, keepdims=True)
+    rank_col = rank_col.astype(jnp.int32)
+    slot_row = shard_row * capacity + rank_row
+    in_slot = lax.broadcasted_iota(jnp.int32, (slots, half_ents), 0) == slot_row
+    wanted = jnp.sum(
+        jnp.where(in_slot, (r.row[...] + 1).astype(full), 0.0), 1, keepdims=True
+    )
+    wanted = wanted.astype(jnp.int32) - 1
+    r.ask[...] = jnp.broadcast_to(wanted, (slots, 128)).reshape(owners, capacity, 128)
+    r.outbox[...] = jnp.where(in_slot, 1.0, 0.0).astype(low)
+    answer_col = shard_col * (2 * capacity) + x * capacity + rank_col
+    answer_lane = lax.broadcasted_iota(jnp.int32, (half_ents, 2 * slots), 1)
+    r.select[aligned(x, half_ents), :] = jnp.where(answer_lane == answer_col, 1.0, 0.0).astype(low)
+    r.asked[flat] = r.ask[flat]
+    r.x_all[aligned(x, half_words), :] = r.words[...]
+    r.x_own[0:half_words, :] = r.words[...].astype(full)
+    r.cotangent[0:half_words, :] = r.cot_words[...]
+    r.cotangent[half_words:rows, :] = r.cot_ents[...]
+    r.vec[0] = jnp.zeros(r.vec.shape[1:], full)
+
+    pl.semaphore_wait(barrier, owners)
+
+    def ask_copy(k):
+        other, peer = others[k]
+        return send(r.ask.at[other], r.asked.at[flat], r.ask_s.at[k], r.ask_r.at[k], peer)
+
+    def answer_copy(k):
+        other, peer = others[k]
+        return send(
+            r.found.at[other // 2], r.answer.at[flat], r.answer_s.at[k], r.answer_r.at[k], peer
+        )
+
+    def slope_copy(k):
+        other, peer = others[k]
+        return send(r.slope.at[other], r.slopes.at[flat], r.slope_s.at[k], r.slope_r.at[k], peer)
+
+    for k in range(owners - 1):
+        ask_copy(k).start()
+    my_select = r.select.at[aligned(x, half_ents), :]
+    select_copy = send(my_select, my_select, r.pair_s.at[0], r.pair_r.at[0], x_peer)
+    select_copy.start()
+    my_words = r.x_all.at[aligned(x, half_words), :]
+    words_copy = send(r.words, my_words, r.pair_s.at[1], r.pair_r.at[1], x_peer)
+    words_copy.start()
+
+    loaded(r.w_query)
+    loaded(r.w_keyval)
+
+    def gather_columns(which):
+        for h in range(heads):
+            own = slice(which * side + h * HD, which * side + (h + 1) * HD)
+            for place, words_part, ents_part in (
+                (0, r.w_query[0, :, own], r.w_query[2, :, own]),
+                (1, r.w_query[1, :, own], r.w_query[3, :, own]),
+                (2, r.w_keyval[0, :, own], None),
+                (3, r.w_keyval[1, :, own], None),
+            ):
+                lanes = slice((4 * h + place) * HD, (4 * h + place + 1) * HD)
+                r.cat_words[:, lanes] = words_part
+                r.cat_ents[:, lanes] = words_part if ents_part is None else ents_part
+            zero = jnp.zeros((1, HD), full)
+            value = r.b_value[...].reshape(1, -1)[:, own]
+            query = r.b_query[:, own]
+            lanes = slice(4 * h * HD, 4 * (h + 1) * HD)
+            r.bias_words[:, lanes] = jnp.concatenate([query[0:1], query[1:2], zero, value], 1)
+            r.bias_ents[:, lanes] = jnp.concatenate([query[2:3], query[3:4], zero, value], 1)
+
+    for which in range(2):
+
+        @pl.when(x == which)
+        def _(which=which):
+            gather_columns(which)
+
+    def project(start, count, weight, bias):
+        def body(h, carry):
+            lanes = aligned(h, 4 * HD)
+            total = dot_nn(r.x_all[pl.ds(start, count), :], weight[:, lanes]) + bias[:, lanes]
+            r.qkv[pl.ds(start, count), lanes] = total.astype(low)
+            return carry
+
+        lax.fori_loop(0, heads, body, 0)
+
+    project(pl.multiple_of(x * half_words, half_words), half_words, r.cat_words, r.bias_words)
+
+    segments = jnp.concatenate([r.word_seg[...], r.ent_seg[...]], 1)
+    for i in range(everyone // 128):
+        own_seg = jnp.broadcast_to(segments[:, i * 128 : (i + 1) * 128].astype(full), (128, 128)).T
+        equal = own_seg[:, 0:1].astype(jnp.int32) == segments
+        r.mask[i * 128 : (i + 1) * 128, :] = jnp.where(equal, 0.0, masked_score).astype(low)
+
+    for k in range(owners - 1):
+        ask_copy(k).wait()
+    ids = r.asked[...].reshape(slots, 128)
+    lane = lax.broadcasted_iota(jnp.int32, (slots, 128), 1)
+
+    def pick_body(j, carry):
+        r.pick[:, aligned(j, 128)] = jnp.where(ids == lane + 128 * j, 1.0, 0.0).astype(low)
+        return carry
+
+    lax.fori_loop(0, r.table.shape[0] // 128, pick_body, 0)
+    loaded(r.table)
+    found = dot_nn(r.pick[...], r.table[...]).astype(low)
+    r.found[...] = found.reshape(r.found.shape)
+    r.answer[flat] = r.found[dp]
+    for k in range(owners - 1):
+        answer_copy(k).start()
+
+    words_copy.wait()
+    project(pl.multiple_of((1 - x) * half_words, half_words), half_words, r.cat_words, r.bias_words)
+    r.words_t[...] = r.x_all[0:words, :].T
+
+    select_copy.wait()
+    for k in range(owners - 1):
+        answer_copy(k).wait()
+    looked = dot_nn(r.select[...], r.answer[...].reshape(2 * slots, r.table.shape[1])).astype(low)
+    r.looked[...] = looked
+    loaded(r.w_entity)
+    ent_lin = dot_nn(looked, r.w_entity[...])
+    normed, _ = normalize(ent_lin)
+    x_entity = normed * r.gain[0:1, :] + r.shift[0:1, :]
+    r.ent_lin[...] = ent_lin
+    r.x_ent[...] = x_entity
+    r.x_all[words:everyone, :] = x_entity.astype(low)
+    r.x_own[half_words:rows, :] = r.x_ent[aligned(x, half_ents), :]
+    project(words, 2 * half_ents, r.cat_ents, r.bias_ents)
+    r.ents_t[...] = r.x_all[words:everyone, :].T
+    for h in range(heads):
+        r.key[h] = r.qkv[:, h * 4 * HD + 2 * HD : h * 4 * HD + 3 * HD]
+        r.value[h] = r.qkv[:, h * 4 * HD + 3 * HD : h * 4 * HD + 4 * HD]
+
+    def row_start(i, which):
+        start = jnp.where(
+            i < word_blocks, which * half_words + i * block, words + which * half_ents
+        )
+        return pl.ds(pl.multiple_of(start, block), block)
+
+    def attend(which, target):
+        def body(i, carry):
+            here = row_start(i, which)
+            outs = []
+            for h in range(heads):
+                query = r.qkv[here, h * 4 * HD : h * 4 * HD + 2 * HD]
+                score = jnp.concatenate(
+                    [
+                        dot_nt(query[:, :HD], r.key[h, 0:words, :]),
+                        dot_nt(query[:, HD:], r.key[h, words:everyone, :]),
+                    ],
+                    1,
+                )
+                score = score * score_scale + r.mask[here, :].astype(full)
+                power = jnp.exp(score - jnp.max(score, 1, keepdims=True))
+                prob = power / jnp.sum(power, 1, keepdims=True)
+                r.prob[h, here, :] = prob
+                outs.append(dot_nn(prob.astype(low), r.value[h]))
+            target[aligned(i, block), :] = jnp.concatenate(outs, 1).astype(low)
+            return carry
+
+        lax.fori_loop(0, blocks, body, 0)
+
+    attend(1 - x, r.heads_far)
+    heads_copy = send(r.heads_far, r.heads_in, r.pair_s.at[2], r.pair_r.at[2], x_peer)
+    heads_copy.start()
+    attend(x, r.heads_near)
+    heads_copy.wait()
+
+    @pl.when(x == 0)
+    def _():
+        r.heads_all[:, 0:side] = r.heads_near[...]
+        r.heads_all[:, side:] = r.heads_in[...]
+
+    @pl.when(x == 1)
+    def _():
+        r.heads_all[:, 0:side] = r.heads_in[...]
+        r.heads_all[:, side:] = r.heads_near[...]
+
+    def swap(which, turn, first, count):
+        part = pl.ds(first, count)
+        return send(
+            r.mail_out.at[which, part], r.mail_in.at[which, part], r.swap_s.at[turn],
+            r.swap_r.at[turn], core,
+        )
+
+    def columns(count, fill):
+        def body(j, carry):
+            fill(aligned(j, wide), j)
+            return carry
+
+        lax.fori_loop(0, count // wide, body, 0)
+
+    def fill_attn(lanes, _):
+        r.mail_out[0, 0:rows, lanes] = dot_nn(r.heads_all[...], r.w_out[:, lanes])
+
+    loaded(r.w_out)
+    columns(width, fill_attn)
+    attn_swap = swap(0, 0, 0, rows)
+    attn_swap.start()
+    attn_swap.wait()
+
+    def over_rows(body):
+        def step(i, carry):
+            body(aligned(i, block))
+            return carry
+
+        lax.fori_loop(0, blocks, step, 0)
+
+    def first_norm(here):
+        attn = r.mail_out[0, here, :] + r.mail_in[0, here, :] + r.b_out[...].reshape(1, -1)
+        normed, scale = normalize(r.x_own[here, :] + attn)
+        r.normed[here, :] = normed
+        r.scale[here, :] = jnp.broadcast_to(scale, (block, 128))
+        r.first[here, :] = (normed * r.gain[1:2, :] + r.shift[1:2, :]).astype(low)
+
+    over_rows(first_norm)
+
+    def fill_up(lanes, _):
+        up = dot_nn(r.first[...], r.w_up[:, lanes]) + r.b_up[lanes].reshape(1, -1)
+        chance = 0.5 + 0.5 * lax.erf(up * (0.5**0.5))
+        r.act[:, lanes] = (up * chance).astype(low)
+        r.slope_up[:, lanes] = chance + up * (jnp.exp(-0.5 * up * up) * (0.5 / math.pi) ** 0.5)
+
+    loaded(r.w_up)
+    columns(hidden, fill_up)
+
+    def fill_down(lanes, _):
+        r.mail_out[1, 0:rows, lanes] = dot_nn(r.act[...], r.w_down[:, lanes])
+
+    loaded(r.w_down)
+    columns(width, fill_down)
+    ffn_swap = swap(1, 1, 0, rows)
+    ffn_swap.start()
+    r.first_t[...] = r.first[...].T
+    ffn_swap.wait()
+
+    vec = r.vec.at[0]
+
+    def second_norm(here):
+        ffn = r.mail_out[1, here, :] + r.mail_in[1, here, :] + r.b_down[...].reshape(1, -1)
+        entering = r.normed[here, :] * r.gain[1:2, :] + r.shift[1:2, :]
+        normed, scale = normalize(entering + ffn)
+        r.final[here, :] = (normed * r.gain[2:3, :] + r.shift[2:3, :]).astype(low)
+        grad = r.cotangent[here, :].astype(full)
+        vec[2:3, :] += row_sum(grad * normed)
+        vec[5:6, :] += row_sum(grad)
+        back = normalize_back(grad, normed, scale, r.gain[2:3, :])
+        r.grad_second[here, :] = back
+        r.grad_low[here, :] = back.astype(low)
+        vec[7:8, :] += row_sum(back.astype(low).astype(full))
+
+    over_rows(second_norm)
+
+    def halves(source, c, axis_flip):
+        if axis_flip:
+            return source.at[c, :, 1 - y], source.at[c, :, y]
+        return source.at[c, :, :, 1 - x], source.at[c, :, :, x]
+
+    def stage_one(kit, c, flip):
+        away, _ = halves(kit.grads, c, flip)
+        return send(away, kit.near.at[c], kit.s1.at[c], kit.r1.at[c], y_peer if flip else x_peer)
+
+    def stage_two(kit, c, flip):
+        away = kit.near.at[c, :, 1 - x] if flip else kit.near.at[c, :, 1 - y]
+        return send(away, kit.next.at[c], kit.s2.at[c], kit.r2.at[c], x_peer if flip else y_peer)
+
+    def stage_three(kit, c, k):
+        return send(
+            kit.next.at[c, lax.rem(z + k, deep)],
+            kit.far.at[c, k - 1],
+            kit.s3.at[c, k - 1],
+            kit.r3.at[c, k - 1],
+            z_peers[k - 1],
+        )
+
+    def to_two(kit, c, flip):
+        stage_one(kit, c, flip).wait()
+        _, own = halves(kit.grads, c, flip)
+
+        def body(i, carry):
+            total = own[i].astype(full) + kit.near[c, i].astype(full)
+            kit.near[c, i] = total.astype(low)
+            return carry
+
+        lax.fori_loop(0, deep, body, 0)
+        stage_two(kit, c, flip).start()
+
+    def to_three(kit, c, flip):
+        stage_two(kit, c, flip).wait()
+        own = kit.near.at[c, :, x] if flip else kit.near.at[c, :, y]
+
+        def body(i, carry):
+            total = own[i].astype(full) + kit.next[c, i].astype(full)
+            kit.next[c, i] = total.astype(low)
+            return carry
+
+        lax.fori_loop(0, deep, body, 0)
+        for k in range(1, deep):
+            stage_three(kit, c, k).start()
+
+    def finish(kit, c):
+        for k in range(1, deep):
+            stage_three(kit, c, k).wait()
+        total = kit.next[c, z].astype(full)
+        for k in range(1, deep):
+            total = total + kit.far[c, k - 1].astype(full)
+        kit.out[c] = total
+
+    kit_a = types.SimpleNamespace(
+        grads=r.grads, near=r.near, next=r.next, far=r.far, out=r.out_a,
+        s1=r.a_s1, r1=r.a_r1, s2=r.a_s2, r2=r.a_r2, s3=r.a_s3, r3=r.a_r3,
+    )
+    kit_e = types.SimpleNamespace(
+        grads=r.e_grads, near=r.e_near, next=r.e_next, far=r.e_far, out=r.e_sum,
+        s1=r.e_s1, r1=r.e_r1, s2=r.e_s2, r2=r.e_r2, s3=r.e_s3, r3=r.e_r3,
+    )
+
+    def head_one(h):
+        return send(r.q_grads.at[h, :, 1 - y], r.q_near.at[h], r.q_s1.at[h], r.q_r1.at[h], y_peer)
+
+    def head_two(h, k):
+        return send(
+            r.q_near.at[h, lax.rem(z + k, deep)],
+            r.q_far.at[h, k - 1],
+            r.q_s2.at[h, k - 1],
+            r.q_r2.at[h, k - 1],
+            z_peers[k - 1],
+        )
+
+    def head_three(h):
+        return send(r.q_sum.at[h, 1 - x], r.q_in.at[h], r.q_s3.at[h], r.q_r3.at[h], x_peer)
+
+    def head_to_two(h):
+        head_one(h).wait()
+
+        def body(i, carry):
+            total = r.q_grads[h, i, y].astype(full) + r.q_near[h, i].astype(full)
+            r.q_near[h, i] = total.astype(low)
+            return carry
+
+        lax.fori_loop(0, deep, body, 0)
+        for k in range(1, deep):
+            head_two(h, k).start()
+
+    def head_to_three(h):
+        for k in range(1, deep):
+            head_two(h, k).wait()
+        total = r.q_near[h, z].astype(full)
+        for k in range(1, deep):
+            total = total + r.q_far[h, k - 1].astype(full)
+        r.q_sum[h] = total
+        head_three(h).start()
+        r.out_q[h, x] = r.q_sum[h, x]
+
+    def head_finish(h):
+        head_three(h).wait()
+        r.out_q[h, 1 - x] = r.q_in[h]
+
+    band = 4 * share
+    chunk = r.grads.shape[5]
+
+    def make_grad(c, left_t, right, lanes):
+        def body(i, carry):
+            part = dot_nn(left_t[aligned(i, band), :], right[:, lanes])
+            r.grads[c, i] = part.astype(low).reshape(2, 2, share, chunk)
+            return carry
+
+        lax.fori_loop(0, deep, body, 0)
+        stage_one(kit_a, c, flips[c]).start()
+
+    downs = hidden // chunk
+    r.grad_t[...] = r.grad_low[...].T
+    for c in range(downs):
+        make_grad(c, r.grad_t, r.act, slice(c * chunk, (c + 1) * chunk))
+
+    def fill_dup(lanes, j):
+        grad_act = dot_nt(r.grad_low[...], r.w_down[lanes, :])
+        grad_up = (grad_act * r.slope_up[:, lanes]).astype(low)
+        r.grad_up[:, lanes] = grad_up
+        vec[pl.ds(8 + j // (width // wide), 1), aligned(lax.rem(j, width // wide), wide)] = row_sum(
+            grad_up.astype(full)
+        )
+
+    columns(hidden, fill_dup)
+
+    def fill_back(lanes, _):
+        r.mail_out[0, 0:rows, lanes] = dot_nt(r.grad_up[...], r.w_up[lanes, :])
+
+    columns(width, fill_back)
+    back_swap = swap(0, 2, 0, rows)
+    back_swap.start()
+    r.out_words[...] = r.final[pl.ds(pl.multiple_of(t * (half_words // 2), half_words // 2), half_words // 2), :]
+    r.out_ents[...] = r.final[
+        pl.ds(pl.multiple_of(half_words + t * (half_ents // 2), half_ents // 2), half_ents // 2), :
+    ]
+    for c in range(downs):
+        make_grad(downs + c, r.first_t, r.grad_up, slice(c * chunk, (c + 1) * chunk))
+    back_swap.wait()
+
+    def first_back(here):
+        grad = r.grad_second[here, :] + r.mail_out[0, here, :] + r.mail_in[0, here, :]
+        normed = r.normed[here, :]
+        vec[1:2, :] += row_sum(grad * normed)
+        vec[4:5, :] += row_sum(grad)
+        back = normalize_back(grad, normed, r.scale[here, 0:1], r.gain[1:2, :])
+        r.grad_first[here, :] = back
+        r.grad_low[here, :] = back.astype(low)
+        vec[6:7, :] += row_sum(back.astype(low).astype(full))
+
+    over_rows(first_back)
+    near_rows = aligned(x, side)
+    far_rows = aligned(1 - x, side)
+    r.back_far[...] = dot_nt(r.grad_low[...], r.w_out[far_rows, :]).astype(low)
+    mine = [(aligned(x, half_words), 0, half_words)]
+    mine.append((pl.ds(pl.multiple_of(words + x * half_ents, half_ents), half_ents), half_words, half_ents))
+    back_copies = [
+        send(
+            r.back_far.at[pl.ds(first, count), :], r.back_heads.at[place, :],
+            r.pair_s.at[3 + n], r.pair_r.at[3 + n], x_peer,
+        )
+        for n, (place, first, count) in enumerate(mine)
+    ]
+    for copy in back_copies:
+        copy.start()
+    near = dot_nt(r.grad_low[...], r.w_out[near_rows, :]).astype(low)
+    for place, first, count in mine:
+        r.back_heads[place, :] = near[first : first + count, :]
+    r.grad_t[...] = r.grad_low[...].T
+    outs = 2 * downs
+    make_grad(outs, r.grad_t, r.heads_all, slice(0, chunk))
+
+    def ticks(events):
+        for kind, c in events:
+            if kind == "f":
+                to_two(kit_a, c, flips[c])
+            if kind == "s":
+                to_three(kit_a, c, flips[c])
+            if kind == "q":
+                head_to_two(c)
+            if kind == "r":
+                head_to_three(c)
+
+    ticks(schedule[0])
+    for copy in back_copies:
+        copy.wait()
+
+    pair = 2 * HD
+    for h in range(heads):
+        base = h * 4 * HD
+
+        def score_back(i, carry):
+            here = aligned(i, block)
+            prob = r.prob[h, here, :]
+            grad_prob = dot_nt(r.back_heads[here, h * HD : (h + 1) * HD], r.value[h])
+            inner = jnp.sum(prob * grad_prob, 1, keepdims=True)
+            grad_score = (prob * (grad_prob - inner)).astype(low)
+            r.grad_score[here, :] = grad_score
+            r.prob_low[here, :] = prob.astype(low)
+            queries = jnp.concatenate(
+                [
+                    dot_nn(grad_score[:, :words], r.key[h, 0:words, :]),
+                    dot_nn(grad_score[:, words:], r.key[h, words:everyone, :]),
+                ],
+                1,
+            )
+            r.grad_qkv[here, base : base + pair] = (queries * score_scale).astype(low)
+            return carry
+
+        lax.fori_loop(0, everyone // block, score_back, 0)
+        ticks(schedule[1 + 2 * h])
+        query_t = r.qkv[:, base : base + pair].T
+        keys_t = dot_nn(query_t, r.grad_score[...])
+        keys_t = jnp.concatenate([keys_t[:HD, :words], keys_t[HD:, words:]], 1) * score_scale
+        values_t = dot_nn(r.back_heads[:, h * HD : (h + 1) * HD].T, r.prob_low[...])
+        r.grad_qkv[:, base + pair : base + 2 * pair] = (
+            jnp.concatenate([keys_t, values_t], 0).T.astype(low)
+        )
+
+        def head_grad(i, carry):
+            here = aligned(i, band)
+            of_words = dot_nn(r.words_t[here, :], r.grad_qkv[0:words, base : base + pair])
+            of_ents = dot_nn(r.ents_t[here, :], r.grad_qkv[words:everyone, base : base + pair])
+            keyval = r.grad_qkv[:, base + pair : base + 2 * pair]
+            of_keyval = dot_nn(r.words_t[here, :], keyval[:words]) + dot_nn(
+                r.ents_t[here, :], keyval[words:]
+            )
+            for n, part in enumerate([of_words, of_ents, of_keyval]):
+                r.q_grads[h, i, :, :, :, n * pair : (n + 1) * pair] = part.astype(low).reshape(
+                    2, 2, share, pair
+                )
+            return carry
+
+        lax.fori_loop(0, deep, head_grad, 0)
+        head_one(h).start()
+        sums = jnp.concatenate(
+            [
+                row_sum(r.grad_qkv[0:words, base : base + pair].astype(full)),
+                row_sum(r.grad_qkv[words:everyone, base : base + pair].astype(full)),
+                row_sum(r.grad_qkv[:, base + pair : base + 2 * pair].astype(full)),
+            ],
+            1,
+        )
+        place = h * 3 * pair
+        vec[pl.ds(10 + 2 * x + place // width, 1), place % width : place % width + 3 * pair] = sums
+        ticks(schedule[2 + 2 * h])
+
+    quarter = half_words // 2
+
+    def input_grad(place, weight):
+        return dot_nt(r.grad_qkv[place, :], weight[...])
+
+    ents_part = input_grad(slice(words, everyone), r.cat_ents)
+    r.mail_out[1, words // 2 :, :] = ents_part
+    ents_swap = swap(1, 3, words // 2, 2 * half_ents)
+    ents_swap.start()
+    for n in range(2):
+        r.mail_out[1, n * quarter : (n + 1) * quarter, :] = input_grad(
+            aligned(2 * n + 1 - t, quarter), r.cat_words
+        )
+    words_swap = swap(1, 4, 0, words // 2)
+    words_swap.start()
+    for n in range(2):
+        r.input_part[n] = input_grad(aligned(2 * n + t, quarter), r.cat_words)
+    ents_swap.wait()
+    ents_place = pl.multiple_of(words // 2 + (1 - x) * half_ents, half_ents)
+    ents_far = pl.ds(ents_place, half_ents)
+    ents_near = pl.ds(pl.multiple_of(words // 2 + x * half_ents, half_ents), half_ents)
+    r.ents_back[...] = (r.mail_out[1, ents_far, :] + r.mail_in[1, ents_far, :]).astype(low)
+    ents_copy = send(r.ents_back, r.ents_in, r.pair_s.at[5], r.pair_r.at[5], x_peer)
+    ents_copy.start()
+    words_swap.wait()
+    far_place = aligned(1 - x, quarter)
+    r.words_back[...] = (r.input_part[1 - x] + r.mail_in[1, far_place, :]).astype(low)
+    words_back_copy = send(r.words_back, r.words_in, r.pair_s.at[6], r.pair_r.at[6], x_peer)
+    words_back_copy.start()
+    ents_copy.wait()
+
+    grad = r.grad_first[half_words:rows, :] + (r.mail_out[1, ents_near, :] + r.mail_in[1, ents_near, :])
+    grad = grad + r.ents_in[...].astype(full)
+    own_ents = aligned(x, half_ents)
+    normed, scale = normalize(r.ent_lin[own_ents, :])
+    vec[0:1, :] = row_sum(grad * normed)
+    vec[3:4, :] = row_sum(grad)
+    lin_low = normalize_back(grad, normed, scale, r.gain[0:1, :]).astype(low)
+    slope = dot_nt(lin_low, r.w_entity[...]).astype(low)
+    r.slope[...] = dot_nn(r.outbox[...], slope).reshape(owners, capacity, -1)
+    r.slopes[flat] = r.slope[flat]
+    for k in range(owners - 1):
+        slope_copy(k).start()
+    looked_half = r.looked[own_ents, aligned(t, 128)]
+    r.ents_grad[...] = dot_tn(lin_low, looked_half).astype(low)
+
+    def ents_body(i, carry):
+        r.e_grads[0, i] = r.ents_grad[aligned(i, band), :].reshape(2, 2, share, 128)
+        return carry
+
+    lax.fori_loop(0, deep, ents_body, 0)
+    stage_one(kit_e, 0, False).start()
+    vec_copies = [send(r.vec.at[0], r.vec_in.at[0], r.vec_s.at[0], r.vec_r.at[0], x_peer)]
+    vec_copies[0].start()
+    words_back_copy.wait()
+    r.grad_words[...] = (
+        r.grad_first[aligned(t, quarter), :]
+        + (r.input_part[x] + r.mail_in[1, aligned(x, quarter), :])
+        + r.words_in[...].astype(full)
+    )
+    ticks(schedule[7])
+    to_two(kit_e, 0, False)
+    vec_copies[0].wait()
+    r.vec[1] = r.vec[0] + r.vec_in[0]
+    vec_copies.append(send(r.vec.at[1], r.vec_in.at[1], r.vec_s.at[1], r.vec_r.at[1], y_peer))
+    vec_copies[1].start()
+    ticks(schedule[8])
+    to_three(kit_e, 0, False)
+    vec_copies[1].wait()
+    r.vec[2] = r.vec[1] + r.vec_in[1]
+    for k in range(1, deep):
+        vec_copies.append(
+            send(r.vec.at[2], r.vec_in.at[1 + k], r.vec_s.at[1 + k], r.vec_r.at[1 + k], z_peers[k - 1])
+        )
+        vec_copies[-1].start()
+    for k in range(owners - 1):
+        slope_copy(k).wait()
+    ids_t = r.asked[...].reshape(slots, 128).astype(full).T
+    r.ids_out[...] = ids_t[0:8, :].astype(jnp.int32)
+    r.slopes_out[...] = r.slopes[...].reshape(slots, -1).astype(low)
+    for c in range(2 * downs + 1):
+        finish(kit_a, c)
+    ticks(schedule[9])
+    total = r.vec[2]
+    for k in range(1, deep):
+        vec_copies[1 + k].wait()
+        total = total + r.vec_in[1 + k]
+    r.vec_out[...] = total
+    r.across_out[...] = pltpu.roll(total[0:8, :], width - flat * share, 1)[:, 0:128]
+    finish(kit_e, 0)
+    ents_out = send(r.e_sum.at[0], r.e_in, r.pair_s.at[7], r.pair_r.at[7], core)
+    ents_out.start()
+    r.out_e[t] = r.e_sum[0]
+    for h in range(heads):
+        head_finish(h)
+    ents_out.wait()
+    r.out_e[1 - t] = r.e_in[...]
+
+
+def finish_kernel(names, *refs):
+    r = types.SimpleNamespace(**dict(zip(names, refs, strict=True)))
+    low, full = jnp.bfloat16, jnp.float32
+    step = pl.program_id(0)
+    count, embed = r.adam_first.shape
+    slots = r.ids.shape[1]
+    row = lax.broadcasted_iota(jnp.int32, (count, slots), 0) + step * count
+    chosen = jnp.where(row == r.ids[0:1, :], 1.0, 0.0)
+    touched = jnp.max(chosen, 1, keepdims=True) > 0.0
+    grad = dot_nn(chosen.astype(low), r.slopes[...])
+    first, second = r.adam_first[...], r.adam_second[...]
+    first_next = beta_one * first + (1.0 - beta_one) * grad
+    second_next = beta_two * second + (1.0 - beta_two) * grad * grad
+    direction = (
+        first_next
+        * (1.0 / (1.0 - beta_one**adam_steps))
+        / (jnp.sqrt(second_next * (1.0 / (1.0 - beta_two**adam_steps))) + adam_eps)
+    )
+    r.table_update[...] = jnp.where(touched, direction, 0.0)
+    r.new_first[...] = jnp.where(touched, first_next, first)
+    r.new_second[...] = jnp.where(touched, second_next, second)
+
+    chunks, share, chunk = r.out_a.shape
+    downs = chunks // 2
+    heads, side = r.out_q.shape[0], r.out_q.shape[0] * HD
+    last = pl.num_programs(0) - 1
+
+    @pl.when(step == 0)
+    def _():
+        for c in range(downs):
+            r.red_down[c * chunk : (c + 1) * chunk, :] = r.out_a[c].T
+            r.red_up[:, c * chunk : (c + 1) * chunk] = r.out_a[downs + c]
+        r.red_out[...] = r.out_a[2 * downs].T
+
+    @pl.when(step == last // 2)
+    def _():
+        for n in range(2):
+            r.red_entity[n * 128 : (n + 1) * 128, :] = r.out_e[n].T
+            for h in range(heads):
+                place = h * 6 * HD
+                line = 10 + 2 * n + place // r.vec.shape[1]
+                for j in range(6):
+                    lanes = slice(n * side + h * HD, n * side + (h + 1) * HD)
+                    part = r.out_q[h, n, :, j * HD : (j + 1) * HD]
+                    begin = place % r.vec.shape[1] + j * HD
+                    line_part = r.vec[line : line + 1, begin : begin + HD]
+                    if j < 4:
+                        r.red_query[j, :, lanes] = part
+                        r.red_query_bias[j : j + 1, lanes] = line_part
+                    else:
+                        r.red_keyval[j - 4, :, lanes] = part
+                    if j == 5:
+                        r.value_row[:, lanes] = line_part
+        r.red_gain[...] = r.across[0:3, 0:share]
+        r.red_shift[...] = r.across[3:6, 0:share]
+        r.red_value_bias[...] = r.value_row[...].reshape(-1)
+        r.red_out_bias[...] = r.across[6:7, 0:share].reshape(-1)
+        r.red_down_bias[...] = r.across[7:8, 0:share].reshape(-1)
+        width = r.vec.shape[1]
+        for n in range(2):
+            r.red_up_bias[n * width : (n + 1) * width] = r.vec[8 + n : 9 + n, :].reshape(-1)
+
+
+SCHEDULE = (
+    [("f", 0), ("f", 1)],
+    [("f", 2)],
+    [("s", 0), ("s", 1), ("f", 3)],
+    [("f", 4)],
+    [("s", 2), ("f", 5), ("s", 3)],
+    [("f", 6), ("s", 4)],
+    [("f", 7), ("s", 5), ("f", 8)],
+    [("s", 6), ("s", 7), ("s", 8), ("q", 0)],
+    [("q", 1), ("q", 2)],
+    [("r", 0), ("r", 1), ("r", 2)],
+)
+FLIPS = (False, True, False, False, True, False, False, True, False)
+
+
+def fused_local(
+    word_states,
+    entity_shard,
+    entity_row,
+    word_segments,
+    entity_segments,
+    entity_table,
+    adam_first,
+    adam_second,
+    w_entity,
+    norm_gain,
+    norm_bias,
+    w_query,
+    b_query,
+    w_keyval,
+    b_value,
+    w_out,
+    b_out,
+    w_up,
+    b_up,
+    w_down,
+    b_down,
+    cot_words,
+    cot_entities,
+):
+    low, full = jnp.bfloat16, jnp.float32
+    _, half_words, width = word_states.shape
+    half_ents = entity_row.shape[2]
+    rows, everyone = half_words + half_ents, 2 * (half_words + half_ents)
+    words, ents = 2 * half_words, 2 * half_ents
+    table_rows, embed = entity_table.shape
+    local_width, hidden = w_query.shape[2], w_up.shape[1]
+    owners = lax.axis_size(("dp", "stream"))
+    deep = lax.axis_size("dp") // 2
+    share = width // owners
+    capacity = 2 * half_ents // owners
+    side = local_width // 2
+    heads = side // HD
+    chunk = local_width
+    chunks = 2 * (hidden // chunk) + 1
+
+    operands = dict(
+        words=word_states.reshape(half_words, width),
+        shard=entity_shard.reshape(1, half_ents),
+        row=entity_row.reshape(1, half_ents),
+        word_seg=word_segments,
+        ent_seg=entity_segments,
+        gain=norm_gain,
+        shift=norm_bias,
+        b_query=b_query,
+        b_value=b_value,
+        b_out=b_out,
+        b_up=b_up,
+        b_down=b_down,
+        cot_words=cot_words.reshape(half_words, width),
+        cot_ents=cot_entities.reshape(half_ents, width),
+    )
+    streamed = dict(
+        hbm_query=w_query,
+        hbm_keyval=w_keyval,
+        hbm_table=entity_table,
+        hbm_entity=w_entity,
+        hbm_out=w_out,
+        hbm_up=w_up,
+        hbm_down=w_down,
+    )
+    results = dict(
+        out_words=((half_words // 2, width), low),
+        out_ents=((half_ents // 2, width), low),
+        grad_words=((half_words // 2, width), full),
+        out_a=((chunks, share, chunk), full),
+        out_e=((2, share, 128), full),
+        out_q=((heads, 2, share, chunk), full),
+        vec_out=((16, width), full),
+        across_out=((8, 128), full),
+        ids_out=((8, owners * capacity), jnp.int32),
+        slopes_out=((owners * capacity, embed), low),
+    )
+    mail_rows = max(rows, words // 2 + ents)
+    dma = pltpu.SemaphoreType.DMA
+    scratch = dict(
+        w_query=(w_query.shape, low),
+        w_keyval=(w_keyval.shape, low),
+        table=(entity_table.shape, low),
+        w_entity=(w_entity.shape, low),
+        w_out=(w_out.shape, low),
+        w_up=(w_up.shape, low),
+        w_down=(w_down.shape, low),
+        cat_words=((width, 4 * side), low),
+        cat_ents=((width, 4 * side), low),
+        bias_words=((1, 4 * side), full),
+        bias_ents=((1, 4 * side), full),
+        cotangent=((rows, width), low),
+        ask=((owners, capacity, 128), jnp.int32),
+        asked=((owners, capacity, 128), jnp.int32),
+        outbox=((owners * capacity, half_ents), low),
+        select=((ents, owners * 2 * capacity), low),
+        pick=((owners * capacity, table_rows), low),
+        found=((owners // 2, 2 * capacity, embed), low),
+        answer=((owners, 2 * capacity, embed), low),
+        looked=((ents, embed), low),
+        ent_lin=((ents, width), full),
+        x_ent=((ents, width), full),
+        x_all=((everyone, width), low),
+        x_own=((rows, width), full),
+        words_t=((width, words), low),
+        ents_t=((width, ents), low),
+        mask=((everyone, everyone), low),
+        qkv=((everyone, 4 * side), low),
+        key=((heads, everyone, HD), low),
+        value=((heads, everyone, HD), low),
+        prob=((heads, everyone, everyone), full),
+        heads_far=((rows, side), low),
+        heads_near=((rows, side), low),
+        heads_in=((rows, side), low),
+        heads_all=((rows, 2 * side), low),
+        mail_out=((2, mail_rows, width), full),
+        mail_in=((2, mail_rows, width), full),
+        normed=((rows, width), full),
+        scale=((rows, 128), full),
+        first=((rows, width), low),
+        first_t=((width, rows), low),
+        act=((rows, hidden), low),
+        slope_up=((rows, hidden), full),
+        final=((rows, width), low),
+        grad_second=((rows, width), full),
+        grad_low=((rows, width), low),
+        grad_t=((width, rows), low),
+        grad_up=((rows, hidden), low),
+        grad_first=((rows, width), full),
+        back_far=((rows, side), low),
+        back_heads=((everyone, side), low),
+        grad_score=((everyone, everyone), low),
+        prob_low=((everyone, everyone), low),
+        grad_qkv=((everyone, 4 * side), low),
+        input_part=((2, half_words // 2, width), full),
+        ents_back=((half_ents, width), low),
+        ents_in=((half_ents, width), low),
+        words_back=((half_words // 2, width), low),
+        words_in=((half_words // 2, width), low),
+        slope=((owners, capacity, embed), full),
+        slopes=((owners, capacity, embed), full),
+        ents_grad=((width, 128), low),
+        e_sum=((1, share, 128), full),
+        e_in=((share, 128), full),
+        vec=((3, 16, width), full),
+        vec_in=((deep + 1, 16, width), full),
+        grads=((chunks, deep, 2, 2, share, chunk), low),
+        near=((chunks, deep, 2, share, chunk), low),
+        next=((chunks, deep, share, chunk), low),
+        far=((chunks, deep - 1, share, chunk), low),
+        e_grads=((1, deep, 2, 2, share, 128), low),
+        e_near=((1, deep, 2, share, 128), low),
+        e_next=((1, deep, share, 128), low),
+        e_far=((1, deep - 1, share, 128), low),
+        q_grads=((heads, deep, 2, 2, share, chunk), low),
+        q_near=((heads, deep, 2, share, chunk), low),
+        q_far=((heads, deep - 1, 2, share, chunk), low),
+        q_sum=((heads, 2, share, chunk), full),
+        q_in=((heads, share, chunk), full),
+    )
+    signals = dict(
+        load_s=(7,),
+        ask_s=(owners - 1,),
+        ask_r=(owners - 1,),
+        answer_s=(owners - 1,),
+        answer_r=(owners - 1,),
+        slope_s=(owners - 1,),
+        slope_r=(owners - 1,),
+        pair_s=(8,),
+        pair_r=(8,),
+        swap_s=(5,),
+        swap_r=(5,),
+        vec_s=(deep + 1,),
+        vec_r=(deep + 1,),
+    )
+    one, many = (1,), (1, deep - 1)
+    signals.update(e_s1=one, e_r1=one, e_s2=one, e_r2=one, e_s3=many, e_r3=many)
+    one, many = (chunks,), (chunks, deep - 1)
+    signals.update(a_s1=one, a_r1=one, a_s2=one, a_r2=one, a_s3=many, a_r3=many)
+    one, many = (heads,), (heads, deep - 1)
+    signals.update(q_s1=one, q_r1=one, q_s2=many, q_r2=many, q_s3=one, q_r3=one)
+    names = [*operands, *streamed, *results, *scratch, *signals]
+    kernel = functools.partial(layer_kernel, names, FLIPS, SCHEDULE)
+    made = pl.pallas_call(
+        kernel,
+        name="layer",
+        out_shape=[jax.ShapeDtypeStruct(*item) for item in results.values()],
+        in_specs=[pl.BlockSpec(memory_space=pltpu.VMEM)] * len(operands)
+        + [pl.BlockSpec(memory_space=pl.ANY)] * len(streamed),
+        out_specs=[pl.BlockSpec(memory_space=pltpu.VMEM)] * len(results),
+        scratch_shapes=[pltpu.VMEM(*item) for item in scratch.values()]
+        + [dma(shape) for shape in signals.values()],
+        compiler_params=pltpu.CompilerParams(
+            collective_id=0, has_side_effects=True, vmem_limit_bytes=67_043_328
+        ),
+    )(*operands.values(), *streamed.values())
+    got = types.SimpleNamespace(**dict(zip(results, made, strict=True)))
+
+    step = table_rows // 8
+    table = pl.BlockSpec((step, embed), lambda i: (i, 0))
+
+    def whole(shape):
+        return pl.BlockSpec(shape, lambda i: (0,) * len(shape))
+
+    given = dict(
+        adam_first=adam_first,
+        adam_second=adam_second,
+        ids=got.ids_out,
+        slopes=got.slopes_out,
+        out_a=got.out_a,
+        out_e=got.out_e,
+        out_q=got.out_q,
+        vec=got.vec_out,
+        across=got.across_out,
+    )
+    final = dict(
+        red_entity=(embed, share),
+        red_gain=(3, share),
+        red_shift=(3, share),
+        red_query=(4, share, local_width),
+        red_query_bias=(4, local_width),
+        red_keyval=(2, share, local_width),
+        red_value_bias=(local_width,),
+        red_out=(local_width, share),
+        red_out_bias=(share,),
+        red_up=(share, hidden),
+        red_up_bias=(hidden,),
+        red_down=(hidden, share),
+        red_down_bias=(share,),
+        table_update=adam_first.shape,
+        new_first=adam_first.shape,
+        new_second=adam_first.shape,
+    )
+    finished = pl.pallas_call(
+        functools.partial(finish_kernel, [*given, *final, *dict(value_row=0)]),
+        name="finish",
+        grid=(8,),
+        out_shape=[jax.ShapeDtypeStruct(shape, full) for shape in final.values()],
+        in_specs=[table, table] + [whole(item.shape) for item in list(given.values())[2:]],
+        out_specs=[whole(shape) for shape in list(final.values())[:-3]] + [table] * 3,
+        scratch_shapes=[pltpu.VMEM((1, local_width), full)],
+        compiler_params=pltpu.CompilerParams(vmem_limit_bytes=40 * 2**20),
+    )(*given.values())
+    return (got.out_words[None], got.out_ents[None], got.grad_words[None], *finished)
+
+
+def plain_local(
     word_states,
     entity_shard,
     entity_row,
@@ -453,6 +1496,14 @@
         P("dp", "stream", None),
         P("dp", "stream", None),
     )
+    fits = mesh.shape["stream"] == 2 and mesh.shape["tensor"] == 2 and mesh.shape["dp"] % 2 == 0
+
+    def local(*blocks):
+        width, owners = blocks[0].shape[2], mesh.shape["dp"] * mesh.shape["stream"]
+        if fits and width % (16 * owners) == 0 and blocks[0].shape[0] == 1:
+            return fused_local(*blocks)
+        return plain_local(*blocks)
+
     return jax.shard_map(
         local,
         mesh=mesh,

time: 1270 us -> 189 us (0.15)
  waiting for transfers between devices: 952 us -> 0 us
  Pallas kernels: 0 us -> 173 us
  blocking collectives: 77.1 us -> 0 us
  matrix products: 65.8 us -> 0 us
  other arithmetic: 58.1 us -> 0 us
  local copies, waits for them, and re-layouts: 61.7 us -> 14.7 us
  starting transfers between devices: 26.6 us -> 0 us
  between operations: 16.5 us -> 0.7 us
    reduce_scatter x4 -> x0, waiting for transfers between devices: 535 us -> none  [the longest x1 142 us: local(): lax.psum_scatter(grad_down, ('dp', 'stream'), scatter_dimension=1, tiled=...]
    unnamed x14 -> x0, waiting for transfers between devices: 341 us -> none
    pallas_call x0 -> x2, Pallas kernels: none -> 173 us  [the longest x1 165 us: fused_local(): pl.pallas_call(kernel, name='layer', out_shape=[jax.ShapeDtypeStruct(*ite...]
    psum x1 -> x0, blocking collectives: 77.1 us -> none  [local(): lax.psum((grad_query_bias, grad_value_bias, grad_up_bias), ('dp', 'stream'))]
    dot_general x36 -> x0, matrix products: 65.8 us -> none  [the longest x4 11.1 us: matmul(): return jnp.dot(matrix_a, matrix_b, preferred_element_type=jnp.float32)]
    psum x4 -> x0, waiting for transfers between devices: 61.1 us -> none  [tensor_total(): return lax.psum(values_in, 'tensor')]
    all_to_all x3 -> x0, starting transfers between devices: 20.7 us -> none  [the longest x1 8.31 us: local(): lax.all_to_all(request, ('dp', 'stream'), split_axis=0, concat_axis=0, ti...]
    select_n x5 -> x0, other arithmetic: 15 us -> none  [the longest x1 12.1 us: local(): new_second = jnp.where(touched, second_next, adam_second)]
  transfers between devices with their start and end apart: 18 -> 0, of which waited for: 15 -> 0; matrix products, arithmetic and copies ran while one was open for 9% -> 0% of each run, Pallas kernels for 0% -> 0%
where the time goes in v2:
time: 189 us
  Pallas kernels  173 us (92%)
  local copies, waits for them, and re-layouts  14.7 us (8%)
    pallas_call x1, Pallas kernels, fused_local(): pl.pallas_call(kernel, name='layer', out_shape=[jax.ShapeDtypeStruct(*ite...  165 us
    unnamed x30, local copies, waits for them, and re-layouts  14.7 us
    pallas_call x1, Pallas kernels, fused_local(): pl.pallas_call(functools.partial(finish_kernel, [*given, *final, *dict(va...  8.17 us

profile of v2, /device:TPU:0, one launch (start us, length us, event | category | flops | bytes accessed | tf_op | source)
XLA Modules:
  0.0 188.9 jit_solution(16922464762301430726)
XLA Ops:
  0.7 165.3 %layer.1 = (bf16[128,768]{1,0:T(8,128)(2,1)}, bf16[32,768]{1,0:T(8,128)(2,1)}, f32[128,768]{1,0:T(8,128)}, f32[9,48,384]{2,1,0:T(8,128)}, f32[2,48,128]{2,1,0:T(...) custom-call(bf16[256,768]{1,0:T(8,128)(2,1)} %bitcast.8, ...), custom_call_target="tpu_custom_call" | custom-call | tf_op jit(solution)/shard_map/layer/pallas_call | solution.py:1026
  166.0 0.0 copy-start
  166.0 2.2 %copy-done = f32[4096,256]{1,0:T(8,128)S(1)} copy-done((f32[4096,256]{1,0:T(8,128)S(1)}, f32[4096,256]{1,0:T(8,128)}, u32[]{:S(2)}) %copy-start) | copy-done | bytes 4194328
  168.2 0.0 copy-start.1
  168.2 2.2 %copy-done.1 = f32[4096,256]{1,0:T(8,128)S(1)} copy-done((f32[4096,256]{1,0:T(8,128)S(1)}, f32[4096,256]{1,0:T(8,128)}, u32[]{:S(2)}) %copy-start.1) | copy-done | bytes 4194328
  170.4 0.0 copy-start.2
  170.4 1.1 copy-done.2
  171.4 0.0 copy-start.3
  171.4 1.0 copy-done.3
  172.5 0.0 copy-start.4
  172.5 0.8 copy-done.4
  173.3 0.0 copy-start.5
  173.3 0.8 copy-done.5
  174.1 0.0 copy-start.6
  174.1 0.8 copy-done.6
  174.9 0.0 copy-start.7
  174.9 0.7 copy-done.7
  175.6 0.0 copy-start.8
  175.6 0.7 copy-done.8
  176.3 0.0 copy-start.10
  176.3 0.0 copy-start.11
  176.3 0.0 copy-start.9
  176.3 8.2 %finish.1 = (f32[256,48]{1,0:T(8,128)S(1)}, f32[3,48]{1,0:T(4,128)}, f32[3,48]{1,0:T(4,128)}, f32[4,48,384]{2,1,0:T(8,128)}, f32[4,384]{1,0:T(4,128)}, /*index=5...) custom-call(f32[4096,256]{1,0:T(8,128)S(1)} %copy-done, ...), custom_call_target="tpu_custom_call" | custom-call | tf_op jit(solution)/shard_map/finish/pallas_call | solution.py:1076
  184.4 0.7 copy.42
  185.1 0.7 copy.43
  185.9 1.0 copy.44
  186.8 0.0 copy-done.10
  186.8 0.7 copy.48
  187.5 0.0 copy-done.11
  187.5 0.6 copy.49
  188.1 0.0 copy-done.9
  188.1 0.7 copy.50
Async XLA Ops:
  166.0 2.2 %copy-start = (f32[4096,256]{1,0:T(8,128)S(1)}, f32[4096,256]{1,0:T(8,128)}, u32[]{:S(2)}) copy-start(f32[4096,256]{1,0:T(8,128)} %refs_0_.1) | copy-start | bytes 12582916
  168.2 2.2 %copy-start.1 = (f32[4096,256]{1,0:T(8,128)S(1)}, f32[4096,256]{1,0:T(8,128)}, u32[]{:S(2)}) copy-start(f32[4096,256]{1,0:T(8,128)} %refs_1_.1) | copy-start | bytes 12582916
  170.4 1.1 copy-start.2
  171.4 1.0 copy-start.3
  172.5 0.8 copy-start.4
  173.3 0.8 copy-start.5
  174.1 0.8 copy-start.6
  174.9 0.7 copy-start.7
  175.6 0.7 copy-start.8
  176.3 10.6 %copy-start.10 = (bf16[128,768]{1,0:T(8,128)(2,1)S(1)}, bf16[128,768]{1,0:T(8,128)(2,1)}, u32[]{:S(2)}) copy-start(bf16[128,768]{1,0:T(8,128)(2,1)} %get-tuple-element.45) | copy-start | bytes 589828
  176.3 11.3 %copy-start.11 = (bf16[32,768]{1,0:T(8,128)(2,1)S(1)}, bf16[32,768]{1,0:T(8,128)(2,1)}, u32[]{:S(2)}) copy-start(bf16[32,768]{1,0:T(8,128)(2,1)} %get-tuple-element.46) | copy-start | bytes 147460
  176.3 11.9 %copy-start.9 = (f32[128,768]{1,0:T(8,128)S(1)}, f32[128,768]{1,0:T(8,128)}, u32[]{:S(2)}) copy-start(f32[128,768]{1,0:T(8,128)} %get-tuple-element.47) | copy-start | bytes 1179652

commit v3 on v2

--- a/solution.py
+++ b/solution.py
@@ -107,7 +107,7 @@
     y, z = lax.rem(dp, 2), dp // 2
     deep = lax.axis_size("dp") // 2
     owners = 4 * deep
-    half_words, width = r.words.shape
+    _, half_words, width = r.hbm_words.shape
     half_ents = r.shard.shape[1]
     rows, words = half_words + half_ents, 2 * half_words
     everyone = 2 * rows
@@ -143,10 +143,15 @@
     def loaded(target):
         loads.pop(id(target)).wait()
 
+    my_words = r.x_all.at[aligned(x, half_words), :]
+    load(r.hbm_words.at[0], my_words)
     load(r.hbm_query, r.w_query)
     load(r.hbm_keyval, r.w_keyval)
     load(r.hbm_table, r.table)
     load(r.hbm_entity, r.w_entity)
+    cot_words, cot_ents = r.cotangent.at[0:half_words, :], r.cotangent.at[half_words:rows, :]
+    load(r.hbm_cot_words.at[0], cot_words)
+    load(r.hbm_cot_ents.at[0], cot_ents)
     load(r.hbm_out, r.w_out)
     load(r.hbm_up, r.w_up)
     load(r.hbm_down, r.w_down)
@@ -173,36 +178,7 @@
     answer_lane = lax.broadcasted_iota(jnp.int32, (half_ents, 2 * slots), 1)
     r.select[aligned(x, half_ents), :] = jnp.where(answer_lane == answer_col, 1.0, 0.0).astype(low)
     r.asked[flat] = r.ask[flat]
-    r.x_all[aligned(x, half_words), :] = r.words[...]
-    r.x_own[0:half_words, :] = r.words[...].astype(full)
-    r.cotangent[0:half_words, :] = r.cot_words[...]
-    r.cotangent[half_words:rows, :] = r.cot_ents[...]
     r.vec[0] = jnp.zeros(r.vec.shape[1:], full)
-
-    pl.semaphore_wait(barrier, owners)
-
-    def ask_copy(k):
-        other, peer = others[k]
-        return send(r.ask.at[other], r.asked.at[flat], r.ask_s.at[k], r.ask_r.at[k], peer)
-
-    def answer_copy(k):
-        other, peer = others[k]
-        return send(
-            r.found.at[other // 2], r.answer.at[flat], r.answer_s.at[k], r.answer_r.at[k], peer
-        )
-
-    def slope_copy(k):
-        other, peer = others[k]
-        return send(r.slope.at[other], r.slopes.at[flat], r.slope_s.at[k], r.slope_r.at[k], peer)
-
-    for k in range(owners - 1):
-        ask_copy(k).start()
-    my_select = r.select.at[aligned(x, half_ents), :]
-    select_copy = send(my_select, my_select, r.pair_s.at[0], r.pair_r.at[0], x_peer)
-    select_copy.start()
-    my_words = r.x_all.at[aligned(x, half_words), :]
-    words_copy = send(r.words, my_words, r.pair_s.at[1], r.pair_r.at[1], x_peer)
-    words_copy.start()
 
     loaded(r.w_query)
     loaded(r.w_keyval)
@@ -232,11 +208,40 @@
         def _(which=which):
             gather_columns(which)
 
+    loaded(my_words)
+    r.x_own[0:half_words, :] = my_words[...].astype(full)
+    pl.semaphore_wait(barrier, owners)
+
+    def ask_copy(k):
+        other, peer = others[k]
+        return send(r.ask.at[other], r.asked.at[flat], r.ask_s.at[k], r.ask_r.at[k], peer)
+
+    def answer_copy(k):
+        other, peer = others[k]
+        return send(
+            r.found.at[other // 2], r.answer.at[flat], r.answer_s.at[k], r.answer_r.at[k], peer
+        )
+
+    def slope_copy(k):
+        other, peer = others[k]
+        return send(r.slope.at[other], r.slopes.at[flat], r.slope_s.at[k], r.slope_r.at[k], peer)
+
+    for k in range(owners - 1):
+        ask_copy(k).start()
+    my_select = r.select.at[aligned(x, half_ents), :]
+    select_copy = send(my_select, my_select, r.pair_s.at[0], r.pair_r.at[0], x_peer)
+    select_copy.start()
+    words_copy = send(my_words, my_words, r.pair_s.at[1], r.pair_r.at[1], x_peer)
+    words_copy.start()
+
+    is_query = lax.broadcasted_iota(jnp.int32, (1, 4 * HD), 1) < 2 * HD
+    scaling = jnp.where(is_query, score_scale, 1.0)
+
     def project(start, count, weight, bias):
         def body(h, carry):
             lanes = aligned(h, 4 * HD)
             total = dot_nn(r.x_all[pl.ds(start, count), :], weight[:, lanes]) + bias[:, lanes]
-            r.qkv[pl.ds(start, count), lanes] = total.astype(low)
+            r.qkv[pl.ds(start, count), lanes] = (total * scaling).astype(low)
             return carry
 
         lax.fori_loop(0, heads, body, 0)
@@ -253,14 +258,15 @@
         ask_copy(k).wait()
     ids = r.asked[...].reshape(slots, 128)
     lane = lax.broadcasted_iota(jnp.int32, (slots, 128), 1)
-
-    def pick_body(j, carry):
-        r.pick[:, aligned(j, 128)] = jnp.where(ids == lane + 128 * j, 1.0, 0.0).astype(low)
-        return carry
-
-    lax.fori_loop(0, r.table.shape[0] // 128, pick_body, 0)
     loaded(r.table)
-    found = dot_nn(r.pick[...], r.table[...]).astype(low)
+    piece = 4 * 128
+
+    def pick_body(j, found):
+        ones = [jnp.where(ids == lane + (j * piece + n * 128), 1.0, 0.0) for n in range(4)]
+        return found + dot_nn(jnp.concatenate(ones, 1).astype(low), r.table[aligned(j, piece), :])
+
+    found = jnp.zeros((slots, r.table.shape[1]), full)
+    found = lax.fori_loop(0, r.table.shape[0] // piece, pick_body, found).astype(low)
     r.found[...] = found.reshape(r.found.shape)
     r.answer[flat] = r.found[dp]
     for k in range(owners - 1):
@@ -289,34 +295,35 @@
         r.key[h] = r.qkv[:, h * 4 * HD + 2 * HD : h * 4 * HD + 3 * HD]
         r.value[h] = r.qkv[:, h * 4 * HD + 3 * HD : h * 4 * HD + 4 * HD]
 
-    def row_start(i, which):
-        start = jnp.where(
-            i < word_blocks, which * half_words + i * block, words + which * half_ents
-        )
-        return pl.ds(pl.multiple_of(start, block), block)
+    def both_kinds(which):
+        of_words = pl.ds(pl.multiple_of(which * half_words, half_words), half_words)
+        of_ents = pl.ds(pl.multiple_of(words + which * half_ents, half_ents), half_ents)
+        return (of_words, slice(0, half_words)), (of_ents, slice(half_words, rows))
+
+    def soften(start):
+        def body(i, carry):
+            here = pl.ds(pl.multiple_of(start + i * SOFT, SOFT), SOFT)
+            bias = r.mask[here, :].astype(full)
+            for h in range(heads):
+                score = r.prob[h, here, :] + bias
+                power = jnp.exp(score - jnp.max(score, 1, keepdims=True))
+                r.prob[h, here, :] = power * (1.0 / jnp.sum(power, 1, keepdims=True))
+            return carry
+
+        return body
 
     def attend(which, target):
-        def body(i, carry):
-            here = row_start(i, which)
-            outs = []
+        for here, _ in both_kinds(which):
             for h in range(heads):
                 query = r.qkv[here, h * 4 * HD : h * 4 * HD + 2 * HD]
-                score = jnp.concatenate(
-                    [
-                        dot_nt(query[:, :HD], r.key[h, 0:words, :]),
-                        dot_nt(query[:, HD:], r.key[h, words:everyone, :]),
-                    ],
-                    1,
-                )
-                score = score * score_scale + r.mask[here, :].astype(full)
-                power = jnp.exp(score - jnp.max(score, 1, keepdims=True))
-                prob = power / jnp.sum(power, 1, keepdims=True)
-                r.prob[h, here, :] = prob
-                outs.append(dot_nn(prob.astype(low), r.value[h]))
-            target[aligned(i, block), :] = jnp.concatenate(outs, 1).astype(low)
-            return carry
-
-        lax.fori_loop(0, blocks, body, 0)
+                r.prob[h, here, 0:words] = dot_nt(query[:, :HD], r.key[h, 0:words, :])
+                r.prob[h, here, words:] = dot_nt(query[:, HD:], r.key[h, words:everyone, :])
+        lax.fori_loop(0, half_words // SOFT, soften(which * half_words), 0)
+        lax.fori_loop(0, half_ents // SOFT, soften(words + which * half_ents), 0)
+        for here, there in both_kinds(which):
+            for h in range(heads):
+                out = dot_nn(r.prob[h, here, :].astype(low), r.value[h])
+                target[there, h * HD : (h + 1) * HD] = out.astype(low)
 
     attend(1 - x, r.heads_far)
     heads_copy = send(r.heads_far, r.heads_in, r.pair_s.at[2], r.pair_r.at[2], x_peer)
@@ -333,6 +340,16 @@
     def _():
         r.heads_all[:, 0:side] = r.heads_in[...]
         r.heads_all[:, side:] = r.heads_near[...]
+
+    def strip(which, turn, j):
+        part = (which, slice(0, rows), aligned(j, wide))
+        return send(
+            r.mail_out.at[part], r.mail_in.at[part], r.strip_s.at[turn, j], r.strip_r.at[turn, j], core
+        )
+
+    def wait_strips(which, turn):
+        for j in range(width // wide):
+            strip(which, turn, j).wait()
 
     def swap(which, turn, first, count):
         part = pl.ds(first, count)
@@ -348,14 +365,13 @@
 
         lax.fori_loop(0, count // wide, body, 0)
 
-    def fill_attn(lanes, _):
+    def fill_attn(lanes, j):
         r.mail_out[0, 0:rows, lanes] = dot_nn(r.heads_all[...], r.w_out[:, lanes])
+        strip(0, 0, j).start()
 
     loaded(r.w_out)
     columns(width, fill_attn)
-    attn_swap = swap(0, 0, 0, rows)
-    attn_swap.start()
-    attn_swap.wait()
+    wait_strips(0, 0)
 
     def over_rows(body):
         def step(i, carry):
@@ -382,15 +398,13 @@
     loaded(r.w_up)
     columns(hidden, fill_up)
 
-    def fill_down(lanes, _):
+    def fill_down(lanes, j):
         r.mail_out[1, 0:rows, lanes] = dot_nn(r.act[...], r.w_down[:, lanes])
+        strip(1, 1, j).start()
 
     loaded(r.w_down)
     columns(width, fill_down)
-    ffn_swap = swap(1, 1, 0, rows)
-    ffn_swap.start()
-    r.first_t[...] = r.first[...].T
-    ffn_swap.wait()
+    wait_strips(1, 1)
 
     vec = r.vec.at[0]
 
@@ -407,6 +421,8 @@
         r.grad_low[here, :] = back.astype(low)
         vec[7:8, :] += row_sum(back.astype(low).astype(full))
 
+    loaded(cot_words)
+    loaded(cot_ents)
     over_rows(second_norm)
 
     def halves(source, c, axis_flip):
@@ -436,8 +452,7 @@
         _, own = halves(kit.grads, c, flip)
 
         def body(i, carry):
-            total = own[i].astype(full) + kit.near[c, i].astype(full)
-            kit.near[c, i] = total.astype(low)
+            kit.near[c, i] = own[i] + kit.near[c, i]
             return carry
 
         lax.fori_loop(0, deep, body, 0)
@@ -448,8 +463,7 @@
         own = kit.near.at[c, :, x] if flip else kit.near.at[c, :, y]
 
         def body(i, carry):
-            total = own[i].astype(full) + kit.next[c, i].astype(full)
-            kit.next[c, i] = total.astype(low)
+            kit.next[c, i] = own[i] + kit.next[c, i]
             return carry
 
         lax.fori_loop(0, deep, body, 0)
@@ -492,8 +506,7 @@
         head_one(h).wait()
 
         def body(i, carry):
-            total = r.q_grads[h, i, y].astype(full) + r.q_near[h, i].astype(full)
-            r.q_near[h, i] = total.astype(low)
+            r.q_near[h, i] = r.q_grads[h, i, y] + r.q_near[h, i]
             return carry
 
         lax.fori_loop(0, deep, body, 0)
@@ -518,18 +531,49 @@
     chunk = r.grads.shape[5]
 
     def make_grad(c, left_t, right, lanes):
-        def body(i, carry):
-            part = dot_nn(left_t[aligned(i, band), :], right[:, lanes])
-            r.grads[c, i] = part.astype(low).reshape(2, 2, share, chunk)
-            return carry
-
-        lax.fori_loop(0, deep, body, 0)
-        stage_one(kit_a, c, flips[c]).start()
+        part = dot_nn(left_t[...], right[:, lanes]).astype(low)
+        r.grads[c] = part.reshape(deep, 2, 2, share, chunk)
+
+    plan = iter(schedule)
+
+    def vec_copy(n):
+        peer = x_peer if n == 0 else y_peer if n == 1 else z_peers[n - 2]
+        return send(r.vec.at[min(n, 2)], r.vec_in.at[n], r.vec_s.at[n], r.vec_r.at[n], peer)
+
+    def act_on(events):
+        for kind, c in events:
+            if kind == BEGIN:
+                stage_one(kit_a, c, flips[c]).start()
+            if kind == TURN:
+                to_two(kit_a, c, flips[c])
+            if kind == CLIMB:
+                to_three(kit_a, c, flips[c])
+            if kind == HEAD_CLIMB:
+                head_to_two(c)
+            if kind == HEAD_MEET:
+                head_to_three(c)
+            if kind == ENTS_TURN:
+                to_two(kit_e, 0, False)
+            if kind == ENTS_CLIMB:
+                to_three(kit_e, 0, False)
+            if kind == VEC_TURN:
+                vec_copy(0).wait()
+                r.vec[1] = r.vec[0] + r.vec_in[0]
+                vec_copy(1).start()
+            if kind == VEC_CLIMB:
+                vec_copy(1).wait()
+                r.vec[2] = r.vec[1] + r.vec_in[1]
+                for k in range(1, deep):
+                    vec_copy(1 + k).start()
+
+    def tick():
+        act_on(next(plan))
 
     downs = hidden // chunk
     r.grad_t[...] = r.grad_low[...].T
     for c in range(downs):
         make_grad(c, r.grad_t, r.act, slice(c * chunk, (c + 1) * chunk))
+        tick()
 
     def fill_dup(lanes, j):
         grad_act = dot_nt(r.grad_low[...], r.w_down[lanes, :])
@@ -540,20 +584,23 @@
         )
 
     columns(hidden, fill_dup)
-
-    def fill_back(lanes, _):
+    tick()
+
+    def fill_back(lanes, j):
         r.mail_out[0, 0:rows, lanes] = dot_nt(r.grad_up[...], r.w_up[lanes, :])
+        strip(0, 2, j).start()
 
     columns(width, fill_back)
-    back_swap = swap(0, 2, 0, rows)
-    back_swap.start()
+    tick()
+    r.first_t[...] = r.first[...].T
     r.out_words[...] = r.final[pl.ds(pl.multiple_of(t * (half_words // 2), half_words // 2), half_words // 2), :]
     r.out_ents[...] = r.final[
         pl.ds(pl.multiple_of(half_words + t * (half_ents // 2), half_ents // 2), half_ents // 2), :
     ]
     for c in range(downs):
         make_grad(downs + c, r.first_t, r.grad_up, slice(c * chunk, (c + 1) * chunk))
-    back_swap.wait()
+        tick()
+    wait_strips(0, 2)
 
     def first_back(here):
         grad = r.grad_second[here, :] + r.mail_out[0, here, :] + r.mail_in[0, here, :]
@@ -566,6 +613,7 @@
         vec[6:7, :] += row_sum(back.astype(low).astype(full))
 
     over_rows(first_back)
+    tick()
     near_rows = aligned(x, side)
     far_rows = aligned(1 - x, side)
     r.back_far[...] = dot_nt(r.grad_low[...], r.w_out[far_rows, :]).astype(low)
@@ -586,69 +634,62 @@
     r.grad_t[...] = r.grad_low[...].T
     outs = 2 * downs
     make_grad(outs, r.grad_t, r.heads_all, slice(0, chunk))
-
-    def ticks(events):
-        for kind, c in events:
-            if kind == "f":
-                to_two(kit_a, c, flips[c])
-            if kind == "s":
-                to_three(kit_a, c, flips[c])
-            if kind == "q":
-                head_to_two(c)
-            if kind == "r":
-                head_to_three(c)
-
-    ticks(schedule[0])
-    for copy in back_copies:
-        copy.wait()
+    tick()
+
 
     pair = 2 * HD
     for h in range(heads):
         base = h * 4 * HD
 
-        def score_back(i, carry):
-            here = aligned(i, block)
-            prob = r.prob[h, here, :]
-            grad_prob = dot_nt(r.back_heads[here, h * HD : (h + 1) * HD], r.value[h])
-            inner = jnp.sum(prob * grad_prob, 1, keepdims=True)
-            grad_score = (prob * (grad_prob - inner)).astype(low)
-            r.grad_score[here, :] = grad_score
-            r.prob_low[here, :] = prob.astype(low)
-            queries = jnp.concatenate(
-                [
-                    dot_nn(grad_score[:, :words], r.key[h, 0:words, :]),
-                    dot_nn(grad_score[:, words:], r.key[h, words:everyone, :]),
-                ],
-                1,
-            )
-            r.grad_qkv[here, base : base + pair] = (queries * score_scale).astype(low)
-            return carry
-
-        lax.fori_loop(0, everyone // block, score_back, 0)
-        ticks(schedule[1 + 2 * h])
+        def score_back(start):
+            def body(i, carry):
+                here = pl.ds(pl.multiple_of(start + i * SOFT, SOFT), SOFT)
+                prob, grad_prob = r.prob[h, here, :], r.grad_prob[here, :]
+                inner = jnp.sum(prob * grad_prob, 1, keepdims=True)
+                r.grad_score[here, :] = (prob * (grad_prob - inner)).astype(low)
+                r.prob_low[here, :] = prob.astype(low)
+                return carry
+
+            return body
+
+        for which in (x, 1 - x):
+            if which is not x:
+                tick()
+            if h == 0 and which is not x:
+                for copy in back_copies:
+                    copy.wait()
+            for here, _ in both_kinds(which):
+                r.grad_prob[here, :] = dot_nt(r.back_heads[here, h * HD : (h + 1) * HD], r.value[h])
+            lax.fori_loop(0, half_words // SOFT, score_back(which * half_words), 0)
+            lax.fori_loop(0, half_ents // SOFT, score_back(words + which * half_ents), 0)
+        queries = jnp.concatenate(
+            [
+                dot_nn(r.grad_score[:, :words], r.key[h, 0:words, :]),
+                dot_nn(r.grad_score[:, words:], r.key[h, words:everyone, :]),
+            ],
+            1,
+        )
+        r.grad_qkv[:, base : base + pair] = (queries * score_scale).astype(low)
+        tick()
         query_t = r.qkv[:, base : base + pair].T
         keys_t = dot_nn(query_t, r.grad_score[...])
-        keys_t = jnp.concatenate([keys_t[:HD, :words], keys_t[HD:, words:]], 1) * score_scale
+        keys_t = jnp.concatenate([keys_t[:HD, :words], keys_t[HD:, words:]], 1)
         values_t = dot_nn(r.back_heads[:, h * HD : (h + 1) * HD].T, r.prob_low[...])
         r.grad_qkv[:, base + pair : base + 2 * pair] = (
             jnp.concatenate([keys_t, values_t], 0).T.astype(low)
         )
 
-        def head_grad(i, carry):
-            here = aligned(i, band)
-            of_words = dot_nn(r.words_t[here, :], r.grad_qkv[0:words, base : base + pair])
-            of_ents = dot_nn(r.ents_t[here, :], r.grad_qkv[words:everyone, base : base + pair])
-            keyval = r.grad_qkv[:, base + pair : base + 2 * pair]
-            of_keyval = dot_nn(r.words_t[here, :], keyval[:words]) + dot_nn(
-                r.ents_t[here, :], keyval[words:]
+        tick()
+        keyval = slice(base + pair, base + 2 * pair)
+        query = slice(base, base + pair)
+        of_words = dot_nn(r.words_t[...], r.grad_qkv[0:words, query])
+        of_ents = dot_nn(r.ents_t[...], r.grad_qkv[words:everyone, query])
+        of_keyval = dot_nn(r.words_t[...], r.grad_qkv[0:words, keyval])
+        of_keyval = of_keyval + dot_nn(r.ents_t[...], r.grad_qkv[words:everyone, keyval])
+        for n, part in enumerate([of_words, of_ents, of_keyval]):
+            r.q_grads[h, :, :, :, :, n * pair : (n + 1) * pair] = part.astype(low).reshape(
+                deep, 2, 2, share, pair
             )
-            for n, part in enumerate([of_words, of_ents, of_keyval]):
-                r.q_grads[h, i, :, :, :, n * pair : (n + 1) * pair] = part.astype(low).reshape(
-                    2, 2, share, pair
-                )
-            return carry
-
-        lax.fori_loop(0, deep, head_grad, 0)
         head_one(h).start()
         sums = jnp.concatenate(
             [
@@ -660,7 +701,7 @@
         )
         place = h * 3 * pair
         vec[pl.ds(10 + 2 * x + place // width, 1), place % width : place % width + 3 * pair] = sums
-        ticks(schedule[2 + 2 * h])
+        tick()
 
     quarter = half_words // 2
 
@@ -669,16 +710,18 @@
 
     ents_part = input_grad(slice(words, everyone), r.cat_ents)
     r.mail_out[1, words // 2 :, :] = ents_part
-    ents_swap = swap(1, 3, words // 2, 2 * half_ents)
+    ents_swap = swap(1, 0, words // 2, 2 * half_ents)
     ents_swap.start()
+    tick()
     for n in range(2):
         r.mail_out[1, n * quarter : (n + 1) * quarter, :] = input_grad(
             aligned(2 * n + 1 - t, quarter), r.cat_words
         )
-    words_swap = swap(1, 4, 0, words // 2)
+    words_swap = swap(1, 1, 0, words // 2)
     words_swap.start()
     for n in range(2):
         r.input_part[n] = input_grad(aligned(2 * n + t, quarter), r.cat_words)
+    tick()
     ents_swap.wait()
     ents_place = pl.multiple_of(words // 2 + (1 - x) * half_ents, half_ents)
     ents_far = pl.ds(ents_place, half_ents)
@@ -686,11 +729,13 @@
     r.ents_back[...] = (r.mail_out[1, ents_far, :] + r.mail_in[1, ents_far, :]).astype(low)
     ents_copy = send(r.ents_back, r.ents_in, r.pair_s.at[5], r.pair_r.at[5], x_peer)
     ents_copy.start()
+    tick()
     words_swap.wait()
     far_place = aligned(1 - x, quarter)
     r.words_back[...] = (r.input_part[1 - x] + r.mail_in[1, far_place, :]).astype(low)
     words_back_copy = send(r.words_back, r.words_in, r.pair_s.at[6], r.pair_r.at[6], x_peer)
     words_back_copy.start()
+    tick()
     ents_copy.wait()
 
     grad = r.grad_first[half_words:rows, :] + (r.mail_out[1, ents_near, :] + r.mail_in[1, ents_near, :])
@@ -714,29 +759,14 @@
 
     lax.fori_loop(0, deep, ents_body, 0)
     stage_one(kit_e, 0, False).start()
-    vec_copies = [send(r.vec.at[0], r.vec_in.at[0], r.vec_s.at[0], r.vec_r.at[0], x_peer)]
-    vec_copies[0].start()
+    vec_copy(0).start()
     words_back_copy.wait()
     r.grad_words[...] = (
         r.grad_first[aligned(t, quarter), :]
         + (r.input_part[x] + r.mail_in[1, aligned(x, quarter), :])
         + r.words_in[...].astype(full)
     )
-    ticks(schedule[7])
-    to_two(kit_e, 0, False)
-    vec_copies[0].wait()
-    r.vec[1] = r.vec[0] + r.vec_in[0]
-    vec_copies.append(send(r.vec.at[1], r.vec_in.at[1], r.vec_s.at[1], r.vec_r.at[1], y_peer))
-    vec_copies[1].start()
-    ticks(schedule[8])
-    to_three(kit_e, 0, False)
-    vec_copies[1].wait()
-    r.vec[2] = r.vec[1] + r.vec_in[1]
-    for k in range(1, deep):
-        vec_copies.append(
-            send(r.vec.at[2], r.vec_in.at[1 + k], r.vec_s.at[1 + k], r.vec_r.at[1 + k], z_peers[k - 1])
-        )
-        vec_copies[-1].start()
+    tick()
     for k in range(owners - 1):
         slope_copy(k).wait()
     ids_t = r.asked[...].reshape(slots, 128).astype(full).T
@@ -744,10 +774,9 @@
     r.slopes_out[...] = r.slopes[...].reshape(slots, -1).astype(low)
     for c in range(2 * downs + 1):
         finish(kit_a, c)
-    ticks(schedule[9])
     total = r.vec[2]
     for k in range(1, deep):
-        vec_copies[1 + k].wait()
+        vec_copy(1 + k).wait()
         total = total + r.vec_in[1 + k]
     r.vec_out[...] = total
     r.across_out[...] = pltpu.roll(total[0:8, :], width - flat * share, 1)[:, 0:128]
@@ -764,79 +793,170 @@
 def finish_kernel(names, *refs):
     r = types.SimpleNamespace(**dict(zip(names, refs, strict=True)))
     low, full = jnp.bfloat16, jnp.float32
-    step = pl.program_id(0)
-    count, embed = r.adam_first.shape
-    slots = r.ids.shape[1]
-    row = lax.broadcasted_iota(jnp.int32, (count, slots), 0) + step * count
-    chosen = jnp.where(row == r.ids[0:1, :], 1.0, 0.0)
-    touched = jnp.max(chosen, 1, keepdims=True) > 0.0
-    grad = dot_nn(chosen.astype(low), r.slopes[...])
-    first, second = r.adam_first[...], r.adam_second[...]
-    first_next = beta_one * first + (1.0 - beta_one) * grad
-    second_next = beta_two * second + (1.0 - beta_two) * grad * grad
-    direction = (
-        first_next
-        * (1.0 / (1.0 - beta_one**adam_steps))
-        / (jnp.sqrt(second_next * (1.0 / (1.0 - beta_two**adam_steps))) + adam_eps)
-    )
-    r.table_update[...] = jnp.where(touched, direction, 0.0)
-    r.new_first[...] = jnp.where(touched, first_next, first)
-    r.new_second[...] = jnp.where(touched, second_next, second)
-
-    chunks, share, chunk = r.out_a.shape
+    table_rows, embed = r.hbm_first.shape
+    slots = r.hbm_ids.shape[1]
+    steps = r.in_s.shape[1]
+    count = table_rows // steps
+    chunks, share, chunk = r.hbm_a.shape
     downs = chunks // 2
-    heads, side = r.out_q.shape[0], r.out_q.shape[0] * HD
-    last = pl.num_programs(0) - 1
-
-    @pl.when(step == 0)
-    def _():
-        for c in range(downs):
-            r.red_down[c * chunk : (c + 1) * chunk, :] = r.out_a[c].T
-            r.red_up[:, c * chunk : (c + 1) * chunk] = r.out_a[downs + c]
-        r.red_out[...] = r.out_a[2 * downs].T
-
-    @pl.when(step == last // 2)
-    def _():
+    heads, side = r.hbm_q.shape[0], r.hbm_q.shape[0] * HD
+
+    pairs = [(r.hbm_ids, r.ids), (r.hbm_slopes, r.slopes)]
+    pairs += [(r.hbm_q, r.out_q), (r.hbm_e, r.out_e), (r.hbm_vec, r.vec), (r.hbm_across, r.across)]
+    layers = [(r.hbm_a.at[2 * downs], r.out_part)]
+    for c in range(downs):
+        lanes = slice(c * chunk, (c + 1) * chunk)
+        layers.append((r.hbm_a.at[c], r.down_part.at[:, lanes]))
+        layers.append((r.hbm_a.at[downs + c], r.up_part.at[:, lanes]))
+    layers += [(r.hbm_words, r.words_part), (r.hbm_ents, r.ents_part), (r.hbm_grad, r.grad_part)]
+    smalls = [
+        pltpu.make_async_copy(source, target, r.small_s.at[n])
+        for n, (source, target) in enumerate(pairs + layers)
+    ]
+    outs = [
+        pltpu.make_async_copy(source, target, r.done_s.at[n])
+        for n, (source, target) in enumerate(
+            [
+                (r.out_part, r.red_out),
+                (r.down_part, r.red_down),
+                (r.up_part, r.red_up),
+                (r.words_part, r.words_done.at[0]),
+                (r.ents_part, r.ents_done.at[0]),
+                (r.grad_part, r.grad_words_done.at[0]),
+                (r.query_part, r.red_query),
+                (r.keyval_part, r.red_keyval),
+            ]
+        )
+    ]
+
+    def moves(i, inward):
+        here = pl.ds(i * count, count)
+        if inward:
+            ends = [(r.hbm_first, r.first), (r.hbm_second, r.second)]
+            flags = r.in_s
+        else:
+            ends = [(r.update, r.table_update), (r.first, r.new_first), (r.second, r.new_second)]
+            flags = r.out_s
+        return [
+            pltpu.make_async_copy(source.at[here, :], target.at[here, :], flags.at[n, i])
+            for n, (source, target) in enumerate(ends)
+        ]
+
+    early, late = smalls[:2], smalls[2:]
+    for copy in early + moves(0, True) + moves(1, True) + late:
+        copy.start()
+    for i in range(2, steps):
+        for copy in moves(i, True):
+            copy.start()
+    for copy in early:
+        copy.wait()
+    r.addends[:, 0:embed] = r.slopes[...]
+    r.addends[:, embed:] = jnp.ones((slots, 128), low)
+
+    def adam(i):
+        for copy in moves(i, True):
+            copy.wait()
+        here = pl.ds(i * count, count)
+        row = lax.broadcasted_iota(jnp.int32, (count, slots), 0) + i * count
+        chosen = jnp.where(row == r.ids[0:1, :], 1.0, 0.0).astype(low)
+        total = dot_nn(chosen, r.addends[...])
+        touched = total[:, embed:] > 0.0
+        for start in range(0, embed, 128):
+            lanes = slice(start, start + 128)
+            grad = total[:, lanes]
+            first, second = r.first[here, lanes], r.second[here, lanes]
+            first_next = beta_one * first + (1.0 - beta_one) * grad
+            second_next = beta_two * second + (1.0 - beta_two) * grad * grad
+            direction = (
+                first_next
+                * (1.0 / (1.0 - beta_one**adam_steps))
+                / (jnp.sqrt(second_next * (1.0 / (1.0 - beta_two**adam_steps))) + adam_eps)
+            )
+            r.update[here, lanes] = jnp.where(touched, direction, 0.0)
+            r.first[here, lanes] = jnp.where(touched, first_next, first)
+            r.second[here, lanes] = jnp.where(touched, second_next, second)
+        for copy in moves(i, False):
+            copy.start()
+
+    def lay_out_rest():
+        for copy in late:
+            copy.wait()
+        for copy in outs[:6]:
+            copy.start()
+        width = r.vec.shape[1]
         for n in range(2):
-            r.red_entity[n * 128 : (n + 1) * 128, :] = r.out_e[n].T
+            r.red_entity[:, n * 128 : (n + 1) * 128] = r.out_e[n]
             for h in range(heads):
                 place = h * 6 * HD
-                line = 10 + 2 * n + place // r.vec.shape[1]
+                line = 10 + 2 * n + place // width
                 for j in range(6):
                     lanes = slice(n * side + h * HD, n * side + (h + 1) * HD)
                     part = r.out_q[h, n, :, j * HD : (j + 1) * HD]
-                    begin = place % r.vec.shape[1] + j * HD
+                    begin = place % width + j * HD
                     line_part = r.vec[line : line + 1, begin : begin + HD]
                     if j < 4:
-                        r.red_query[j, :, lanes] = part
+                        r.query_part[j, :, lanes] = part
                         r.red_query_bias[j : j + 1, lanes] = line_part
                     else:
-                        r.red_keyval[j - 4, :, lanes] = part
+                        r.keyval_part[j - 4, :, lanes] = part
                     if j == 5:
                         r.value_row[:, lanes] = line_part
+        for copy in outs[6:]:
+            copy.start()
         r.red_gain[...] = r.across[0:3, 0:share]
         r.red_shift[...] = r.across[3:6, 0:share]
         r.red_value_bias[...] = r.value_row[...].reshape(-1)
         r.red_out_bias[...] = r.across[6:7, 0:share].reshape(-1)
         r.red_down_bias[...] = r.across[7:8, 0:share].reshape(-1)
-        width = r.vec.shape[1]
         for n in range(2):
             r.red_up_bias[n * width : (n + 1) * width] = r.vec[8 + n : 9 + n, :].reshape(-1)
 
-
+    for i in range(steps):
+        adam(i)
+        if i == steps // 2:
+            lay_out_rest()
+    for i in range(steps):
+        for copy in moves(i, False):
+            copy.wait()
+    for copy in outs:
+        copy.wait()
+
+
+SOFT = 32
+STEPS = 8
+BEGIN, TURN, CLIMB, HEAD_CLIMB, HEAD_MEET, ENTS_TURN, ENTS_CLIMB, VEC_TURN, VEC_CLIMB = range(9)
 SCHEDULE = (
-    [("f", 0), ("f", 1)],
-    [("f", 2)],
-    [("s", 0), ("s", 1), ("f", 3)],
-    [("f", 4)],
-    [("s", 2), ("f", 5), ("s", 3)],
-    [("f", 6), ("s", 4)],
-    [("f", 7), ("s", 5), ("f", 8)],
-    [("s", 6), ("s", 7), ("s", 8), ("q", 0)],
-    [("q", 1), ("q", 2)],
-    [("r", 0), ("r", 1), ("r", 2)],
+    ((BEGIN, 0),),
+    (),
+    ((BEGIN, 2),),
+    (),
+    (),
+    (),
+    (),
+    ((BEGIN, 5),),
+    (),
+    ((BEGIN, 7),),
+    ((TURN, 0),),
+    ((TURN, 7), (BEGIN, 8),),
+    ((BEGIN, 1), (TURN, 5),),
+    (),
+    ((CLIMB, 0),),
+    ((CLIMB, 7),),
+    (),
+    (),
+    ((BEGIN, 4),),
+    ((CLIMB, 5),),
+    ((TURN, 8),),
+    ((HEAD_CLIMB, 0),),
+    (),
+    (),
+    ((HEAD_CLIMB, 1),),
+    ((TURN, 2), (BEGIN, 3), (TURN, 4), (BEGIN, 6),),
+    ((CLIMB, 8), (HEAD_CLIMB, 2),),
+    ((CLIMB, 4), (TURN, 1), (TURN, 3), (CLIMB, 2),),
+    ((HEAD_MEET, 0), (TURN, 6), (CLIMB, 1), (ENTS_TURN, 0), (VEC_TURN, 0), (CLIMB, 3), (CLIMB, 6), (HEAD_MEET, 1), (HEAD_MEET, 2), (ENTS_CLIMB, 0), (VEC_CLIMB, 0),),
 )
-FLIPS = (False, True, False, False, True, False, False, True, False)
+FLIPS = (False, False, True, False, False, False, True, True, False)
 
 
 def fused_local(
@@ -881,7 +1001,6 @@
     chunks = 2 * (hidden // chunk) + 1
 
     operands = dict(
-        words=word_states.reshape(half_words, width),
         shard=entity_shard.reshape(1, half_ents),
         row=entity_row.reshape(1, half_ents),
         word_seg=word_segments,
@@ -893,10 +1012,11 @@
         b_out=b_out,
         b_up=b_up,
         b_down=b_down,
-        cot_words=cot_words.reshape(half_words, width),
-        cot_ents=cot_entities.reshape(half_ents, width),
     )
     streamed = dict(
+        hbm_words=word_states,
+        hbm_cot_words=cot_words,
+        hbm_cot_ents=cot_entities,
         hbm_query=w_query,
         hbm_keyval=w_keyval,
         hbm_table=entity_table,
@@ -936,7 +1056,6 @@
         asked=((owners, capacity, 128), jnp.int32),
         outbox=((owners * capacity, half_ents), low),
         select=((ents, owners * 2 * capacity), low),
-        pick=((owners * capacity, table_rows), low),
         found=((owners // 2, 2 * capacity, embed), low),
         answer=((owners, 2 * capacity, embed), low),
         looked=((ents, embed), low),
@@ -971,6 +1090,7 @@
         grad_first=((rows, width), full),
         back_far=((rows, side), low),
         back_heads=((everyone, side), low),
+        grad_prob=((everyone, everyone), full),
         grad_score=((everyone, everyone), low),
         prob_low=((everyone, everyone), low),
         grad_qkv=((everyone, 4 * side), low),
@@ -1001,7 +1121,7 @@
         q_in=((heads, share, chunk), full),
     )
     signals = dict(
-        load_s=(7,),
+        load_s=(10,),
         ask_s=(owners - 1,),
         ask_r=(owners - 1,),
         answer_s=(owners - 1,),
@@ -1010,8 +1130,10 @@
         slope_r=(owners - 1,),
         pair_s=(8,),
         pair_r=(8,),
-        swap_s=(5,),
-        swap_r=(5,),
+        strip_s=(3, width // 256),
+        strip_r=(3, width // 256),
+        swap_s=(2,),
+        swap_r=(2,),
         vec_s=(deep + 1,),
         vec_r=(deep + 1,),
     )
@@ -1038,52 +1160,84 @@
     )(*operands.values(), *streamed.values())
     got = types.SimpleNamespace(**dict(zip(results, made, strict=True)))
 
-    step = table_rows // 8
-    table = pl.BlockSpec((step, embed), lambda i: (i, 0))
-
-    def whole(shape):
-        return pl.BlockSpec(shape, lambda i: (0,) * len(shape))
-
     given = dict(
-        adam_first=adam_first,
-        adam_second=adam_second,
-        ids=got.ids_out,
-        slopes=got.slopes_out,
-        out_a=got.out_a,
-        out_e=got.out_e,
-        out_q=got.out_q,
-        vec=got.vec_out,
-        across=got.across_out,
+        hbm_first=adam_first,
+        hbm_second=adam_second,
+        hbm_ids=got.ids_out,
+        hbm_slopes=got.slopes_out,
+        hbm_a=got.out_a,
+        hbm_e=got.out_e,
+        hbm_q=got.out_q,
+        hbm_vec=got.vec_out,
+        hbm_across=got.across_out,
+        hbm_words=got.out_words,
+        hbm_ents=got.out_ents,
+        hbm_grad=got.grad_words,
     )
     final = dict(
-        red_entity=(embed, share),
+        words_done=(1, half_words // 2, width),
+        ents_done=(1, half_ents // 2, width),
+        grad_words_done=(1, half_words // 2, width),
+        red_entity=(share, embed),
         red_gain=(3, share),
         red_shift=(3, share),
         red_query=(4, share, local_width),
         red_query_bias=(4, local_width),
         red_keyval=(2, share, local_width),
         red_value_bias=(local_width,),
-        red_out=(local_width, share),
+        red_out=(share, local_width),
         red_out_bias=(share,),
         red_up=(share, hidden),
         red_up_bias=(hidden,),
-        red_down=(hidden, share),
+        red_down=(share, hidden),
         red_down_bias=(share,),
         table_update=adam_first.shape,
         new_first=adam_first.shape,
         new_second=adam_first.shape,
     )
+    room = dict(
+        value_row=((1, local_width), full),
+        ids=(got.ids_out.shape, jnp.int32),
+        slopes=(got.slopes_out.shape, low),
+        addends=((owners * capacity, embed + 128), low),
+        out_e=(got.out_e.shape, full),
+        out_q=(got.out_q.shape, full),
+        vec=(got.vec_out.shape, full),
+        across=(got.across_out.shape, full),
+        first=(adam_first.shape, full),
+        second=(adam_first.shape, full),
+        update=(adam_first.shape, full),
+        out_part=((share, local_width), full),
+        down_part=((share, hidden), full),
+        up_part=((share, hidden), full),
+        words_part=(got.out_words.shape, low),
+        ents_part=(got.out_ents.shape, low),
+        grad_part=(got.grad_words.shape, full),
+        query_part=((4, share, local_width), full),
+        keyval_part=((2, share, local_width), full),
+    )
+    flags = dict(small_s=(chunks + 9,), done_s=(8,), in_s=(2, STEPS), out_s=(3, STEPS))
+    in_place, in_vmem = (pl.BlockSpec(memory_space=space) for space in (pl.ANY, pltpu.VMEM))
+    manual = set(dict(words_done=0, ents_done=0, grad_words_done=0, red_query=0, red_keyval=0))
+    manual |= set(dict(red_out=0, red_up=0, red_down=0, table_update=0, new_first=0, new_second=0))
     finished = pl.pallas_call(
-        functools.partial(finish_kernel, [*given, *final, *dict(value_row=0)]),
+        functools.partial(finish_kernel, [*given, *final, *room, *flags]),
         name="finish",
-        grid=(8,),
-        out_shape=[jax.ShapeDtypeStruct(shape, full) for shape in final.values()],
-        in_specs=[table, table] + [whole(item.shape) for item in list(given.values())[2:]],
-        out_specs=[whole(shape) for shape in list(final.values())[:-3]] + [table] * 3,
-        scratch_shapes=[pltpu.VMEM((1, local_width), full)],
-        compiler_params=pltpu.CompilerParams(vmem_limit_bytes=40 * 2**20),
+        out_shape=[
+            jax.ShapeDtypeStruct(shape, low if n < 2 else full)
+            for n, shape in enumerate(final.values())
+        ],
+        in_specs=[in_place] * len(given),
+        out_specs=[in_place if name in manual else in_vmem for name in final],
+        scratch_shapes=[pltpu.VMEM(*item) for item in room.values()]
+        + [dma(shape) for shape in flags.values()],
+        compiler_params=pltpu.CompilerParams(vmem_limit_bytes=67_043_328),
     )(*given.values())
-    return (got.out_words[None], got.out_ents[None], got.grad_words[None], *finished)
+    done = dict(zip(final, finished, strict=True))
+    return tuple(
+        item.T if name in ("red_entity", "red_out", "red_down") else item
+        for name, item in done.items()
+    )
 
 
 def plain_local(

time: 189 us -> 135 us (0.71)
  Pallas kernels: 173 us -> 133 us
  local copies, waits for them, and re-layouts: 14.7 us -> 0 us
    pallas_call x1, Pallas kernels: 165 us -> 123 us  [fused_local(): pl.pallas_call(kernel, name='layer', out_shape=[jax.ShapeDtypeStruct(*ite...]
    unnamed x30 -> x0, local copies, waits for them, and re-layouts: 14.7 us -> none
    pallas_call x1, Pallas kernels: 8.17 us -> 10.4 us  [fused_local(): pl.pallas_call(functools.partial(finish_kernel, [*given, *final, *room, *...]
where the time goes in v3:
time: 135 us; the launch traced here: 134 us
  Pallas kernels  133 us (99%)
    pallas_call x1, Pallas kernels, fused_local(): pl.pallas_call(kernel, name='layer', out_shape=[jax.ShapeDtypeStruct(*ite...  123 us
    pallas_call x1, Pallas kernels, fused_local(): pl.pallas_call(functools.partial(finish_kernel, [*given, *final, *room, *...  10.4 us

profile of v3, /device:TPU:0, one launch (start us, length us, event | category | flops | bytes accessed | tf_op | source)
XLA Modules:
  0.0 134.3 jit_solution(14718127868307887955)
XLA Ops:
  0.7 123.1 %layer.1 = (bf16[128,768]{1,0:T(8,128)(2,1)}, bf16[32,768]{1,0:T(8,128)(2,1)}, f32[128,768]{1,0:T(8,128)}, f32[9,48,384]{2,1,0:T(8,128)}, f32[2,48,128]{2,1,0:T(...) custom-call(s32[1,64]{1,0:T(1,128)} %bitcast.5, ...), custom_call_target="tpu_custom_call" | custom-call | tf_op jit(solution)/shard_map/layer/pallas_call | solution.py:1148
  123.8 10.4 %finish.1 = (bf16[1,128,768]{2,1,0:T(8,128)(2,1)}, bf16[1,32,768]{2,1,0:T(8,128)(2,1)}, f32[1,128,768]{2,1,0:T(8,128)}, f32[48,256]{1,0:T(8,128)}, f32[3,48]{1,0...) custom-call(f32[4096,256]{1,0:T(8,128)} %refs_0_.1, ...), custom_call_target="tpu_custom_call" | custom-call | tf_op jit(solution)/shard_map/finish/pallas_call | solution.py:1223

commit v4 on v3

--- a/solution.py
+++ b/solution.py
@@ -100,13 +100,12 @@
     return pl.ds(pl.multiple_of(index * step, step), step)
 
 
-def layer_kernel(names, flips, schedule, *refs):
+def layer_kernel(names, orders, schedule, *refs):
     r = types.SimpleNamespace(**dict(zip(names, refs, strict=True)))
     low, full = jnp.bfloat16, jnp.float32
     dp, x, t = lax.axis_index("dp"), lax.axis_index("stream"), lax.axis_index("tensor")
     y, z = lax.rem(dp, 2), dp // 2
-    deep = lax.axis_size("dp") // 2
-    owners = 4 * deep
+    owners = lax.axis_size("dp") * 2
     _, half_words, width = r.hbm_words.shape
     half_ents = r.shard.shape[1]
     rows, words = half_words + half_ents, 2 * half_words
@@ -123,19 +122,22 @@
     wide = 256
 
     core, x_peer, y_peer = {"tensor": 1 - t}, {"stream": 1 - x}, {"dp": z * 2 + 1 - y}
-    z_peers = [{"dp": lax.rem(z + k, deep) * 2 + y} for k in range(1, deep)]
+    z_low, z_high = lax.rem(z, 2), z // 2
+    near_peer = {"dp": (z + 1 - 2 * z_low) * 2 + y}
+    far_peer = {"dp": (z + 2 - 4 * z_high) * 2 + y}
+    mine_on = (z_high, z_low, y, x)
+    peer_on = (far_peer, near_peer, y_peer, x_peer)
     flat = dp * 2 + x
     others = []
     for k in range(1, owners):
         other = lax.rem(flat + k, owners)
         others.append((other, {"dp": other // 2, "stream": lax.rem(other, 2)}))
 
+    loads = {}
     barrier = pltpu.get_barrier_semaphore()
     for peer in [core] + [peer for _, peer in others]:
         pl.semaphore_signal(barrier, inc=1, device_id=peer, device_id_type=MESH_ID)
 
-    loads = {}
-
     def load(source, target):
         loads[id(target)] = pltpu.make_async_copy(source, target, r.load_s.at[len(loads)])
         loads[id(target)].start()
@@ -143,10 +145,19 @@
     def loaded(target):
         loads.pop(id(target)).wait()
 
+    load(r.hbm_shard, r.shard)
+    load(r.hbm_row, r.row)
     my_words = r.x_all.at[aligned(x, half_words), :]
     load(r.hbm_words.at[0], my_words)
     load(r.hbm_query, r.w_query)
     load(r.hbm_keyval, r.w_keyval)
+    smalls = [
+        (r.hbm_b_query, r.b_query), (r.hbm_b_value, r.b_value), (r.hbm_word_seg, r.word_seg),
+        (r.hbm_ent_seg, r.ent_seg), (r.hbm_gain, r.gain), (r.hbm_shift, r.shift),
+        (r.hbm_b_out, r.b_out), (r.hbm_b_up, r.b_up), (r.hbm_b_down, r.b_down),
+    ]
+    for source, target in smalls:
+        load(source, target)
     load(r.hbm_table, r.table)
     load(r.hbm_entity, r.w_entity)
     cot_words, cot_ents = r.cotangent.at[0:half_words, :], r.cotangent.at[half_words:rows, :]
@@ -156,6 +167,14 @@
     load(r.hbm_up, r.w_up)
     load(r.hbm_down, r.w_down)
 
+    flushes = []
+
+    def flush(source, target):
+        flushes.append(pltpu.make_async_copy(source, target, r.flush_s.at[len(flushes)]))
+        flushes[-1].start()
+
+    loaded(r.shard)
+    loaded(r.row)
     shard_row = r.shard[...]
     shard_all = jnp.broadcast_to(shard_row.astype(full), (half_ents, half_ents)).T
     shard_all = shard_all.astype(jnp.int32)
@@ -182,6 +201,8 @@
 
     loaded(r.w_query)
     loaded(r.w_keyval)
+    for _, target in smalls:
+        loaded(target)
 
     def gather_columns(which):
         for h in range(heads):
@@ -231,7 +252,9 @@
     my_select = r.select.at[aligned(x, half_ents), :]
     select_copy = send(my_select, my_select, r.pair_s.at[0], r.pair_r.at[0], x_peer)
     select_copy.start()
-    words_copy = send(my_words, my_words, r.pair_s.at[1], r.pair_r.at[1], x_peer)
+    half = half_words // 2
+    my_half = r.x_all.at[aligned(2 * x + t, half), :]
+    words_copy = send(my_half, my_half, r.pair_s.at[1], r.pair_r.at[1], x_peer)
     words_copy.start()
 
     is_query = lax.broadcasted_iota(jnp.int32, (1, 4 * HD), 1) < 2 * HD
@@ -254,6 +277,11 @@
         equal = own_seg[:, 0:1].astype(jnp.int32) == segments
         r.mask[i * 128 : (i + 1) * 128, :] = jnp.where(equal, 0.0, masked_score).astype(low)
 
+    words_copy.wait()
+    far_half = r.x_all.at[aligned(2 * (1 - x) + t, half), :]
+    relay = send(far_half, far_half, r.pair_s.at[8], r.pair_r.at[8], core)
+    relay.start()
+
     for k in range(owners - 1):
         ask_copy(k).wait()
     ids = r.asked[...].reshape(slots, 128)
@@ -272,9 +300,45 @@
     for k in range(owners - 1):
         answer_copy(k).start()
 
-    words_copy.wait()
+    relay.wait()
     project(pl.multiple_of((1 - x) * half_words, half_words), half_words, r.cat_words, r.bias_words)
-    r.words_t[...] = r.x_all[0:words, :].T
+
+    def take_heads(here):
+        for h in range(heads):
+            r.key[h, here, :] = r.qkv[here, h * 4 * HD + 2 * HD : h * 4 * HD + 3 * HD]
+            r.value[h, here, :] = r.qkv[here, h * 4 * HD + 3 * HD : h * 4 * HD + 4 * HD]
+
+    of_words, of_ents = slice(0, words), slice(words, everyone)
+    take_heads(of_words)
+    for h in range(heads):
+        query = r.qkv[of_words, h * 4 * HD : h * 4 * HD + HD]
+        r.prob[h, of_words, of_words] = dot_nt(query, r.key[h, of_words, :])
+
+    def mass_lanes(which, h):
+        return pl.ds(pl.multiple_of((which * heads + h) * 128, 128), 128)
+
+    def soften_words(which):
+        def body(i, carry):
+            here = pl.ds(pl.multiple_of(which * half_words + i * SOFT, SOFT), SOFT)
+            bias = r.mask[here, of_words].astype(full)
+            for h in range(heads):
+                score = r.prob[h, here, of_words] + bias
+                peak = jnp.max(score, 1, keepdims=True)
+                power = jnp.exp(score - peak)
+                r.prob[h, here, of_words] = power
+                r.factor[h, here, :] = jnp.broadcast_to(peak, (SOFT, 128))
+                mass = jnp.broadcast_to(jnp.sum(power, 1, keepdims=True), (SOFT, 128))
+                r.mail_out[1, aligned(i, SOFT), mass_lanes(which, h)] = mass
+            return carry
+
+        lax.fori_loop(0, half_words // SOFT, body, 0)
+
+    soften_words(0)
+    soften_words(1)
+    for h in range(heads):
+        weights = r.prob[h, of_words, of_words].astype(low)
+        r.grad_prob[of_words, h * 128 : h * 128 + HD] = dot_nn(weights, r.value[h, of_words, :])
+        r.factor[h, of_ents, :] = jnp.ones((2 * half_ents, 128), full)
 
     select_copy.wait()
     for k in range(owners - 1):
@@ -290,46 +354,73 @@
     r.x_all[words:everyone, :] = x_entity.astype(low)
     r.x_own[half_words:rows, :] = r.x_ent[aligned(x, half_ents), :]
     project(words, 2 * half_ents, r.cat_ents, r.bias_ents)
-    r.ents_t[...] = r.x_all[words:everyone, :].T
-    for h in range(heads):
-        r.key[h] = r.qkv[:, h * 4 * HD + 2 * HD : h * 4 * HD + 3 * HD]
-        r.value[h] = r.qkv[:, h * 4 * HD + 3 * HD : h * 4 * HD + 4 * HD]
+    take_heads(of_ents)
 
     def both_kinds(which):
-        of_words = pl.ds(pl.multiple_of(which * half_words, half_words), half_words)
-        of_ents = pl.ds(pl.multiple_of(words + which * half_ents, half_ents), half_ents)
-        return (of_words, slice(0, half_words)), (of_ents, slice(half_words, rows))
-
-    def soften(start):
-        def body(i, carry):
-            here = pl.ds(pl.multiple_of(start + i * SOFT, SOFT), SOFT)
-            bias = r.mask[here, :].astype(full)
-            for h in range(heads):
-                score = r.prob[h, here, :] + bias
-                power = jnp.exp(score - jnp.max(score, 1, keepdims=True))
-                r.prob[h, here, :] = power * (1.0 / jnp.sum(power, 1, keepdims=True))
-            return carry
-
-        return body
-
-    def attend(which, target):
-        for here, _ in both_kinds(which):
-            for h in range(heads):
-                query = r.qkv[here, h * 4 * HD : h * 4 * HD + 2 * HD]
-                r.prob[h, here, 0:words] = dot_nt(query[:, :HD], r.key[h, 0:words, :])
-                r.prob[h, here, words:] = dot_nt(query[:, HD:], r.key[h, words:everyone, :])
-        lax.fori_loop(0, half_words // SOFT, soften(which * half_words), 0)
-        lax.fori_loop(0, half_ents // SOFT, soften(words + which * half_ents), 0)
-        for here, there in both_kinds(which):
-            for h in range(heads):
-                out = dot_nn(r.prob[h, here, :].astype(low), r.value[h])
-                target[there, h * HD : (h + 1) * HD] = out.astype(low)
-
-    attend(1 - x, r.heads_far)
-    heads_copy = send(r.heads_far, r.heads_in, r.pair_s.at[2], r.pair_r.at[2], x_peer)
-    heads_copy.start()
-    attend(x, r.heads_near)
-    heads_copy.wait()
+        near_words = pl.ds(pl.multiple_of(which * half_words, half_words), half_words)
+        near_ents = pl.ds(pl.multiple_of(words + which * half_ents, half_ents), half_ents)
+        return (near_words, slice(0, half_words)), (near_ents, slice(half_words, rows))
+
+    def soften_ents(here):
+        bias = r.mask[here, :].astype(full)
+        for h in range(heads):
+            score = r.prob[h, here, :] + bias
+            power = jnp.exp(score - jnp.max(score, 1, keepdims=True))
+            r.prob[h, here, :] = power * (1.0 / jnp.sum(power, 1, keepdims=True))
+
+    def complete_words(which, here):
+        bias = r.mask[here, of_ents].astype(full)
+        for h in range(heads):
+            score = r.prob[h, here, of_ents] + bias
+            peak = r.factor[h, here, :]
+            best = jnp.broadcast_to(jnp.max(score, 1, keepdims=True), (half_words, 128))
+            top = jnp.maximum(peak, best)
+            power, shrink = jnp.exp(score - top), jnp.exp(peak - top)
+            added = jnp.broadcast_to(jnp.sum(power, 1, keepdims=True), (half_words, 128))
+            mass = r.mail_out[1, 0:half_words, mass_lanes(which, h)]
+            share_of = 1.0 / (mass * shrink + added)
+            r.prob[h, here, of_ents] = power * share_of
+            r.factor[h, here, :] = shrink * share_of
+
+    def attend_words(which, target):
+        (here, there), _ = both_kinds(which)
+        for h in range(heads):
+            query = r.qkv[here, h * 4 * HD + HD : h * 4 * HD + 2 * HD]
+            r.prob[h, here, of_ents] = dot_nt(query, r.key[h, of_ents, :])
+        complete_words(which, here)
+        for h in range(heads):
+            out = r.grad_prob[here, h * 128 : h * 128 + HD] * r.factor[h, here, 0:HD]
+            out = out + dot_nn(r.prob[h, here, of_ents].astype(low), r.value[h, of_ents, :])
+            target[there, h * HD : (h + 1) * HD] = out.astype(low)
+
+    def attend_ents(which, target):
+        _, (here, there) = both_kinds(which)
+        for h in range(heads):
+            query = r.qkv[here, h * 4 * HD : h * 4 * HD + 2 * HD]
+            r.prob[h, here, of_words] = dot_nt(query[:, :HD], r.key[h, of_words, :])
+            r.prob[h, here, of_ents] = dot_nt(query[:, HD:], r.key[h, of_ents, :])
+        soften_ents(here)
+        for h in range(heads):
+            out = dot_nn(r.prob[h, here, :].astype(low), r.value[h])
+            target[there, h * HD : (h + 1) * HD] = out.astype(low)
+
+    def heads_part(n, part):
+        return send(
+            r.heads_far.at[part, :], r.heads_in.at[part, :], r.heads_s.at[n], r.heads_r.at[n], x_peer
+        )
+
+    attend_words(1 - x, r.heads_far)
+    heads_copies = [heads_part(0, slice(0, half_words))]
+    heads_copies[0].start()
+    attend_ents(1 - x, r.heads_far)
+    heads_copies.append(heads_part(1, slice(half_words, rows)))
+    heads_copies[1].start()
+    attend_words(x, r.heads_near)
+    attend_ents(x, r.heads_near)
+    r.words_t[...] = r.x_all[of_words, :].T
+    r.ents_t[...] = r.x_all[of_ents, :].T
+    for copy in heads_copies:
+        copy.wait()
 
     @pl.when(x == 0)
     def _():
@@ -425,149 +516,96 @@
     loaded(cot_ents)
     over_rows(second_norm)
 
-    def halves(source, c, axis_flip):
-        if axis_flip:
-            return source.at[c, :, 1 - y], source.at[c, :, y]
-        return source.at[c, :, :, 1 - x], source.at[c, :, :, x]
-
-    def stage_one(kit, c, flip):
-        away, _ = halves(kit.grads, c, flip)
-        return send(away, kit.near.at[c], kit.s1.at[c], kit.r1.at[c], y_peer if flip else x_peer)
-
-    def stage_two(kit, c, flip):
-        away = kit.near.at[c, :, 1 - x] if flip else kit.near.at[c, :, 1 - y]
-        return send(away, kit.next.at[c], kit.s2.at[c], kit.r2.at[c], x_peer if flip else y_peer)
-
-    def stage_three(kit, c, k):
-        return send(
-            kit.next.at[c, lax.rem(z + k, deep)],
-            kit.far.at[c, k - 1],
-            kit.s3.at[c, k - 1],
-            kit.r3.at[c, k - 1],
-            z_peers[k - 1],
+    def halved(ref, place, index):
+        return ref.at[(slice(None),) * place + (index,)]
+
+    def stage(kit, c, order, n):
+        left = [axis for axis in range(4) if axis not in order[:n]]
+        axis, place = order[n], left.index(order[n])
+        held = kit.held[n].at[c]
+        copy = send(
+            halved(held, place, 1 - mine_on[axis]), kit.held[n + 1].at[c],
+            kit.sent.at[c, n], kit.got.at[c, n], peer_on[axis],
         )
-
-    def to_two(kit, c, flip):
-        stage_one(kit, c, flip).wait()
-        _, own = halves(kit.grads, c, flip)
+        return copy, halved(held, place, mine_on[axis])
+
+    def advance(kit, c, order, n):
+        copy, own = stage(kit, c, order, n - 1)
+        copy.wait()
+        total = kit.held[n].at[c]
 
         def body(i, carry):
-            kit.near[c, i] = own[i] + kit.near[c, i]
+            total[i] = own[i] + total[i]
             return carry
 
-        lax.fori_loop(0, deep, body, 0)
-        stage_two(kit, c, flip).start()
-
-    def to_three(kit, c, flip):
-        stage_two(kit, c, flip).wait()
-        own = kit.near.at[c, :, x] if flip else kit.near.at[c, :, y]
-
-        def body(i, carry):
-            kit.next[c, i] = own[i] + kit.next[c, i]
-            return carry
-
-        lax.fori_loop(0, deep, body, 0)
-        for k in range(1, deep):
-            stage_three(kit, c, k).start()
-
-    def finish(kit, c):
-        for k in range(1, deep):
-            stage_three(kit, c, k).wait()
-        total = kit.next[c, z].astype(full)
-        for k in range(1, deep):
-            total = total + kit.far[c, k - 1].astype(full)
-        kit.out[c] = total
+        lax.fori_loop(0, 2, body, 0)
+        stage(kit, c, order, n)[0].start()
+
+    def finish(kit, c, order):
+        copy, own = stage(kit, c, order, 3)
+        copy.wait()
+        kit.out[c] = own[...].astype(full) + kit.held[4][c].astype(full)
 
     kit_a = types.SimpleNamespace(
-        grads=r.grads, near=r.near, next=r.next, far=r.far, out=r.out_a,
-        s1=r.a_s1, r1=r.a_r1, s2=r.a_s2, r2=r.a_r2, s3=r.a_s3, r3=r.a_r3,
+        held=(r.grads, r.near, r.next, r.far, r.last), out=r.out_a, sent=r.a_s, got=r.a_r
     )
     kit_e = types.SimpleNamespace(
-        grads=r.e_grads, near=r.e_near, next=r.e_next, far=r.e_far, out=r.e_sum,
-        s1=r.e_s1, r1=r.e_r1, s2=r.e_s2, r2=r.e_r2, s3=r.e_s3, r3=r.e_r3,
-    )
-
-    def head_one(h):
-        return send(r.q_grads.at[h, :, 1 - y], r.q_near.at[h], r.q_s1.at[h], r.q_r1.at[h], y_peer)
-
-    def head_two(h, k):
-        return send(
-            r.q_near.at[h, lax.rem(z + k, deep)],
-            r.q_far.at[h, k - 1],
-            r.q_s2.at[h, k - 1],
-            r.q_r2.at[h, k - 1],
-            z_peers[k - 1],
-        )
-
-    def head_three(h):
-        return send(r.q_sum.at[h, 1 - x], r.q_in.at[h], r.q_s3.at[h], r.q_r3.at[h], x_peer)
-
-    def head_to_two(h):
-        head_one(h).wait()
-
-        def body(i, carry):
-            r.q_near[h, i] = r.q_grads[h, i, y] + r.q_near[h, i]
-            return carry
-
-        lax.fori_loop(0, deep, body, 0)
-        for k in range(1, deep):
-            head_two(h, k).start()
-
-    def head_to_three(h):
-        for k in range(1, deep):
-            head_two(h, k).wait()
-        total = r.q_near[h, z].astype(full)
-        for k in range(1, deep):
-            total = total + r.q_far[h, k - 1].astype(full)
-        r.q_sum[h] = total
-        head_three(h).start()
+        held=(r.e_grads, r.e_near, r.e_next, r.e_far, r.e_last), out=r.e_sum, sent=r.e_s, got=r.e_r
+    )
+    along = dict(zip(range(3), ((3, 2, 1, 0), (2, 3, 1, 0), (1, 0, 3, 2))))
+
+    kit_q = types.SimpleNamespace(held=(r.q_grads, r.q_near, r.q_next, r.q_far), sent=r.q_s, got=r.q_r)
+    head_order = (2, 1, 0, 3)
+
+    def head_start(h):
+        stage(kit_q, h, head_order, 0)[0].start()
+
+    def head_meet(h):
+        return send(r.q_sum.at[h, 1 - x], r.q_in.at[h], r.q_s.at[h, 3], r.q_r.at[h, 3], x_peer)
+
+    def head_advance(h, n):
+        if n < 3:
+            advance(kit_q, h, head_order, n)
+            return
+        copy, own = stage(kit_q, h, head_order, 2)
+        copy.wait()
+        r.q_sum[h] = own[...].astype(full) + r.q_far[h].astype(full)
+        head_meet(h).start()
         r.out_q[h, x] = r.q_sum[h, x]
 
     def head_finish(h):
-        head_three(h).wait()
+        head_meet(h).wait()
         r.out_q[h, 1 - x] = r.q_in[h]
 
-    band = 4 * share
-    chunk = r.grads.shape[5]
+    def vec_copy(n):
+        return send(r.vec.at[n], r.vec_in.at[n], r.vec_s.at[n], r.vec_r.at[n], peer_on[3 - n])
+
+    def vec_advance(n):
+        vec_copy(n - 1).wait()
+        r.vec[n] = r.vec[n - 1] + r.vec_in[n - 1]
+        if n < 4:
+            vec_copy(n).start()
+
+    chunk = r.grads.shape[-1]
 
     def make_grad(c, left_t, right, lanes):
         part = dot_nn(left_t[...], right[:, lanes]).astype(low)
-        r.grads[c] = part.reshape(deep, 2, 2, share, chunk)
+        r.grads[c] = part.reshape(2, 2, 2, 2, share, chunk)
 
     plan = iter(schedule)
 
-    def vec_copy(n):
-        peer = x_peer if n == 0 else y_peer if n == 1 else z_peers[n - 2]
-        return send(r.vec.at[min(n, 2)], r.vec_in.at[n], r.vec_s.at[n], r.vec_r.at[n], peer)
-
-    def act_on(events):
-        for kind, c in events:
-            if kind == BEGIN:
-                stage_one(kit_a, c, flips[c]).start()
-            if kind == TURN:
-                to_two(kit_a, c, flips[c])
-            if kind == CLIMB:
-                to_three(kit_a, c, flips[c])
-            if kind == HEAD_CLIMB:
-                head_to_two(c)
-            if kind == HEAD_MEET:
-                head_to_three(c)
-            if kind == ENTS_TURN:
-                to_two(kit_e, 0, False)
-            if kind == ENTS_CLIMB:
-                to_three(kit_e, 0, False)
-            if kind == VEC_TURN:
-                vec_copy(0).wait()
-                r.vec[1] = r.vec[0] + r.vec_in[0]
-                vec_copy(1).start()
-            if kind == VEC_CLIMB:
-                vec_copy(1).wait()
-                r.vec[2] = r.vec[1] + r.vec_in[1]
-                for k in range(1, deep):
-                    vec_copy(1 + k).start()
-
     def tick():
-        act_on(next(plan))
+        for what, c, n in next(plan):
+            if what == CHUNK and n == 0:
+                stage(kit_a, c, along[orders[c]], 0)[0].start()
+            elif what == CHUNK:
+                advance(kit_a, c, along[orders[c]], n)
+            elif what == HEAD:
+                head_advance(c, n)
+            elif what == ENTS:
+                advance(kit_e, c, along[0], n)
+            else:
+                vec_advance(n)
 
     downs = hidden // chunk
     r.grad_t[...] = r.grad_low[...].T
@@ -593,10 +631,9 @@
     columns(width, fill_back)
     tick()
     r.first_t[...] = r.first[...].T
-    r.out_words[...] = r.final[pl.ds(pl.multiple_of(t * (half_words // 2), half_words // 2), half_words // 2), :]
-    r.out_ents[...] = r.final[
-        pl.ds(pl.multiple_of(half_words + t * (half_ents // 2), half_ents // 2), half_ents // 2), :
-    ]
+    flush(r.final.at[aligned(t, half_words // 2), :], r.to_out_words)
+    ents_share = pl.multiple_of(half_words + t * (half_ents // 2), half_ents // 2)
+    flush(r.final.at[pl.ds(ents_share, half_ents // 2), :], r.to_out_ents)
     for c in range(downs):
         make_grad(downs + c, r.first_t, r.grad_up, slice(c * chunk, (c + 1) * chunk))
         tick()
@@ -644,7 +681,10 @@
         def score_back(start):
             def body(i, carry):
                 here = pl.ds(pl.multiple_of(start + i * SOFT, SOFT), SOFT)
-                prob, grad_prob = r.prob[h, here, :], r.grad_prob[here, :]
+                factor = jnp.concatenate([r.factor[h, here, :]] * (words // 128), 1)
+                scaled = r.prob[h, here, of_words] * factor
+                prob = jnp.concatenate([scaled, r.prob[h, here, of_ents]], 1)
+                grad_prob = r.grad_prob[here, :]
                 inner = jnp.sum(prob * grad_prob, 1, keepdims=True)
                 r.grad_score[here, :] = (prob * (grad_prob - inner)).astype(low)
                 r.prob_low[here, :] = prob.astype(low)
@@ -682,15 +722,15 @@
         tick()
         keyval = slice(base + pair, base + 2 * pair)
         query = slice(base, base + pair)
-        of_words = dot_nn(r.words_t[...], r.grad_qkv[0:words, query])
-        of_ents = dot_nn(r.ents_t[...], r.grad_qkv[words:everyone, query])
-        of_keyval = dot_nn(r.words_t[...], r.grad_qkv[0:words, keyval])
-        of_keyval = of_keyval + dot_nn(r.ents_t[...], r.grad_qkv[words:everyone, keyval])
-        for n, part in enumerate([of_words, of_ents, of_keyval]):
-            r.q_grads[h, :, :, :, :, n * pair : (n + 1) * pair] = part.astype(low).reshape(
-                deep, 2, 2, share, pair
+        by_words = dot_nn(r.words_t[...], r.grad_qkv[0:words, query])
+        by_ents = dot_nn(r.ents_t[...], r.grad_qkv[words:everyone, query])
+        by_keyval = dot_nn(r.words_t[...], r.grad_qkv[0:words, keyval])
+        by_keyval = by_keyval + dot_nn(r.ents_t[...], r.grad_qkv[words:everyone, keyval])
+        for n, part in enumerate([by_words, by_ents, by_keyval]):
+            r.q_grads[h, :, :, :, :, :, n * pair : (n + 1) * pair] = part.astype(low).reshape(
+                2, 2, 2, 2, share, pair
             )
-        head_one(h).start()
+        head_start(h)
         sums = jnp.concatenate(
             [
                 row_sum(r.grad_qkv[0:words, base : base + pair].astype(full)),
@@ -751,14 +791,9 @@
     for k in range(owners - 1):
         slope_copy(k).start()
     looked_half = r.looked[own_ents, aligned(t, 128)]
-    r.ents_grad[...] = dot_tn(lin_low, looked_half).astype(low)
-
-    def ents_body(i, carry):
-        r.e_grads[0, i] = r.ents_grad[aligned(i, band), :].reshape(2, 2, share, 128)
-        return carry
-
-    lax.fori_loop(0, deep, ents_body, 0)
-    stage_one(kit_e, 0, False).start()
+    ents_grad = dot_tn(lin_low, looked_half).astype(low)
+    r.e_grads[0] = ents_grad.reshape(2, 2, 2, 2, share, 128)
+    stage(kit_e, 0, along[0], 0)[0].start()
     vec_copy(0).start()
     words_back_copy.wait()
     r.grad_words[...] = (
@@ -766,28 +801,35 @@
         + (r.input_part[x] + r.mail_in[1, aligned(x, quarter), :])
         + r.words_in[...].astype(full)
     )
+    flush(r.grad_words, r.to_grad_words)
     tick()
     for k in range(owners - 1):
         slope_copy(k).wait()
     ids_t = r.asked[...].reshape(slots, 128).astype(full).T
     r.ids_out[...] = ids_t[0:8, :].astype(jnp.int32)
     r.slopes_out[...] = r.slopes[...].reshape(slots, -1).astype(low)
+    flush(r.ids_out, r.to_ids_out)
+    flush(r.slopes_out, r.to_slopes_out)
     for c in range(2 * downs + 1):
-        finish(kit_a, c)
-    total = r.vec[2]
-    for k in range(1, deep):
-        vec_copy(1 + k).wait()
-        total = total + r.vec_in[1 + k]
-    r.vec_out[...] = total
+        finish(kit_a, c, along[orders[c]])
+        flush(r.out_a.at[c], r.to_out_a.at[c])
+    vec_advance(4)
+    total = r.vec[4]
+    flush(r.vec.at[4], r.to_vec_out)
     r.across_out[...] = pltpu.roll(total[0:8, :], width - flat * share, 1)[:, 0:128]
-    finish(kit_e, 0)
+    flush(r.across_out, r.to_across_out)
+    finish(kit_e, 0, along[0])
     ents_out = send(r.e_sum.at[0], r.e_in, r.pair_s.at[7], r.pair_r.at[7], core)
     ents_out.start()
     r.out_e[t] = r.e_sum[0]
     for h in range(heads):
         head_finish(h)
+        flush(r.out_q.at[h], r.to_out_q.at[h])
     ents_out.wait()
     r.out_e[1 - t] = r.e_in[...]
+    flush(r.out_e, r.to_out_e)
+    for copy in flushes:
+        copy.wait()
 
 
 def finish_kernel(names, *refs):
@@ -924,39 +966,39 @@
 
 SOFT = 32
 STEPS = 8
-BEGIN, TURN, CLIMB, HEAD_CLIMB, HEAD_MEET, ENTS_TURN, ENTS_CLIMB, VEC_TURN, VEC_CLIMB = range(9)
+CHUNK, HEAD, ENTS, VEC = range(4)
 SCHEDULE = (
-    ((BEGIN, 0),),
     (),
-    ((BEGIN, 2),),
+    ((CHUNK, 1, 0), (CHUNK, 0, 0),),
+    (),
+    ((CHUNK, 3, 0),),
+    (),
+    (),
+    ((CHUNK, 4, 0),),
+    (),
+    (),
+    ((CHUNK, 2, 0),),
+    ((CHUNK, 7, 0), (CHUNK, 0, 1),),
+    ((CHUNK, 1, 1), (CHUNK, 8, 0), (CHUNK, 6, 0), (CHUNK, 4, 1),),
+    ((CHUNK, 2, 1), (CHUNK, 3, 1),),
     (),
     (),
     (),
     (),
-    ((BEGIN, 5),),
-    (),
-    ((BEGIN, 7),),
-    ((TURN, 0),),
-    ((TURN, 7), (BEGIN, 8),),
-    ((BEGIN, 1), (TURN, 5),),
-    (),
-    ((CLIMB, 0),),
-    ((CLIMB, 7),),
+    ((CHUNK, 7, 1),),
+    ((CHUNK, 2, 2), (CHUNK, 5, 0),),
+    ((CHUNK, 0, 2), (CHUNK, 8, 1),),
     (),
     (),
-    ((BEGIN, 4),),
-    ((CLIMB, 5),),
-    ((TURN, 8),),
-    ((HEAD_CLIMB, 0),),
-    (),
-    (),
-    ((HEAD_CLIMB, 1),),
-    ((TURN, 2), (BEGIN, 3), (TURN, 4), (BEGIN, 6),),
-    ((CLIMB, 8), (HEAD_CLIMB, 2),),
-    ((CLIMB, 4), (TURN, 1), (TURN, 3), (CLIMB, 2),),
-    ((HEAD_MEET, 0), (TURN, 6), (CLIMB, 1), (ENTS_TURN, 0), (VEC_TURN, 0), (CLIMB, 3), (CLIMB, 6), (HEAD_MEET, 1), (HEAD_MEET, 2), (ENTS_CLIMB, 0), (VEC_CLIMB, 0),),
+    ((HEAD, 0, 1),),
+    ((CHUNK, 0, 3), (CHUNK, 3, 2),),
+    ((CHUNK, 2, 3),),
+    ((CHUNK, 4, 2), (CHUNK, 7, 2),),
+    ((CHUNK, 1, 2), (CHUNK, 6, 1), (HEAD, 0, 2), (CHUNK, 5, 1),),
+    ((HEAD, 1, 1), (CHUNK, 4, 3), (CHUNK, 7, 3), (HEAD, 2, 1),),
+    ((CHUNK, 1, 3), (HEAD, 1, 2), (CHUNK, 8, 2), (CHUNK, 5, 2), (ENTS, 0, 1), (HEAD, 0, 3), (HEAD, 2, 2), (CHUNK, 6, 2), (VEC, 0, 1), (ENTS, 0, 2), (CHUNK, 5, 3), (CHUNK, 8, 3), (VEC, 0, 2), (CHUNK, 3, 3), (HEAD, 1, 3), (CHUNK, 6, 3), (HEAD, 2, 3), (ENTS, 0, 3), (VEC, 0, 3),),
 )
-FLIPS = (False, False, True, False, False, False, True, True, False)
+ORDERS = (0, 2, 0, 1, 2, 0, 0, 1, 2)
 
 
 def fused_local(
@@ -992,7 +1034,6 @@
     table_rows, embed = entity_table.shape
     local_width, hidden = w_query.shape[2], w_up.shape[1]
     owners = lax.axis_size(("dp", "stream"))
-    deep = lax.axis_size("dp") // 2
     share = width // owners
     capacity = 2 * half_ents // owners
     side = local_width // 2
@@ -1001,19 +1042,17 @@
     chunks = 2 * (hidden // chunk) + 1
 
     operands = dict(
-        shard=entity_shard.reshape(1, half_ents),
-        row=entity_row.reshape(1, half_ents),
-        word_seg=word_segments,
-        ent_seg=entity_segments,
-        gain=norm_gain,
-        shift=norm_bias,
-        b_query=b_query,
-        b_value=b_value,
-        b_out=b_out,
-        b_up=b_up,
-        b_down=b_down,
-    )
-    streamed = dict(
+        hbm_shard=entity_shard.reshape(1, half_ents),
+        hbm_row=entity_row.reshape(1, half_ents),
+        hbm_word_seg=word_segments,
+        hbm_ent_seg=entity_segments,
+        hbm_gain=norm_gain,
+        hbm_shift=norm_bias,
+        hbm_b_query=b_query,
+        hbm_b_value=b_value,
+        hbm_b_out=b_out,
+        hbm_b_up=b_up,
+        hbm_b_down=b_down,
         hbm_words=word_states,
         hbm_cot_words=cot_words,
         hbm_cot_ents=cot_entities,
@@ -1026,20 +1065,38 @@
         hbm_down=w_down,
     )
     results = dict(
-        out_words=((half_words // 2, width), low),
-        out_ents=((half_ents // 2, width), low),
+        to_out_words=((half_words // 2, width), low),
+        to_out_ents=((half_ents // 2, width), low),
+        to_grad_words=((half_words // 2, width), full),
+        to_out_a=((chunks, share, chunk), full),
+        to_out_e=((2, share, 128), full),
+        to_out_q=((heads, 2, share, chunk), full),
+        to_vec_out=((16, width), full),
+        to_across_out=((8, 128), full),
+        to_ids_out=((8, owners * capacity), jnp.int32),
+        to_slopes_out=((owners * capacity, embed), low),
+    )
+    mail_rows = max(rows, words // 2 + ents)
+    dma = pltpu.SemaphoreType.DMA
+    scratch = dict(
+        shard=((1, half_ents), jnp.int32),
+        row=((1, half_ents), jnp.int32),
+        word_seg=(word_segments.shape, jnp.int32),
+        ent_seg=(entity_segments.shape, jnp.int32),
+        gain=(norm_gain.shape, full),
+        shift=(norm_bias.shape, full),
+        b_query=(b_query.shape, full),
+        b_value=(b_value.shape, full),
+        b_out=(b_out.shape, full),
+        b_up=(b_up.shape, full),
+        b_down=(b_down.shape, full),
         grad_words=((half_words // 2, width), full),
         out_a=((chunks, share, chunk), full),
         out_e=((2, share, 128), full),
         out_q=((heads, 2, share, chunk), full),
-        vec_out=((16, width), full),
         across_out=((8, 128), full),
         ids_out=((8, owners * capacity), jnp.int32),
         slopes_out=((owners * capacity, embed), low),
-    )
-    mail_rows = max(rows, words // 2 + ents)
-    dma = pltpu.SemaphoreType.DMA
-    scratch = dict(
         w_query=(w_query.shape, low),
         w_keyval=(w_keyval.shape, low),
         table=(entity_table.shape, low),
@@ -1070,6 +1127,7 @@
         key=((heads, everyone, HD), low),
         value=((heads, everyone, HD), low),
         prob=((heads, everyone, everyone), full),
+        factor=((heads, everyone, 128), full),
         heads_far=((rows, side), low),
         heads_near=((rows, side), low),
         heads_in=((rows, side), low),
@@ -1101,78 +1159,82 @@
         words_in=((half_words // 2, width), low),
         slope=((owners, capacity, embed), full),
         slopes=((owners, capacity, embed), full),
-        ents_grad=((width, 128), low),
         e_sum=((1, share, 128), full),
         e_in=((share, 128), full),
-        vec=((3, 16, width), full),
-        vec_in=((deep + 1, 16, width), full),
-        grads=((chunks, deep, 2, 2, share, chunk), low),
-        near=((chunks, deep, 2, share, chunk), low),
-        next=((chunks, deep, share, chunk), low),
-        far=((chunks, deep - 1, share, chunk), low),
-        e_grads=((1, deep, 2, 2, share, 128), low),
-        e_near=((1, deep, 2, share, 128), low),
-        e_next=((1, deep, share, 128), low),
-        e_far=((1, deep - 1, share, 128), low),
-        q_grads=((heads, deep, 2, 2, share, chunk), low),
-        q_near=((heads, deep, 2, share, chunk), low),
-        q_far=((heads, deep - 1, 2, share, chunk), low),
+        vec=((5, 16, width), full),
+        vec_in=((4, 16, width), full),
+        grads=((chunks, 2, 2, 2, 2, share, chunk), low),
+        near=((chunks, 2, 2, 2, share, chunk), low),
+        next=((chunks, 2, 2, share, chunk), low),
+        far=((chunks, 2, share, chunk), low),
+        last=((chunks, share, chunk), low),
+        e_grads=((1, 2, 2, 2, 2, share, 128), low),
+        e_near=((1, 2, 2, 2, share, 128), low),
+        e_next=((1, 2, 2, share, 128), low),
+        e_far=((1, 2, share, 128), low),
+        e_last=((1, share, 128), low),
+        q_grads=((heads, 2, 2, 2, 2, share, chunk), low),
+        q_near=((heads, 2, 2, 2, share, chunk), low),
+        q_next=((heads, 2, 2, share, chunk), low),
+        q_far=((heads, 2, share, chunk), low),
         q_sum=((heads, 2, share, chunk), full),
         q_in=((heads, share, chunk), full),
     )
     signals = dict(
-        load_s=(10,),
+        load_s=(len(operands),),
+        flush_s=(len(results) + chunks + heads,),
         ask_s=(owners - 1,),
         ask_r=(owners - 1,),
         answer_s=(owners - 1,),
         answer_r=(owners - 1,),
         slope_s=(owners - 1,),
         slope_r=(owners - 1,),
-        pair_s=(8,),
-        pair_r=(8,),
+        heads_s=(2,),
+        heads_r=(2,),
+        pair_s=(9,),
+        pair_r=(9,),
         strip_s=(3, width // 256),
         strip_r=(3, width // 256),
         swap_s=(2,),
         swap_r=(2,),
-        vec_s=(deep + 1,),
-        vec_r=(deep + 1,),
-    )
-    one, many = (1,), (1, deep - 1)
-    signals.update(e_s1=one, e_r1=one, e_s2=one, e_r2=one, e_s3=many, e_r3=many)
-    one, many = (chunks,), (chunks, deep - 1)
-    signals.update(a_s1=one, a_r1=one, a_s2=one, a_r2=one, a_s3=many, a_r3=many)
-    one, many = (heads,), (heads, deep - 1)
-    signals.update(q_s1=one, q_r1=one, q_s2=many, q_r2=many, q_s3=one, q_r3=one)
-    names = [*operands, *streamed, *results, *scratch, *signals]
-    kernel = functools.partial(layer_kernel, names, FLIPS, SCHEDULE)
+        vec_s=(4,),
+        vec_r=(4,),
+        a_s=(chunks, 4),
+        a_r=(chunks, 4),
+        e_s=(1, 4),
+        e_r=(1, 4),
+        q_s=(heads, 4),
+        q_r=(heads, 4),
+    )
+    names = [*operands, *results, *scratch, *signals]
+    kernel = functools.partial(layer_kernel, names, ORDERS, SCHEDULE)
     made = pl.pallas_call(
         kernel,
         name="layer",
         out_shape=[jax.ShapeDtypeStruct(*item) for item in results.values()],
-        in_specs=[pl.BlockSpec(memory_space=pltpu.VMEM)] * len(operands)
-        + [pl.BlockSpec(memory_space=pl.ANY)] * len(streamed),
-        out_specs=[pl.BlockSpec(memory_space=pltpu.VMEM)] * len(results),
+        in_specs=[pl.BlockSpec(memory_space=pl.ANY)] * len(operands),
+        out_specs=[pl.BlockSpec(memory_space=pl.ANY)] * len(results),
         scratch_shapes=[pltpu.VMEM(*item) for item in scratch.values()]
         + [dma(shape) for shape in signals.values()],
         compiler_params=pltpu.CompilerParams(
             collective_id=0, has_side_effects=True, vmem_limit_bytes=67_043_328
         ),
-    )(*operands.values(), *streamed.values())
+    )(*operands.values())
     got = types.SimpleNamespace(**dict(zip(results, made, strict=True)))
 
     given = dict(
         hbm_first=adam_first,
         hbm_second=adam_second,
-        hbm_ids=got.ids_out,
-        hbm_slopes=got.slopes_out,
-        hbm_a=got.out_a,
-        hbm_e=got.out_e,
-        hbm_q=got.out_q,
-        hbm_vec=got.vec_out,
-        hbm_across=got.across_out,
-        hbm_words=got.out_words,
-        hbm_ents=got.out_ents,
-        hbm_grad=got.grad_words,
+        hbm_ids=got.to_ids_out,
+        hbm_slopes=got.to_slopes_out,
+        hbm_a=got.to_out_a,
+        hbm_e=got.to_out_e,
+        hbm_q=got.to_out_q,
+        hbm_vec=got.to_vec_out,
+        hbm_across=got.to_across_out,
+        hbm_words=got.to_out_words,
+        hbm_ents=got.to_out_ents,
+        hbm_grad=got.to_grad_words,
     )
     final = dict(
         words_done=(1, half_words // 2, width),
@@ -1197,22 +1259,22 @@
     )
     room = dict(
         value_row=((1, local_width), full),
-        ids=(got.ids_out.shape, jnp.int32),
-        slopes=(got.slopes_out.shape, low),
+        ids=(got.to_ids_out.shape, jnp.int32),
+        slopes=(got.to_slopes_out.shape, low),
         addends=((owners * capacity, embed + 128), low),
-        out_e=(got.out_e.shape, full),
-        out_q=(got.out_q.shape, full),
-        vec=(got.vec_out.shape, full),
-        across=(got.across_out.shape, full),
+        out_e=(got.to_out_e.shape, full),
+        out_q=(got.to_out_q.shape, full),
+        vec=(got.to_vec_out.shape, full),
+        across=(got.to_across_out.shape, full),
         first=(adam_first.shape, full),
         second=(adam_first.shape, full),
         update=(adam_first.shape, full),
         out_part=((share, local_width), full),
         down_part=((share, hidden), full),
         up_part=((share, hidden), full),
-        words_part=(got.out_words.shape, low),
-        ents_part=(got.out_ents.shape, low),
-        grad_part=(got.grad_words.shape, full),
+        words_part=(got.to_out_words.shape, low),
+        ents_part=(got.to_out_ents.shape, low),
+        grad_part=(got.to_grad_words.shape, full),
         query_part=((4, share, local_width), full),
         keyval_part=((2, share, local_width), full),
     )
@@ -1650,7 +1712,7 @@
         P("dp", "stream", None),
         P("dp", "stream", None),
     )
-    fits = mesh.shape["stream"] == 2 and mesh.shape["tensor"] == 2 and mesh.shape["dp"] % 2 == 0
+    fits = mesh.shape["stream"] == 2 and mesh.shape["tensor"] == 2 and mesh.shape["dp"] == 8
 
     def local(*blocks):
         width, owners = blocks[0].shape[2], mesh.shape["dp"] * mesh.shape["stream"]

time: 135 us -> 121 us (0.90)
  Pallas kernels: 133 us -> 120 us
    pallas_call x1, Pallas kernels: 123 us -> 110 us  [fused_local(): pl.pallas_call(kernel, name='layer', out_shape=[jax.ShapeDtypeStruct(*ite...]
where the time goes in v4:
time: 121 us
  Pallas kernels  120 us (99%)
    pallas_call x1, Pallas kernels, fused_local(): pl.pallas_call(kernel, name='layer', out_shape=[jax.ShapeDtypeStruct(*ite...  110 us
    pallas_call x1, Pallas kernels, fused_local(): pl.pallas_call(functools.partial(finish_kernel, [*given, *final, *room, *...  10.4 us

profile of v4, /device:TPU:0, one launch (start us, length us, event | category | flops | bytes accessed | tf_op | source)
XLA Modules:
  0.0 121.2 jit_solution(15372030551886161830)
XLA Ops:
  0.7 110.0 %layer.1 = (bf16[128,768]{1,0:T(8,128)(2,1)}, bf16[32,768]{1,0:T(8,128)(2,1)}, f32[128,768]{1,0:T(8,128)}, f32[9,48,384]{2,1,0:T(8,128)}, f32[2,48,128]{2,1,0:T(...) custom-call(s32[1,64]{1,0:T(1,128)} %bitcast.5, ...), custom_call_target="tpu_custom_call" | custom-call | tf_op jit(solution)/shard_map/layer/pallas_call | solution.py:1211
  110.7 10.4 %finish.1 = (bf16[1,128,768]{2,1,0:T(8,128)(2,1)}, bf16[1,32,768]{2,1,0:T(8,128)(2,1)}, f32[1,128,768]{2,1,0:T(8,128)}, f32[48,256]{1,0:T(8,128)}, f32[3,48]{1,0...) custom-call(f32[4096,256]{1,0:T(8,128)} %refs_0_.1, ...), custom_call_target="tpu_custom_call" | custom-call | tf_op jit(solution)/shard_map/finish/pallas_call | solution.py:1285

commit v5 on v4

--- a/solution.py
+++ b/solution.py
@@ -100,7 +100,7 @@
     return pl.ds(pl.multiple_of(index * step, step), step)
 
 
-def layer_kernel(names, orders, schedule, *refs):
+def layer_kernel(names, orders, ents_order, vec_order, schedule, *refs):
     r = types.SimpleNamespace(**dict(zip(names, refs, strict=True)))
     low, full = jnp.bfloat16, jnp.float32
     dp, x, t = lax.axis_index("dp"), lax.axis_index("stream"), lax.axis_index("tensor")
@@ -277,11 +277,6 @@
         equal = own_seg[:, 0:1].astype(jnp.int32) == segments
         r.mask[i * 128 : (i + 1) * 128, :] = jnp.where(equal, 0.0, masked_score).astype(low)
 
-    words_copy.wait()
-    far_half = r.x_all.at[aligned(2 * (1 - x) + t, half), :]
-    relay = send(far_half, far_half, r.pair_s.at[8], r.pair_r.at[8], core)
-    relay.start()
-
     for k in range(owners - 1):
         ask_copy(k).wait()
     ids = r.asked[...].reshape(slots, 128)
@@ -294,12 +289,16 @@
         return found + dot_nn(jnp.concatenate(ones, 1).astype(low), r.table[aligned(j, piece), :])
 
     found = jnp.zeros((slots, r.table.shape[1]), full)
-    found = lax.fori_loop(0, r.table.shape[0] // piece, pick_body, found).astype(low)
+    found = lax.fori_loop(0, r.table.shape[0] // piece, pick_body, found, unroll=True).astype(low)
     r.found[...] = found.reshape(r.found.shape)
     r.answer[flat] = r.found[dp]
     for k in range(owners - 1):
         answer_copy(k).start()
 
+    words_copy.wait()
+    far_half = r.x_all.at[aligned(2 * (1 - x) + t, half), :]
+    relay = send(far_half, far_half, r.pair_s.at[8], r.pair_r.at[8], core)
+    relay.start()
     relay.wait()
     project(pl.multiple_of((1 - x) * half_words, half_words), half_words, r.cat_words, r.bias_words)
 
@@ -313,9 +312,6 @@
     for h in range(heads):
         query = r.qkv[of_words, h * 4 * HD : h * 4 * HD + HD]
         r.prob[h, of_words, of_words] = dot_nt(query, r.key[h, of_words, :])
-
-    def mass_lanes(which, h):
-        return pl.ds(pl.multiple_of((which * heads + h) * 128, 128), 128)
 
     def soften_words(which):
         def body(i, carry):
@@ -328,7 +324,7 @@
                 r.prob[h, here, of_words] = power
                 r.factor[h, here, :] = jnp.broadcast_to(peak, (SOFT, 128))
                 mass = jnp.broadcast_to(jnp.sum(power, 1, keepdims=True), (SOFT, 128))
-                r.mail_out[1, aligned(i, SOFT), mass_lanes(which, h)] = mass
+                r.mass[h, here, :] = mass
             return carry
 
         lax.fori_loop(0, half_words // SOFT, body, 0)
@@ -368,7 +364,7 @@
             power = jnp.exp(score - jnp.max(score, 1, keepdims=True))
             r.prob[h, here, :] = power * (1.0 / jnp.sum(power, 1, keepdims=True))
 
-    def complete_words(which, here):
+    def complete_words(here):
         bias = r.mask[here, of_ents].astype(full)
         for h in range(heads):
             score = r.prob[h, here, of_ents] + bias
@@ -377,8 +373,7 @@
             top = jnp.maximum(peak, best)
             power, shrink = jnp.exp(score - top), jnp.exp(peak - top)
             added = jnp.broadcast_to(jnp.sum(power, 1, keepdims=True), (half_words, 128))
-            mass = r.mail_out[1, 0:half_words, mass_lanes(which, h)]
-            share_of = 1.0 / (mass * shrink + added)
+            share_of = 1.0 / (r.mass[h, here, :] * shrink + added)
             r.prob[h, here, of_ents] = power * share_of
             r.factor[h, here, :] = shrink * share_of
 
@@ -387,7 +382,7 @@
         for h in range(heads):
             query = r.qkv[here, h * 4 * HD + HD : h * 4 * HD + 2 * HD]
             r.prob[h, here, of_ents] = dot_nt(query, r.key[h, of_ents, :])
-        complete_words(which, here)
+        complete_words(here)
         for h in range(heads):
             out = r.grad_prob[here, h * 128 : h * 128 + HD] * r.factor[h, here, 0:HD]
             out = out + dot_nn(r.prob[h, here, of_ents].astype(low), r.value[h, of_ents, :])
@@ -438,6 +433,9 @@
             r.mail_out.at[part], r.mail_in.at[part], r.strip_s.at[turn, j], r.strip_r.at[turn, j], core
         )
 
+    def arrived(which, here):
+        return r.mail_out[which, here, :].astype(full) + r.mail_in[which, here, :].astype(full)
+
     def wait_strips(which, turn):
         for j in range(width // wide):
             strip(which, turn, j).wait()
@@ -457,7 +455,7 @@
         lax.fori_loop(0, count // wide, body, 0)
 
     def fill_attn(lanes, j):
-        r.mail_out[0, 0:rows, lanes] = dot_nn(r.heads_all[...], r.w_out[:, lanes])
+        r.mail_out[0, 0:rows, lanes] = dot_nn(r.heads_all[...], r.w_out[:, lanes]).astype(low)
         strip(0, 0, j).start()
 
     loaded(r.w_out)
@@ -472,7 +470,7 @@
         lax.fori_loop(0, blocks, step, 0)
 
     def first_norm(here):
-        attn = r.mail_out[0, here, :] + r.mail_in[0, here, :] + r.b_out[...].reshape(1, -1)
+        attn = arrived(0, here) + r.b_out[...].reshape(1, -1)
         normed, scale = normalize(r.x_own[here, :] + attn)
         r.normed[here, :] = normed
         r.scale[here, :] = jnp.broadcast_to(scale, (block, 128))
@@ -490,7 +488,7 @@
     columns(hidden, fill_up)
 
     def fill_down(lanes, j):
-        r.mail_out[1, 0:rows, lanes] = dot_nn(r.act[...], r.w_down[:, lanes])
+        r.mail_out[1, 0:rows, lanes] = dot_nn(r.act[...], r.w_down[:, lanes]).astype(low)
         strip(1, 1, j).start()
 
     loaded(r.w_down)
@@ -500,7 +498,7 @@
     vec = r.vec.at[0]
 
     def second_norm(here):
-        ffn = r.mail_out[1, here, :] + r.mail_in[1, here, :] + r.b_down[...].reshape(1, -1)
+        ffn = arrived(1, here) + r.b_down[...].reshape(1, -1)
         entering = r.normed[here, :] * r.gain[1:2, :] + r.shift[1:2, :]
         normed, scale = normalize(entering + ffn)
         r.final[here, :] = (normed * r.gain[2:3, :] + r.shift[2:3, :]).astype(low)
@@ -561,7 +559,7 @@
         stage(kit_q, h, head_order, 0)[0].start()
 
     def head_meet(h):
-        return send(r.q_sum.at[h, 1 - x], r.q_in.at[h], r.q_s.at[h, 3], r.q_r.at[h, 3], x_peer)
+        return send(r.q_away.at[h], r.q_in.at[h], r.q_s.at[h, 3], r.q_r.at[h, 3], x_peer)
 
     def head_advance(h, n):
         if n < 3:
@@ -569,16 +567,18 @@
             return
         copy, own = stage(kit_q, h, head_order, 2)
         copy.wait()
-        r.q_sum[h] = own[...].astype(full) + r.q_far[h].astype(full)
+        away = own[1 - x].astype(full) + r.q_far[h, 1 - x].astype(full)
+        r.q_away[h] = away.astype(low)
         head_meet(h).start()
-        r.out_q[h, x] = r.q_sum[h, x]
+        r.out_q[h, x] = own[x].astype(full) + r.q_far[h, x].astype(full)
 
     def head_finish(h):
         head_meet(h).wait()
-        r.out_q[h, 1 - x] = r.q_in[h]
+        r.out_q[h, 1 - x] = r.q_in[h].astype(full)
 
     def vec_copy(n):
-        return send(r.vec.at[n], r.vec_in.at[n], r.vec_s.at[n], r.vec_r.at[n], peer_on[3 - n])
+        peer = peer_on[along[vec_order][n]]
+        return send(r.vec.at[n], r.vec_in.at[n], r.vec_s.at[n], r.vec_r.at[n], peer)
 
     def vec_advance(n):
         vec_copy(n - 1).wait()
@@ -603,7 +603,9 @@
             elif what == HEAD:
                 head_advance(c, n)
             elif what == ENTS:
-                advance(kit_e, c, along[0], n)
+                advance(kit_e, c, along[ents_order], n)
+            elif what == WORDS:
+                words_back_copy.start()
             else:
                 vec_advance(n)
 
@@ -625,7 +627,7 @@
     tick()
 
     def fill_back(lanes, j):
-        r.mail_out[0, 0:rows, lanes] = dot_nt(r.grad_up[...], r.w_up[lanes, :])
+        r.mail_out[0, 0:rows, lanes] = dot_nt(r.grad_up[...], r.w_up[lanes, :]).astype(low)
         strip(0, 2, j).start()
 
     columns(width, fill_back)
@@ -640,7 +642,7 @@
     wait_strips(0, 2)
 
     def first_back(here):
-        grad = r.grad_second[here, :] + r.mail_out[0, here, :] + r.mail_in[0, here, :]
+        grad = r.grad_second[here, :] + arrived(0, here)
         normed = r.normed[here, :]
         vec[1:2, :] += row_sum(grad * normed)
         vec[4:5, :] += row_sum(grad)
@@ -678,9 +680,9 @@
     for h in range(heads):
         base = h * 4 * HD
 
-        def score_back(start):
+        def score_back(start, size):
             def body(i, carry):
-                here = pl.ds(pl.multiple_of(start + i * SOFT, SOFT), SOFT)
+                here = pl.ds(pl.multiple_of(start + i * size, size), size)
                 factor = jnp.concatenate([r.factor[h, here, :]] * (words // 128), 1)
                 scaled = r.prob[h, here, of_words] * factor
                 prob = jnp.concatenate([scaled, r.prob[h, here, of_ents]], 1)
@@ -700,8 +702,8 @@
                     copy.wait()
             for here, _ in both_kinds(which):
                 r.grad_prob[here, :] = dot_nt(r.back_heads[here, h * HD : (h + 1) * HD], r.value[h])
-            lax.fori_loop(0, half_words // SOFT, score_back(which * half_words), 0)
-            lax.fori_loop(0, half_ents // SOFT, score_back(words + which * half_ents), 0)
+            lax.fori_loop(0, half_words // SOFT, score_back(which * half_words, SOFT), 0)
+            score_back(words + which * half_ents, half_ents)(0, 0)
         queries = jnp.concatenate(
             [
                 dot_nn(r.grad_score[:, :words], r.key[h, 0:words, :]),
@@ -749,14 +751,14 @@
         return dot_nt(r.grad_qkv[place, :], weight[...])
 
     ents_part = input_grad(slice(words, everyone), r.cat_ents)
-    r.mail_out[1, words // 2 :, :] = ents_part
+    r.mail_out[1, words // 2 :, :] = ents_part.astype(low)
     ents_swap = swap(1, 0, words // 2, 2 * half_ents)
     ents_swap.start()
     tick()
     for n in range(2):
         r.mail_out[1, n * quarter : (n + 1) * quarter, :] = input_grad(
             aligned(2 * n + 1 - t, quarter), r.cat_words
-        )
+        ).astype(low)
     words_swap = swap(1, 1, 0, words // 2)
     words_swap.start()
     for n in range(2):
@@ -766,19 +768,18 @@
     ents_place = pl.multiple_of(words // 2 + (1 - x) * half_ents, half_ents)
     ents_far = pl.ds(ents_place, half_ents)
     ents_near = pl.ds(pl.multiple_of(words // 2 + x * half_ents, half_ents), half_ents)
-    r.ents_back[...] = (r.mail_out[1, ents_far, :] + r.mail_in[1, ents_far, :]).astype(low)
+    r.ents_back[...] = arrived(1, ents_far).astype(low)
     ents_copy = send(r.ents_back, r.ents_in, r.pair_s.at[5], r.pair_r.at[5], x_peer)
     ents_copy.start()
     tick()
     words_swap.wait()
     far_place = aligned(1 - x, quarter)
-    r.words_back[...] = (r.input_part[1 - x] + r.mail_in[1, far_place, :]).astype(low)
+    r.words_back[...] = (r.input_part[1 - x] + r.mail_in[1, far_place, :].astype(full)).astype(low)
     words_back_copy = send(r.words_back, r.words_in, r.pair_s.at[6], r.pair_r.at[6], x_peer)
-    words_back_copy.start()
     tick()
     ents_copy.wait()
 
-    grad = r.grad_first[half_words:rows, :] + (r.mail_out[1, ents_near, :] + r.mail_in[1, ents_near, :])
+    grad = r.grad_first[half_words:rows, :] + arrived(1, ents_near)
     grad = grad + r.ents_in[...].astype(full)
     own_ents = aligned(x, half_ents)
     normed, scale = normalize(r.ent_lin[own_ents, :])
@@ -793,15 +794,8 @@
     looked_half = r.looked[own_ents, aligned(t, 128)]
     ents_grad = dot_tn(lin_low, looked_half).astype(low)
     r.e_grads[0] = ents_grad.reshape(2, 2, 2, 2, share, 128)
-    stage(kit_e, 0, along[0], 0)[0].start()
+    stage(kit_e, 0, along[ents_order], 0)[0].start()
     vec_copy(0).start()
-    words_back_copy.wait()
-    r.grad_words[...] = (
-        r.grad_first[aligned(t, quarter), :]
-        + (r.input_part[x] + r.mail_in[1, aligned(x, quarter), :])
-        + r.words_in[...].astype(full)
-    )
-    flush(r.grad_words, r.to_grad_words)
     tick()
     for k in range(owners - 1):
         slope_copy(k).wait()
@@ -810,6 +804,13 @@
     r.slopes_out[...] = r.slopes[...].reshape(slots, -1).astype(low)
     flush(r.ids_out, r.to_ids_out)
     flush(r.slopes_out, r.to_slopes_out)
+    words_back_copy.wait()
+    r.grad_words[...] = (
+        r.grad_first[aligned(t, quarter), :]
+        + (r.input_part[x] + r.mail_in[1, aligned(x, quarter), :].astype(full))
+        + r.words_in[...].astype(full)
+    )
+    flush(r.grad_words, r.to_grad_words)
     for c in range(2 * downs + 1):
         finish(kit_a, c, along[orders[c]])
         flush(r.out_a.at[c], r.to_out_a.at[c])
@@ -818,7 +819,7 @@
     flush(r.vec.at[4], r.to_vec_out)
     r.across_out[...] = pltpu.roll(total[0:8, :], width - flat * share, 1)[:, 0:128]
     flush(r.across_out, r.to_across_out)
-    finish(kit_e, 0, along[0])
+    finish(kit_e, 0, along[ents_order])
     ents_out = send(r.e_sum.at[0], r.e_in, r.pair_s.at[7], r.pair_r.at[7], core)
     ents_out.start()
     r.out_e[t] = r.e_sum[0]
@@ -964,41 +965,43 @@
         copy.wait()
 
 
-SOFT = 32
+SOFT = 256
 STEPS = 8
-CHUNK, HEAD, ENTS, VEC = range(4)
+CHUNK, HEAD, ENTS, VEC, WORDS = range(5)
 SCHEDULE = (
-    (),
-    ((CHUNK, 1, 0), (CHUNK, 0, 0),),
-    (),
-    ((CHUNK, 3, 0),),
-    (),
-    (),
-    ((CHUNK, 4, 0),),
-    (),
-    (),
+    ((CHUNK, 0, 0),),
+    ((CHUNK, 1, 0),),
     ((CHUNK, 2, 0),),
-    ((CHUNK, 7, 0), (CHUNK, 0, 1),),
-    ((CHUNK, 1, 1), (CHUNK, 8, 0), (CHUNK, 6, 0), (CHUNK, 4, 1),),
-    ((CHUNK, 2, 1), (CHUNK, 3, 1),),
     (),
     (),
     (),
     (),
-    ((CHUNK, 7, 1),),
-    ((CHUNK, 2, 2), (CHUNK, 5, 0),),
-    ((CHUNK, 0, 2), (CHUNK, 8, 1),),
+    ((CHUNK, 3, 0),),
+    (),
+    ((CHUNK, 7, 0),),
+    (),
+    ((CHUNK, 0, 1), (CHUNK, 4, 0), (CHUNK, 6, 0),),
+    ((CHUNK, 1, 1),),
     (),
     (),
-    ((HEAD, 0, 1),),
-    ((CHUNK, 0, 3), (CHUNK, 3, 2),),
-    ((CHUNK, 2, 3),),
-    ((CHUNK, 4, 2), (CHUNK, 7, 2),),
-    ((CHUNK, 1, 2), (CHUNK, 6, 1), (HEAD, 0, 2), (CHUNK, 5, 1),),
-    ((HEAD, 1, 1), (CHUNK, 4, 3), (CHUNK, 7, 3), (HEAD, 2, 1),),
-    ((CHUNK, 1, 3), (HEAD, 1, 2), (CHUNK, 8, 2), (CHUNK, 5, 2), (ENTS, 0, 1), (HEAD, 0, 3), (HEAD, 2, 2), (CHUNK, 6, 2), (VEC, 0, 1), (ENTS, 0, 2), (CHUNK, 5, 3), (CHUNK, 8, 3), (VEC, 0, 2), (CHUNK, 3, 3), (HEAD, 1, 3), (CHUNK, 6, 3), (HEAD, 2, 3), (ENTS, 0, 3), (VEC, 0, 3),),
+    (),
+    ((CHUNK, 2, 1),),
+    ((CHUNK, 3, 1), (CHUNK, 8, 0), (CHUNK, 5, 0),),
+    ((CHUNK, 7, 1),),
+    ((CHUNK, 2, 2), (HEAD, 0, 1),),
+    ((CHUNK, 6, 1),),
+    (),
+    (),
+    ((HEAD, 1, 1),),
+    ((HEAD, 0, 2),),
+    ((CHUNK, 8, 1), (CHUNK, 0, 2), (CHUNK, 1, 2),),
+    ((CHUNK, 4, 1), (CHUNK, 3, 2), (CHUNK, 2, 3), (HEAD, 2, 1), (HEAD, 1, 2), (CHUNK, 5, 1), (CHUNK, 0, 3), (CHUNK, 6, 2),),
+    ((CHUNK, 8, 2), (CHUNK, 1, 3),),
+    ((WORDS, 0, 0), (CHUNK, 4, 2), (CHUNK, 3, 3), (HEAD, 2, 2), (CHUNK, 5, 2), (CHUNK, 8, 3), (ENTS, 0, 1), (VEC, 0, 1), (CHUNK, 7, 2), (CHUNK, 6, 3), (ENTS, 0, 2), (CHUNK, 5, 3), (VEC, 0, 2), (CHUNK, 4, 3), (CHUNK, 7, 3), (HEAD, 0, 3), (HEAD, 1, 3), (HEAD, 2, 3), (ENTS, 0, 3), (VEC, 0, 3),),
 )
-ORDERS = (0, 2, 0, 1, 2, 0, 0, 1, 2)
+ORDERS = (2, 0, 1, 2, 0, 0, 2, 1, 0)
+VEC_ORDER = 1
+ENTS_ORDER = 0
 
 
 def fused_local(
@@ -1128,12 +1131,13 @@
         value=((heads, everyone, HD), low),
         prob=((heads, everyone, everyone), full),
         factor=((heads, everyone, 128), full),
+        mass=((heads, words, 128), full),
         heads_far=((rows, side), low),
         heads_near=((rows, side), low),
         heads_in=((rows, side), low),
         heads_all=((rows, 2 * side), low),
-        mail_out=((2, mail_rows, width), full),
-        mail_in=((2, mail_rows, width), full),
+        mail_out=((2, mail_rows, width), low),
+        mail_in=((2, mail_rows, width), low),
         normed=((rows, width), full),
         scale=((rows, 128), full),
         first=((rows, width), low),
@@ -1177,8 +1181,8 @@
         q_near=((heads, 2, 2, 2, share, chunk), low),
         q_next=((heads, 2, 2, share, chunk), low),
         q_far=((heads, 2, share, chunk), low),
-        q_sum=((heads, 2, share, chunk), full),
-        q_in=((heads, share, chunk), full),
+        q_away=((heads, share, chunk), low),
+        q_in=((heads, share, chunk), low),
     )
     signals = dict(
         load_s=(len(operands),),
@@ -1207,7 +1211,7 @@
         q_r=(heads, 4),
     )
     names = [*operands, *results, *scratch, *signals]
-    kernel = functools.partial(layer_kernel, names, ORDERS, SCHEDULE)
+    kernel = functools.partial(layer_kernel, names, ORDERS, ENTS_ORDER, VEC_ORDER, SCHEDULE)
     made = pl.pallas_call(
         kernel,
         name="layer",

time: 121 us -> 118 us (0.975)
  Pallas kernels: 120 us -> 117 us
    pallas_call x1, Pallas kernels: 110 us -> 106 us  [fused_local(): pl.pallas_call(kernel, name='layer', out_shape=[jax.ShapeDtypeStruct(*ite...]
where the time goes in v5:
time: 118 us; the launch traced here: 117 us
  Pallas kernels  117 us (99%)
    pallas_call x1, Pallas kernels, fused_local(): pl.pallas_call(kernel, name='layer', out_shape=[jax.ShapeDtypeStruct(*ite...  106 us
    pallas_call x1, Pallas kernels, fused_local(): pl.pallas_call(functools.partial(finish_kernel, [*given, *final, *room, *...  10.4 us

profile of v5, /device:TPU:0, one launch (start us, length us, event | category | flops | bytes accessed | tf_op | source)
XLA Modules:
  0.0 117.4 jit_solution(12142222048957455915)
XLA Ops:
  0.7 106.2 %layer.1 = (bf16[128,768]{1,0:T(8,128)(2,1)}, bf16[32,768]{1,0:T(8,128)(2,1)}, f32[128,768]{1,0:T(8,128)}, f32[9,48,384]{2,1,0:T(8,128)}, f32[2,48,128]{2,1,0:T(...) custom-call(s32[1,64]{1,0:T(1,128)} %bitcast.5, ...), custom_call_target="tpu_custom_call" | custom-call | tf_op jit(solution)/shard_map/layer/pallas_call | solution.py:1215
  106.9 10.4 %finish.1 = (bf16[1,128,768]{2,1,0:T(8,128)(2,1)}, bf16[1,32,768]{2,1,0:T(8,128)(2,1)}, f32[1,128,768]{2,1,0:T(8,128)}, f32[48,256]{1,0:T(8,128)}, f32[3,48]{1,0...) custom-call(f32[4096,256]{1,0:T(8,128)} %refs_0_.1, ...), custom_call_target="tpu_custom_call" | custom-call | tf_op jit(solution)/shard_map/finish/pallas_call | solution.py:1289

commit v6 on v5

--- a/solution.py
+++ b/solution.py
@@ -267,7 +267,7 @@
             r.qkv[pl.ds(start, count), lanes] = (total * scaling).astype(low)
             return carry
 
-        lax.fori_loop(0, heads, body, 0)
+        lax.fori_loop(0, heads, body, 0, unroll=True)
 
     project(pl.multiple_of(x * half_words, half_words), half_words, r.cat_words, r.bias_words)
 
@@ -452,7 +452,7 @@
             fill(aligned(j, wide), j)
             return carry
 
-        lax.fori_loop(0, count // wide, body, 0)
+        lax.fori_loop(0, count // wide, body, 0, unroll=True)
 
     def fill_attn(lanes, j):
         r.mail_out[0, 0:rows, lanes] = dot_nn(r.heads_all[...], r.w_out[:, lanes]).astype(low)
@@ -462,18 +462,20 @@
     columns(width, fill_attn)
     wait_strips(0, 0)
 
+    tall = rows // 1
+
     def over_rows(body):
         def step(i, carry):
-            body(aligned(i, block))
+            body(aligned(i, tall))
             return carry
 
-        lax.fori_loop(0, blocks, step, 0)
+        lax.fori_loop(0, rows // tall, step, 0)
 
     def first_norm(here):
         attn = arrived(0, here) + r.b_out[...].reshape(1, -1)
         normed, scale = normalize(r.x_own[here, :] + attn)
         r.normed[here, :] = normed
-        r.scale[here, :] = jnp.broadcast_to(scale, (block, 128))
+        r.scale[here, :] = jnp.broadcast_to(scale, (tall, 128))
         r.first[here, :] = (normed * r.gain[1:2, :] + r.shift[1:2, :]).astype(low)
 
     over_rows(first_norm)
@@ -971,36 +973,36 @@
 SCHEDULE = (
     ((CHUNK, 0, 0),),
     ((CHUNK, 1, 0),),
+    (),
     ((CHUNK, 2, 0),),
     (),
     (),
     (),
     (),
-    ((CHUNK, 3, 0),),
-    (),
-    ((CHUNK, 7, 0),),
-    (),
-    ((CHUNK, 0, 1), (CHUNK, 4, 0), (CHUNK, 6, 0),),
-    ((CHUNK, 1, 1),),
+    ((CHUNK, 5, 0),),
     (),
     (),
+    ((CHUNK, 4, 0), (CHUNK, 6, 0), (CHUNK, 0, 1),),
     (),
     ((CHUNK, 2, 1),),
-    ((CHUNK, 3, 1), (CHUNK, 8, 0), (CHUNK, 5, 0),),
-    ((CHUNK, 7, 1),),
-    ((CHUNK, 2, 2), (HEAD, 0, 1),),
+    ((CHUNK, 5, 1),),
+    (),
+    ((CHUNK, 1, 1), (CHUNK, 0, 2),),
     ((CHUNK, 6, 1),),
     (),
+    ((CHUNK, 8, 0), (CHUNK, 7, 0),),
+    ((CHUNK, 5, 2),),
+    ((HEAD, 0, 1),),
+    ((CHUNK, 4, 1), (CHUNK, 0, 3),),
     (),
-    ((HEAD, 1, 1),),
-    ((HEAD, 0, 2),),
-    ((CHUNK, 8, 1), (CHUNK, 0, 2), (CHUNK, 1, 2),),
-    ((CHUNK, 4, 1), (CHUNK, 3, 2), (CHUNK, 2, 3), (HEAD, 2, 1), (HEAD, 1, 2), (CHUNK, 5, 1), (CHUNK, 0, 3), (CHUNK, 6, 2),),
-    ((CHUNK, 8, 2), (CHUNK, 1, 3),),
-    ((WORDS, 0, 0), (CHUNK, 4, 2), (CHUNK, 3, 3), (HEAD, 2, 2), (CHUNK, 5, 2), (CHUNK, 8, 3), (ENTS, 0, 1), (VEC, 0, 1), (CHUNK, 7, 2), (CHUNK, 6, 3), (ENTS, 0, 2), (CHUNK, 5, 3), (VEC, 0, 2), (CHUNK, 4, 3), (CHUNK, 7, 3), (HEAD, 0, 3), (HEAD, 1, 3), (HEAD, 2, 3), (ENTS, 0, 3), (VEC, 0, 3),),
+    ((CHUNK, 1, 2),),
+    (),
+    ((CHUNK, 5, 3), (CHUNK, 3, 0), (HEAD, 1, 1), (CHUNK, 8, 1), (CHUNK, 2, 2), (HEAD, 0, 2), (CHUNK, 4, 2), (CHUNK, 1, 3),),
+    ((HEAD, 1, 2),),
+    ((CHUNK, 7, 1), (HEAD, 2, 1), (VEC, 0, 1), (CHUNK, 3, 1), (CHUNK, 6, 2), (CHUNK, 8, 2), (WORDS, 0, 0), (CHUNK, 4, 3), (CHUNK, 7, 2), (ENTS, 0, 1), (CHUNK, 2, 3), (HEAD, 2, 2), (CHUNK, 3, 2), (VEC, 0, 2), (ENTS, 0, 2), (CHUNK, 6, 3), (CHUNK, 7, 3), (CHUNK, 8, 3), (HEAD, 1, 3), (VEC, 0, 3), (ENTS, 0, 3), (CHUNK, 3, 3), (HEAD, 0, 3), (HEAD, 2, 3),),
 )
-ORDERS = (2, 0, 1, 2, 0, 0, 2, 1, 0)
-VEC_ORDER = 1
+ORDERS = (0, 1, 2, 0, 0, 1, 2, 0, 0)
+VEC_ORDER = 2
 ENTS_ORDER = 0
 
 

time: 118 us -> 114 us (0.966)
  Pallas kernels: 117 us -> 113 us
    pallas_call x1, Pallas kernels: 106 us -> 102 us  [fused_local(): pl.pallas_call(kernel, name='layer', out_shape=[jax.ShapeDtypeStruct(*ite...]
where the time goes in v6:
time: 114 us; the launch traced here: 113 us
  Pallas kernels  113 us (99%)
    pallas_call x1, Pallas kernels, fused_local(): pl.pallas_call(kernel, name='layer', out_shape=[jax.ShapeDtypeStruct(*ite...  102 us
    pallas_call x1, Pallas kernels, fused_local(): pl.pallas_call(functools.partial(finish_kernel, [*given, *final, *room, *...  10.4 us

profile of v6, /device:TPU:0, one launch (start us, length us, event | category | flops | bytes accessed | tf_op | source)
XLA Modules:
  0.0 113.4 jit_solution(6564661859052065107)
XLA Ops:
  0.7 102.2 %layer.1 = (bf16[128,768]{1,0:T(8,128)(2,1)}, bf16[32,768]{1,0:T(8,128)(2,1)}, f32[128,768]{1,0:T(8,128)}, f32[9,48,384]{2,1,0:T(8,128)}, f32[2,48,128]{2,1,0:T(...) custom-call(s32[1,64]{1,0:T(1,128)} %bitcast.5, ...), custom_call_target="tpu_custom_call" | custom-call | tf_op jit(solution)/shard_map/layer/pallas_call | solution.py:1217
  102.9 10.4 %finish.1 = (bf16[1,128,768]{2,1,0:T(8,128)(2,1)}, bf16[1,32,768]{2,1,0:T(8,128)(2,1)}, f32[1,128,768]{2,1,0:T(8,128)}, f32[48,256]{1,0:T(8,128)}, f32[3,48]{1,0...) custom-call(f32[4096,256]{1,0:T(8,128)} %refs_0_.1, ...), custom_call_target="tpu_custom_call" | custom-call | tf_op jit(solution)/shard_map/finish/pallas_call | solution.py:1291

commit v7 on v6

--- a/solution.py
+++ b/solution.py
@@ -484,7 +484,8 @@
         up = dot_nn(r.first[...], r.w_up[:, lanes]) + r.b_up[lanes].reshape(1, -1)
         chance = 0.5 + 0.5 * lax.erf(up * (0.5**0.5))
         r.act[:, lanes] = (up * chance).astype(low)
-        r.slope_up[:, lanes] = chance + up * (jnp.exp(-0.5 * up * up) * (0.5 / math.pi) ** 0.5)
+        r.up[:, lanes] = up
+        r.chance[:, lanes] = chance
 
     loaded(r.w_up)
     columns(hidden, fill_up)
@@ -619,7 +620,9 @@
 
     def fill_dup(lanes, j):
         grad_act = dot_nt(r.grad_low[...], r.w_down[lanes, :])
-        grad_up = (grad_act * r.slope_up[:, lanes]).astype(low)
+        up = r.up[:, lanes]
+        slope = r.chance[:, lanes] + up * (jnp.exp(-0.5 * up * up) * (0.5 / math.pi) ** 0.5)
+        grad_up = (grad_act * slope).astype(low)
         r.grad_up[:, lanes] = grad_up
         vec[pl.ds(8 + j // (width // wide), 1), aligned(lax.rem(j, width // wide), wide)] = row_sum(
             grad_up.astype(full)
@@ -1145,7 +1148,8 @@
         first=((rows, width), low),
         first_t=((width, rows), low),
         act=((rows, hidden), low),
-        slope_up=((rows, hidden), full),
+        up=((rows, hidden), full),
+        chance=((rows, hidden), full),
         final=((rows, width), low),
         grad_second=((rows, width), full),
         grad_low=((rows, width), low),

time: 114 us -> 113 us (level)
  no operation moved by 1% of the time
where the time goes in v7:
time: 113 us
  Pallas kernels  112 us (99%)
    pallas_call x1, Pallas kernels, fused_local(): pl.pallas_call(kernel, name='layer', out_shape=[jax.ShapeDtypeStruct(*ite...  102 us
    pallas_call x1, Pallas kernels, fused_local(): pl.pallas_call(functools.partial(finish_kernel, [*given, *final, *room, *...  10.4 us

profile of v7, /device:TPU:0, one launch (start us, length us, event | category | flops | bytes accessed | tf_op | source)
XLA Modules:
  0.0 113.1 jit_solution(12311603568021141973)
XLA Ops:
  0.7 101.9 %layer.1 = (bf16[128,768]{1,0:T(8,128)(2,1)}, bf16[32,768]{1,0:T(8,128)(2,1)}, f32[128,768]{1,0:T(8,128)}, f32[9,48,384]{2,1,0:T(8,128)}, f32[2,48,128]{2,1,0:T(...) custom-call(s32[1,64]{1,0:T(1,128)} %bitcast.5, ...), custom_call_target="tpu_custom_call" | custom-call | tf_op jit(solution)/shard_map/layer/pallas_call | solution.py:1221
  102.6 10.4 %finish.1 = (bf16[1,128,768]{2,1,0:T(8,128)(2,1)}, bf16[1,32,768]{2,1,0:T(8,128)(2,1)}, f32[1,128,768]{2,1,0:T(8,128)}, f32[48,256]{1,0:T(8,128)}, f32[3,48]{1,0...) custom-call(f32[4096,256]{1,0:T(8,128)} %refs_0_.1, ...), custom_call_target="tpu_custom_call" | custom-call | tf_op jit(solution)/shard_map/finish/pallas_call | solution.py:1295
